TPU v7x, 32 devices: a whole 2x2x4 slice. The times are simulated.
32 devices in a mesh: narrow: 4 (over z), wide: 8 (over y, x, core).
Axes of the slice: x: 2, y: 2, z: 4, core: 2. Of those that a mesh axis runs over, the one named last changes fastest.
Arguments:
- layer_input: bfloat16 [32, 512, 640], P(('narrow', 'wide')), may hold values from -6 to 6
- segments: int32 [32, 512], P(('narrow', 'wide')), may hold values from 0 to 7, never falling along the last dimension, each value on 1 to 192 neighbouring positions
- targets: int32 [32, 512], P(('narrow', 'wide')), may hold values from 0 to 24
- loss_mask: int32 [32, 512], P(('narrow', 'wide')), may hold values from 0 to 1
- readout: bfloat16 [640, 25], replicated, may hold values from -0.29882812 to 0.29882812
- attend_gain: bfloat16 [640], P('wide'), may hold values from 0.5 to 1.5
- attend_shift: bfloat16 [640], P('wide'), may hold values from -1.1953125 to 1.1953125
- heads_weight: bfloat16 [640, 1920], P('wide'), may hold values from -0.25 to 0.25
- query_bias: bfloat16 [640], P('wide'), may hold values from -1.1953125 to 1.1953125
- value_bias: bfloat16 [640], P('wide'), may hold values from -1.1953125 to 1.1953125
- output_weight: bfloat16 [640, 640], P('wide'), may hold values from -1.25 to 1.25
- output_bias: bfloat16 [640], P('wide'), may hold values from -1.1953125 to 1.1953125
- forward_gain: bfloat16 [640], P('wide'), may hold values from 0.5 to 1.5
- forward_shift: bfloat16 [640], P('wide'), may hold values from -1.1953125 to 1.1953125
- up_weight: bfloat16 [640, 5120], P('wide'), may hold values from -0.25 to 0.25
- up_bias: bfloat16 [5120], P('wide'), may hold values from -1.1953125 to 1.1953125
- down_weight: bfloat16 [5120, 640], P('wide'), may hold values from -0.125 to 0.125
- down_bias: bfloat16 [640], P('wide'), may hold values from -1.1953125 to 1.1953125
Outputs:
- layer_output: bfloat16 [32, 512, 640], P(('narrow', 'wide'))
- input_grad: float32 [32, 512, 640], P(('narrow', 'wide'))
- attend_gain_grad: float32 [640], P('wide')
- attend_shift_grad: float32 [640], P('wide')
- heads_weight_grad: float32 [640, 1920], P('wide')
- query_bias_grad: float32 [640], P('wide')
- value_bias_grad: float32 [640], P('wide')
- output_weight_grad: float32 [640, 640], P('wide')
- output_bias_grad: float32 [640], P('wide')
- forward_gain_grad: float32 [640], P('wide')
- forward_shift_grad: float32 [640], P('wide')
- up_weight_grad: float32 [640, 5120], P('wide')
- up_bias_grad: float32 [5120], P('wide')
- down_weight_grad: float32 [5120, 640], P('wide')
- down_bias_grad: float32 [640], P('wide')
- loss_sum: float32 [], replicated
- token_count: int32 [], replicated
All inputs are finite; a program needn't handle non-finite values.
Results may differ from a plain program's by a relative error of at most 0.013.
Values may be sent and summed in bfloat16 or wider, within the bound.
No kernel may reach another device: no remote copies, remote signals or barrier semaphores. Data moves between devices by JAX's collectives and lax.ppermute only.
A program may use at most 192 MiB of HBM per device.

v0:
```python
import functools
import math

import jax
import jax.numpy as jnp
from jax import lax
from jax.experimental import pallas as pl
from jax.experimental.pallas import tpu as pltpu
from jax.sharding import PartitionSpec as P

HEADS = 20
HEAD_DIM = 32
LANES = 128
SUBLANES = 8
SEGMENTS = 8
REACH = 192
CHUNK = 256
ROWS = 128
SCALE = 1.0 / math.sqrt(HEAD_DIM)
SCALE2 = math.log2(math.e) * SCALE
F32 = jnp.float32
BF16 = jnp.bfloat16
VECTORS = 8
ATTEND_GAIN, ATTEND_SHIFT, QUERY_BIAS, VALUE_BIAS = 0, 1, 2, 3
OUTPUT_BIAS, FORWARD_GAIN, FORWARD_SHIFT, DOWN_BIAS = 4, 5, 6, 7


def nn(left, right):
    return lax.dot_general(left, right, (((1,), (0,)), ((), ())), preferred_element_type=F32)


def nt(left, right):
    return lax.dot_general(left, right, (((1,), (1,)), ((), ())), preferred_element_type=F32)


def tn(left, right):
    return lax.dot_general(left, right, (((0,), (0,)), ((), ())), preferred_element_type=F32)


def call(kernel, outs, args, positions=None, grid=None, in_specs=None, out_specs=None, scratch=(),
         mib=16):
    whole = pl.BlockSpec(memory_space=pltpu.VMEM)
    in_specs = in_specs or [whole] * len(args)
    args = [
        pltpu.with_memory_space_constraint(arg, pltpu.HBM)
        if spec.memory_space == pltpu.HBM
        else arg
        for arg, spec in zip(args, in_specs)
    ]
    out_specs = out_specs or [whole] * len(outs)
    shapes = [jax.ShapeDtypeStruct(shape, dtype) for shape, dtype in outs]
    extra = [] if positions is None else [positions]
    return pl.pallas_call(
        kernel,
        out_shape=shapes,
        grid_spec=pltpu.PrefetchScalarGridSpec(
            num_scalar_prefetch=len(extra),
            grid=grid or (),
            in_specs=in_specs,
            out_specs=out_specs,
            scratch_shapes=list(scratch),
        ),
        compiler_params=pltpu.CompilerParams(vmem_limit_bytes=mib * 1024 * 1024),
        cost_estimate=pl.CostEstimate(flops=1, bytes_accessed=1, transcendentals=0),
    )(*extra, *args)


def unit(values):
    centred = values - jnp.mean(values, axis=-1, keepdims=True)
    spread = jnp.mean(centred * centred, axis=-1, keepdims=True)
    inverse = lax.rsqrt(spread + 1e-05)
    return centred * inverse, inverse


def unit_back(grad, normal, inverse, gain):
    scaled = grad * gain
    mean = jnp.mean(scaled, axis=-1, keepdims=True)
    along = jnp.mean(scaled * normal, axis=-1, keepdims=True)
    return inverse * (scaled - mean - normal * along)


def spans(length):
    chunk = min(CHUNK, length)
    return [
        (at, at + chunk, max(0, at - REACH), min(length, at + chunk + REACH))
        for at in range(0, length, chunk)
    ]


def split3(values):
    first = values.astype(BF16).astype(F32)
    rest = values - first
    second = rest.astype(BF16).astype(F32)
    return [first, second, rest - second]


def key_marks(segment_column):
    lane = lax.broadcasted_iota(jnp.int32, (segment_column.shape[0], LANES), 1)
    ones = (lane >= SEGMENTS) & (lane < SEGMENTS + 3)
    return jnp.where((lane == segment_column) | ones, 1.0, 0.0).astype(BF16)


def query_marks(segment_row):
    row = lax.broadcasted_iota(jnp.int32, (SEGMENTS, segment_row.shape[1]), 0)
    return jnp.where(row == segment_row, 0.0, -1e30)


def place(rows, head, marks):
    count = rows.shape[1]
    parts = [rows, marks, jnp.zeros((LANES - marks.shape[0], count), BF16)]
    if head < LANES // HEAD_DIM - 1:
        parts.insert(1, jnp.zeros((LANES - HEAD_DIM * (head + 1), count), BF16))
    if head:
        parts.insert(0, jnp.zeros((HEAD_DIM * head, count), BF16))
    return jnp.concatenate(parts, axis=0)


def attend_kernel(column_ref, row_ref, q_ref, k_ref, v_ref, out_ref, across_ref, lse_ref, marks_ref):
    @pl.when(pl.program_id(0) == 0)
    def _():
        marks_ref[...] = key_marks(column_ref[...])

    length = q_ref.shape[0]
    heads = LANES // HEAD_DIM
    queries = q_ref[...].T
    values = v_ref[...].T
    keys = jnp.concatenate([k_ref[...], marks_ref[...]], axis=1)
    blank = jnp.zeros((SUBLANES, length), F32)
    marks = jnp.concatenate([query_marks(row_ref[...]), blank], axis=0).astype(BF16)
    ones = jnp.ones((SUBLANES, length), BF16)
    bodies = [(head, span) for head in range(heads) for span in spans(length)]

    def rows(head):
        return slice(HEAD_DIM * head, HEAD_DIM * (head + 1))

    summed = [jnp.concatenate([values[rows(head)], ones], axis=0) for head in range(heads)]

    def score(head, span):
        begin, end, low, high = span
        return nn(keys[low:high], place(queries[rows(head), begin:end], head, marks[:, begin:end]))

    def finish(head, span, top, probs):
        begin, end, low, high = span
        out = nn(summed[head][:, low:high], probs)
        total = out[HEAD_DIM : HEAD_DIM + 1]
        across_ref[rows(head), begin:end] = out[:HEAD_DIM] * (1.0 / total)
        lse_ref[head : head + 1, begin:end] = (top + jnp.log2(total)) * (1.0 / SCALE2)

    scores = [score(*body) for body in bodies[:2]]
    waiting = None
    for at, body in enumerate(bodies):
        current = scores.pop(0)
        if at + 2 < len(bodies):
            scores.append(score(*bodies[at + 2]))
        top = jnp.max(current, axis=0, keepdims=True) * SCALE2
        probs = jnp.exp2(current * SCALE2 - top).astype(BF16)
        if waiting is not None:
            finish(*waiting)
        waiting = (*body, top, probs)
    finish(*waiting)
    lse_ref[heads:, :] = jnp.zeros((SUBLANES - heads, length), F32)
    out_ref[...] = across_ref[...].T.astype(BF16)


def attend_back_kernel(
    column_ref, row_ref, q_ref, k_ref, v_ref, grad_ref, across_ref, lse_ref,
    gq_ref, gk_ref, gv_ref, marks_ref, turned_ref,
):
    @pl.when(pl.program_id(0) == 0)
    def _():
        marks_ref[...] = key_marks(column_ref[...])

    length = q_ref.shape[0]
    grad = grad_ref[...]
    queries = q_ref[...].T
    turned_keys = k_ref[...].T
    grads = grad.T
    keys = jnp.concatenate([k_ref[...], marks_ref[...]], axis=1)
    values = jnp.concatenate([v_ref[...], marks_ref[...]], axis=1)
    low_marks = query_marks(row_ref[...])
    blank = jnp.zeros((SUBLANES, length), F32)
    lane = lax.broadcasted_iota(jnp.int32, (1, LANES), 1) // HEAD_DIM
    heads = []
    for head in range(LANES // HEAD_DIM):
        rows = slice(HEAD_DIM * head, HEAD_DIM * (head + 1))
        inner = jnp.sum(grads[rows].astype(F32) * across_ref[rows, :], axis=0, keepdims=True)
        lse = lse_ref[head : head + 1, :]
        score_marks = jnp.concatenate([low_marks, *split3(-lse), blank[:5]], axis=0)
        inner_marks = jnp.concatenate([blank, *split3(-inner), blank[:5]], axis=0)
        zero = jnp.zeros_like(grad)
        heads.append(
            (
                rows,
                score_marks.astype(BF16),
                inner_marks.astype(BF16),
                jnp.where(lane == head, q_ref[...], zero),
                jnp.where(lane == head, grad, zero),
            )
        )
    bodies = [
        (head, at, span) for head in range(len(heads)) for at, span in enumerate(spans(length))
    ]
    sums = [[None, None] for _ in spans(length)]

    def pair(head, at, span):
        begin, end, low, high = span
        rows, score_marks, inner_marks, _, _ = heads[head]
        return (
            nn(keys[low:high], place(queries[rows, begin:end], head, score_marks[:, begin:end])),
            nn(values[low:high], place(grads[rows, begin:end], head, inner_marks[:, begin:end])),
        )

    def finish(head, at, span, score_grads, probs):
        begin, end, low, high = span
        rows, _, _, own_queries, own_grads = heads[head]
        for which, (left, right) in enumerate(
            ((score_grads, own_queries[begin:end]), (probs, own_grads[begin:end]))
        ):
            part = nn(left, right)
            sums[at][which] = part if sums[at][which] is None else sums[at][which] + part
        turned_ref[rows, begin:end] = nn(turned_keys[rows, low:high], score_grads)

    ahead = [pair(*bodies[0])]
    waiting = None
    for at, body in enumerate(bodies):
        scores, differences = ahead.pop(0)
        if at + 1 < len(bodies):
            ahead.append(pair(*bodies[at + 1]))
        probs = jnp.exp2(scores * SCALE2)
        score_grads = (probs * differences).astype(BF16)
        if waiting is not None:
            finish(*waiting)
        waiting = (*body, score_grads, probs.astype(BF16))
    finish(*waiting)
    gq_ref[...] = (turned_ref[...].T * SCALE).astype(BF16)
    for which, (ref, factor) in enumerate(((gk_ref, SCALE), (gv_ref, 1.0))):
        total = None
        for at, (_, _, low, high) in enumerate(spans(length)):
            parts = [sums[at][which]]
            if low:
                parts.insert(0, jnp.zeros((low, LANES), F32))
            if high < length:
                parts.append(jnp.zeros((length - high, LANES), F32))
            part = jnp.concatenate(parts, axis=0) if len(parts) > 1 else parts[0]
            total = part if total is None else total + part
        ref[...] = (total * factor).astype(BF16)


def attention_specs(length, width, begin=0):
    tiles = width // LANES

    def tile(at, begin=begin):
        return pl.BlockSpec((length, LANES), lambda i: (0, at + begin + i))

    return (
        tiles,
        tile,
        pl.BlockSpec((length, 1), lambda i: (0, 0)),
        pl.BlockSpec((1, length), lambda i: (0, 0)),
        pl.BlockSpec((LANES, length), lambda i: (begin + i, 0)),
        pl.BlockSpec((SUBLANES, length), lambda i: (begin + i, 0)),
    )


def attend(joined, column, row):
    length = joined.shape[0]
    width = joined.shape[1] // 3
    tiles, tile, column_spec, row_spec, across_spec, lse_spec = attention_specs(length, width)
    return call(
        attend_kernel,
        [((length, width), BF16), ((width, length), F32), ((SUBLANES * tiles, length), F32)],
        (column, row, joined, joined, joined),
        grid=(tiles,),
        in_specs=[column_spec, row_spec, tile(0), tile(tiles), tile(2 * tiles)],
        out_specs=[tile(0), across_spec, lse_spec],
        scratch=[pltpu.VMEM((length, LANES), BF16)],
    )


def attend_back(joined, column, row, grad, across, lse, begin=0, end=None):
    length = joined.shape[0]
    width = joined.shape[1] // 3
    specs = attention_specs(length, width, begin)
    tiles, tile, column_spec, row_spec, across_spec, lse_spec = specs
    count = (end or tiles) - begin
    return call(
        attend_back_kernel,
        [((length, count * LANES), BF16)] * 3,
        (column, row, joined, joined, joined, grad, across, lse),
        grid=(count,),
        in_specs=[column_spec, row_spec, tile(0), tile(tiles), tile(2 * tiles), tile(0), across_spec, lse_spec],
        out_specs=[tile(0, 0)] * 3,
        scratch=[pltpu.VMEM((length, LANES), BF16), pltpu.VMEM((LANES, length), F32)],
        mib=24,
    )


def slab_kernel(heads_ref, out_ref, short_ref, up_ref, slab_ref):
    rows = heads_ref.shape[0]
    width = out_ref.shape[1]
    slab_ref[:rows, : 3 * width] = heads_ref[...]
    slab_ref[:rows, 3 * width :] = out_ref[...]
    slab_ref[rows:, :] = jnp.zeros((VECTORS, 4 * width), BF16)
    slab_ref[rows:, :rows] = short_ref[...]
    slab_ref[rows:, LANES : LANES + up_ref.shape[1]] = jnp.broadcast_to(
        up_ref[...], (VECTORS, up_ref.shape[1])
    )


def halves_kernel(hidden, position_ref, up_ref, mine_ref, other_ref):
    for at in range(mine_ref.shape[1] // hidden):
        here = slice(hidden * at, hidden * (at + 1))
        for core, ref in enumerate((mine_ref, other_ref)):
            begin = (2 * at + (position_ref[0] + core) % 2) * hidden
            ref[:, here] = up_ref[:, pl.ds(pl.multiple_of(begin, LANES), hidden)]


def project_kernel(count, rows, hidden, position_ref, x_ref, *refs):
    slabs, refs = refs[:count], refs[count:]
    length, width = x_ref.shape
    if count:
        low_ref, joined_ref, heads_ref, out_ref, vector_ref, bias_ref, short_ref, sems = refs
        copies = []
        for at, slab in enumerate(slabs):
            begin = pl.multiple_of(position_ref[at] * rows, SUBLANES)
            here = pl.ds(begin, rows)
            for which, (source, target) in enumerate(
                (
                    (slab.at[pl.ds(0, rows), pl.ds(0, 3 * width)], heads_ref.at[here]),
                    (slab.at[pl.ds(0, rows), pl.ds(3 * width, width)], out_ref.at[here]),
                    (slab.at[pl.ds(rows, VECTORS), pl.ds(0, LANES + hidden)], short_ref.at[at]),
                )
            ):
                copy = pltpu.make_async_copy(source, target, sems.at[at, which])
                copy.start()
                copies.append(copy)
    else:
        heads_ref, vector_ref, low_ref, joined_ref = refs
    if count:
        for copy in copies:
            copy.wait()
        vectors = jnp.zeros((VECTORS, width), F32)
        for at in range(count):
            begin = position_ref[at] * rows
            short = short_ref[at, :, :LANES].astype(F32)
            lane = lax.broadcasted_iota(jnp.int32, short.shape, 1)
            short = jnp.where(lane < rows, short, 0.0)
            short = jnp.concatenate([short, jnp.zeros((VECTORS, width - LANES), F32)], axis=1)
            vectors = vectors + pltpu.roll(short, begin, 1)
            if at < count // 2:
                begin = pl.multiple_of(lax.div(position_ref[at], 2) * hidden, LANES)
                bias_ref[:, pl.ds(begin, hidden)] = short_ref[at, :, LANES:].astype(F32)
        vector_ref[...] = vectors
    zero = jnp.zeros((1, width), F32)
    vector = vector_ref[...]
    bias = jnp.concatenate(
        [vector[QUERY_BIAS : QUERY_BIAS + 1], zero, vector[VALUE_BIAS : VALUE_BIAS + 1]], axis=1
    )
    for at in range(0, length, ROWS):
        normal, _ = unit(x_ref[at : at + ROWS, :].astype(F32))
        low_ref[at : at + ROWS, :] = (
            normal * vector[ATTEND_GAIN : ATTEND_GAIN + 1]
            + vector[ATTEND_SHIFT : ATTEND_SHIFT + 1]
        ).astype(BF16)
    for at in range(0, 3 * width, width):
        here = slice(at, at + width)
        joined_ref[:, here] = (nn(low_ref[...], heads_ref[:, here]) + bias[:, here]).astype(BF16)


def middle_kernel(x_ref, attended_ref, out_ref, vector_ref, middle_ref, low_ref):
    vector = vector_ref[...]
    for at in range(0, x_ref.shape[0], ROWS):
        here = slice(at, at + ROWS)
        middle = (
            x_ref[here, :].astype(F32)
            + nn(attended_ref[here, :], out_ref[...])
            + vector[OUTPUT_BIAS : OUTPUT_BIAS + 1]
        )
        middle_ref[here, :] = middle
        normal, _ = unit(middle)
        low_ref[here, :] = (
            normal * vector[FORWARD_GAIN : FORWARD_GAIN + 1]
            + vector[FORWARD_SHIFT : FORWARD_SHIFT + 1]
        ).astype(BF16)


def up_kernel(position_ref, own_ref, other_ref, bias_ref, *refs):
    parts, (act_ref, slope_ref, full_ref) = refs[: len(refs) - 3], refs[len(refs) - 3 :]
    for at, part in enumerate(parts):
        rows = part.shape[0]
        begin = pl.multiple_of(position_ref[at] * rows, SUBLANES)
        full_ref[pl.ds(begin, rows), :] = part[...]
    weight = full_ref[...]
    bias = bias_ref[:1, :]
    length = own_ref.shape[0]
    for which, ref in enumerate((own_ref, other_ref)):
        for at in range(0, length, ROWS):
            upward = nn(ref[at : at + ROWS, :], weight) + bias
            share = 0.5 + 0.5 * lax.erf(upward * math.sqrt(0.5))
            bell = jnp.exp2((upward * upward) * (-0.5 * math.log2(math.e)))
            here = slice(which * length + at, which * length + at + ROWS)
            act_ref[here, :] = (upward * share).astype(BF16)
            slope = share + upward * (bell * (1.0 / math.sqrt(2.0 * math.pi)))
            slope_ref[here, :] = slope.astype(BF16)


def column_specs(half, block):
    block = min(block, half)

    def column(height):
        return pl.BlockSpec((height, block), lambda i, at: (0, i))

    return half // block, block, column


def whole_spec(shape):
    return pl.BlockSpec(shape, lambda i, at: (0,) * len(shape))


def up_project(own, other, bias, parts, positions):
    length, width = own.shape
    half = parts[0].shape[1]
    steps, _, column = column_specs(half, 512)
    whole = whole_spec((length, width))
    return call(
        up_kernel,
        [((2 * length, half), BF16), ((2 * length, half), BF16), ((width, half), BF16)],
        (own, other, bias, *parts),
        positions,
        grid=(steps,),
        in_specs=[whole, whole, column(bias.shape[0])] + [column(part.shape[0]) for part in parts],
        out_specs=[column(2 * length), column(2 * length), column(width)],
    )


def down_kernel(position_ref, act_ref, *refs):
    parts, (own_ref, other_ref, full_ref) = refs[: len(refs) - 3], refs[len(refs) - 3 :]
    length = own_ref.shape[0]
    for at, part in enumerate(parts):
        rows = part.shape[0]
        begin = pl.multiple_of(position_ref[at] * rows, SUBLANES)
        full_ref[pl.ds(begin, rows), :] = part[...]
    for which, ref in enumerate((own_ref, other_ref)):
        here = slice(which * length, (which + 1) * length)
        ref[...] = nn(act_ref[here, :], full_ref[...]).astype(ref.dtype)


def down_project(act, parts, positions):
    length = act.shape[0] // 2
    half = act.shape[1]
    width = parts[0].shape[1]
    return call(
        down_kernel,
        [((length, width), F32), ((length, width), BF16), ((half, width), BF16)],
        (act, *parts),
        positions,
        mib=20,
    )


def loss_kernel(
    middle_ref, own_ref, got_ref, vector_ref, readout_ref, target_ref, mask_ref,
    low_ref, down_ref, grad_ref, sums_ref,
):
    result = (
        middle_ref[...]
        + (own_ref[...] + got_ref[...].astype(F32))
        + vector_ref[DOWN_BIAS : DOWN_BIAS + 1, :]
    ).astype(BF16)
    low_ref[...] = result
    logits = nt(readout_ref[...], result)
    length = logits.shape[1]
    top = jnp.max(logits, axis=0, keepdims=True)
    shifted = jnp.exp(logits - top)
    total = jnp.sum(shifted, axis=0, keepdims=True)
    onehot = lax.broadcasted_iota(jnp.int32, logits.shape, 0) == target_ref[...]
    picked = jnp.sum(jnp.where(onehot, logits, 0.0), axis=0, keepdims=True)
    weight = mask_ref[...].astype(F32)
    loss = (top + jnp.log(total) - picked) * weight
    loss_lanes = jnp.zeros((1, LANES), F32)
    count_lanes = jnp.zeros((1, LANES), F32)
    for at in range(0, length, LANES):
        loss_lanes = loss_lanes + loss[:, at : at + LANES]
        count_lanes = count_lanes + weight[:, at : at + LANES]
    lanes = jnp.concatenate([loss_lanes, count_lanes], axis=0)
    lanes = jnp.concatenate([lanes, jnp.zeros((2, result.shape[1] - LANES), F32)], axis=1)
    grad_logits = (weight * (shifted / total - onehot.astype(F32))).astype(BF16)
    grad = tn(grad_logits, readout_ref[...])
    grad_ref[...] = grad
    low = grad.astype(BF16)
    down_ref[...] = low
    sums = jnp.sum(low.astype(F32), axis=0, keepdims=True)
    blank = jnp.zeros((SUBLANES - 3, result.shape[1]), F32)
    sums_ref[...] = jnp.concatenate([lanes, sums, blank], axis=0)


def down_grad_kernel(chips, position_ref, act_ref, own_ref, other_ref, *out_refs):
    length = own_ref.shape[0]
    hidden = act_ref.shape[1] // chips
    for offset in range(chips):
        if len(out_refs) == 1:
            begin = offset * hidden
        else:
            begin = pl.multiple_of((position_ref[0] ^ offset) * hidden, LANES)
        here = pl.ds(begin, hidden)
        part = tn(act_ref[:length, here], own_ref[...]) + tn(act_ref[length:, here], other_ref[...])
        part = part.astype(BF16)
        if len(out_refs) == 1:
            out_refs[0][begin : begin + hidden, :] = part
            continue
        keep_x, send_x, keep_y, send_y = out_refs
        half = hidden // 2
        (send_x if offset % 2 else keep_x)[offset // 2, :, :] = part[:half]
        (send_y if offset // 2 else keep_y)[offset % 2, :, :] = part[half:]


def down_grad(act, own, other, chips, position):
    half = act.shape[1]
    width = own.shape[1]
    if square():
        outs = [((2, half // chips // 2, width), BF16)] * 4
    else:
        outs = [((half, width), BF16)]
    return call(
        functools.partial(down_grad_kernel, chips), outs, (act, own, other), position, mib=20
    )


def up_grad_kernel(
    rows, position_ref, own_ref, other_ref, slope_ref, second_ref, second_other_ref, down_ref,
    up_ref, bias_ref, *refs,
):
    out_refs, part_ref = refs[:-1], refs[-1]
    length = own_ref.shape[0]
    total = None
    grads = []
    for which, ref in enumerate((own_ref, other_ref)):
        for at in range(0, length, 2 * ROWS):
            here = slice(which * length + at, which * length + at + 2 * ROWS)
            grad = nt(ref[at : at + 2 * ROWS, :], down_ref[...]) * slope_ref[here, :].astype(F32)
            low = grad.astype(BF16)
            up_ref[here, :] = low
            part = jnp.sum(low.astype(F32), axis=0, keepdims=True)
            total = part if total is None else total + part
    bias_ref[...] = total
    part = tn(second_ref[...], up_ref[:length, :]) + tn(second_other_ref[...], up_ref[length:, :])
    if len(out_refs) == 1:
        out_refs[0][...] = part.astype(BF16)
        return
    part_ref[...] = part
    keep_x, send_x, keep_y, send_y = out_refs
    for offset in range(4):
        begin = pl.multiple_of((position_ref[0] ^ offset) * (2 * rows), SUBLANES)
        upper = part_ref[pl.ds(begin, rows), :].astype(BF16)
        lower = part_ref[pl.ds(begin + rows, rows), :].astype(BF16)
        (send_x if offset % 2 else keep_x)[offset // 2, :, :] = upper
        (send_y if offset // 2 else keep_y)[offset % 2, :, :] = lower


def up_grad(own, other, slope, second, second_other, down_full, rows, position):
    length, width = own.shape
    half = slope.shape[1]
    steps, block, column = column_specs(half, 512)
    whole = whole_spec((length, width))
    if square():
        outs = [((2, rows, half), BF16)] * 4
        specs = [pl.BlockSpec((2, rows, block), lambda i, at: (0, 0, i))] * 4
    else:
        outs = [((width, half), BF16)]
        specs = [column(width)]
    return call(
        functools.partial(up_grad_kernel, rows),
        [((2 * length, half), BF16), ((1, half), F32), *outs],
        (own, other, slope, second, second_other, down_full),
        position,
        grid=(steps,),
        in_specs=[
            whole, whole, column(2 * length), whole, whole,
            pl.BlockSpec((block, width), lambda i, at: (i, 0)),
        ],
        out_specs=[column(2 * length), column(1), *specs],
        scratch=[pltpu.VMEM((width, block), F32)],
        mib=20,
    )


def inward_kernel(grad_ref, up_ref, own_ref, other_ref):
    length = own_ref.shape[0]
    other_ref[...] = nt(grad_ref[length:, :], up_ref[...]).astype(BF16)
    own_ref[...] = nt(grad_ref[:length, :], up_ref[...])


def join_kernel(hidden, position_ref, mine_ref, other_ref, out_ref):
    for at in range(mine_ref.shape[1] // hidden):
        here = slice(hidden * at, hidden * (at + 1))
        for core, ref in enumerate((mine_ref, other_ref)):
            begin = (2 * at + (position_ref[0] + core) % 2) * hidden
            out_ref[:, pl.ds(pl.multiple_of(begin, LANES), hidden)] = ref[:, here].astype(F32)


def branch_kernel(
    got_ref, own_far, middle_far, result_far, out_ref, vector_ref,
    grad_ref, branch_ref, attended_ref, sums_ref, own_ref, middle_ref, result_ref, sems,
):
    width = own_ref.shape[1]
    blocks = range(0, own_ref.shape[0], ROWS)
    copies = []
    for at in blocks:
        here = pl.ds(at, ROWS)
        copies.append(
            [
                pltpu.make_async_copy(far.at[here], ref.at[here], sems.at[at // ROWS, which])
                for which, (far, ref) in enumerate(
                    ((own_far, own_ref), (middle_far, middle_ref), (result_far, result_ref))
                )
            ]
        )
        for copy in copies[-1]:
            copy.start()
    gain = vector_ref[FORWARD_GAIN : FORWARD_GAIN + 1, :]
    sums = [jnp.zeros((1, width), F32) for _ in range(3)]
    for at in blocks:
        for copy in copies[at // ROWS]:
            copy.wait()
        here = slice(at, at + ROWS)
        grad = own_ref[here, :] + got_ref[here, :].astype(F32)
        normal, inverse = unit(middle_ref[here, :])
        middle = result_ref[here, :] + unit_back(grad, normal, inverse, gain)
        grad_ref[here, :] = middle
        branch = middle.astype(BF16)
        branch_ref[here, :] = branch
        attended_ref[here, :] = nt(branch, out_ref[...]).astype(BF16)
        for which, part in enumerate((grad * normal, grad, branch.astype(F32))):
            sums[which] = sums[which] + jnp.sum(part, axis=0, keepdims=True)
    blank = jnp.zeros((SUBLANES - 3, width), F32)
    sums_ref[...] = jnp.concatenate([*sums, blank], axis=0)


def last_kernel(count, rows, hidden, pieces, position_ref, x_ref, low_ref, *refs):
    grad_refs, refs = refs[: 3 * pieces], refs[3 * pieces :]
    heads_ref, attended_ref, branch_ref, grad_ref, vector_ref, *refs = refs
    sums_ref, loss_ref, up_ref, *refs = refs
    slabs, (input_ref, vectors_ref, full_ref) = refs[:count], refs[count:]
    width = x_ref.shape[1]

    def grads(which, here):
        parts = [ref[here, :] for ref in grad_refs[which::3]]
        return jnp.concatenate(parts, axis=1) if pieces > 1 else parts[0]

    for at in range(3):
        part = tn(low_ref[...], grads(at, slice(None)))
        full_ref[:, width * at : width * (at + 1)] = part.astype(BF16)
    full_ref[:, 3 * width :] = tn(attended_ref[...], branch_ref[...]).astype(BF16)
    gain = vector_ref[ATTEND_GAIN : ATTEND_GAIN + 1, :]
    sums = [jnp.zeros((1, width), F32) for _ in range(4)]
    for at in range(0, x_ref.shape[0], ROWS):
        here = slice(at, at + ROWS)
        grad_query, grad_key, grad_value = [grads(at, here) for at in range(3)]
        grad = (
            nt(grad_query, heads_ref[:, :width])
            + nt(grad_key, heads_ref[:, width : 2 * width])
            + nt(grad_value, heads_ref[:, 2 * width :])
        )
        normal, inverse = unit(x_ref[here, :].astype(F32))
        input_ref[here, :] = grad_ref[here, :] + unit_back(grad, normal, inverse, gain)
        parts = (grad * normal, grad, grad_query.astype(F32), grad_value.astype(F32))
        for which, part in enumerate(parts):
            sums[which] = sums[which] + jnp.sum(part, axis=0, keepdims=True)
    vectors = jnp.concatenate(
        [*sums, sums_ref[2:3, :], sums_ref[0:1, :], sums_ref[1:2, :], loss_ref[2:3, :]], axis=0
    )
    vectors_ref[...] = vectors
    blank = jnp.zeros((VECTORS - 1, hidden), F32)
    lanes = jnp.concatenate([loss_ref[:2, :LANES], jnp.zeros((VECTORS - 2, LANES), F32)], axis=0)
    for at, slab in enumerate(slabs):
        place_at = position_ref[at]
        begin = pl.multiple_of(place_at * rows, SUBLANES)
        slab[:rows, :] = full_ref[pl.ds(begin, rows), :]
        short = pltpu.roll(vectors, width - begin, 1)[:, :LANES]
        if at < count // 2:
            hidden_at = pl.multiple_of(lax.div(place_at, 2) * hidden, LANES)
            bias = jnp.concatenate([up_ref[:, pl.ds(hidden_at, hidden)], blank], axis=0)
        else:
            bias = jnp.zeros((VECTORS, hidden), F32)
        row = jnp.concatenate([short, bias, lanes], axis=1).astype(BF16)
        pad = jnp.zeros((VECTORS, 4 * width - row.shape[1]), BF16)
        slab[rows:, :] = jnp.concatenate([row, pad], axis=1)


def settle_kernel(cut, rows, place_ref, *refs):
    totals, outers, (heads_ref, out_ref, short_ref) = refs[:2], refs[2:4], refs[4:]
    width = out_ref.shape[1]
    inner = (place_ref[0] == 1) | (place_ref[0] == 2)
    chosen = [
        jnp.where(inner, total[...], outer[...]).astype(F32) for total, outer in zip(totals, outers)
    ]
    for begin, end, values in ((0, cut, chosen[0]), (cut, rows, chosen[1])):
        heads_ref[begin:end, :] = values[: end - begin, : 3 * width]
        out_ref[begin:end, :] = values[: end - begin, 3 * width :]
    short_ref[...] = chosen[1][rows - cut :]


def swap(values, bit):
    return lax.ppermute(values, "wide", [(i, i ^ bit) for i in range(lax.axis_size("wide"))])


def same_core_groups():
    chips = lax.axis_size("wide") // 2
    return [[2 * chip + core for chip in range(chips)] for core in range(2)]


def square():
    return lax.axis_size("wide") == 8


def spread_chips(shard):
    return lax.all_gather(shard, "wide", axis=0, axis_index_groups=same_core_groups())


def add_low(*parts):
    return sum(part.astype(F32) for part in parts).astype(BF16)


def collect_chips(parts):
    return lax.psum_scatter(
        parts, "wide", scatter_dimension=0, axis_index_groups=same_core_groups()
    )


def after(values, *gates):
    leaves, tree = jax.tree.flatten(values)
    held = lax.optimization_barrier((*leaves, *jax.tree.leaves(gates)))
    return jax.tree.unflatten(tree, held[: len(leaves)])


INWARD, ACROSS, OUTWARD = [(0, 1), (3, 2)], [(1, 2), (2, 1)], [(1, 0), (2, 3)]


def hop(parts, pairs):
    return [lax.ppermute(part, "narrow", pairs) for part in parts]


def add_each(left, right):
    return [add_low(a, b) for a, b in zip(left, right)]


def settle(total, outer):
    place_at = lax.axis_index("narrow")
    return jnp.where((place_at == 1) | (place_at == 2), total, outer)


def sum_narrow(shard):
    if lax.axis_size("narrow") != 4:
        return lax.psum(shard, "narrow")
    half = add_low(shard, *hop([shard], INWARD))
    total = add_low(half, *hop([half], ACROSS))
    return settle(total, *hop([total], OUTWARD))


def local(
    layer_input, segments, targets, loss_mask, readout,
    attend_gain, attend_shift, heads_weight, query_bias, value_bias, output_weight, output_bias,
    forward_gain, forward_shift, up_weight, up_bias, down_weight, down_bias,
):
    length = layer_input.shape[1]
    width = layer_input.shape[2]
    wide = lax.axis_size("wide")
    chips = wide // 2
    core = lax.axis_index("wide") % 2
    chip = lax.axis_index("wide") // 2
    rows = heads_weight.shape[0]
    hidden = up_bias.shape[0]
    half = chips * hidden
    x = layer_input[0]
    vmem = pl.BlockSpec(memory_space=pltpu.VMEM)
    far_away = pl.BlockSpec(memory_space=pltpu.HBM)
    column = segments.reshape(length, 1)

    def by_core(mine, other, axis):
        return jnp.where(
            core == 0, jnp.stack([mine, other], axis), jnp.stack([other, mine], axis)
        )

    def mine_of(values, axis, flip=0):
        return lax.dynamic_index_in_dim(values, core ^ flip, axis, keepdims=False)

    short = jnp.stack(
        [
            attend_gain, attend_shift, query_bias, value_bias,
            output_bias, forward_gain, forward_shift, down_bias,
        ]
    )
    core_position = core.reshape(1).astype(jnp.int32)
    chip_position = chip.reshape(1).astype(jnp.int32)
    if square():
        offsets = jnp.arange(4, dtype=jnp.int32)
        (slab,) = call(
            slab_kernel,
            [((rows + VECTORS, 4 * width), BF16)],
            (heads_weight, output_weight, short, up_bias[None]),
        )
        near_x, near_y, far = swap(slab, 2), swap(slab, 4), swap(slab, 6)
        (up_weight,) = after([up_weight], near_x)
        up_mine, up_other = call(
            functools.partial(halves_kernel, hidden),
            [((rows, half), BF16)] * 2,
            (up_weight,),
            core_position,
        )
        other_x, mine_y = swap(up_other, 3), swap(up_mine, 4)
        mine_x, other_y = swap(up_mine, 2), swap(up_other, 5)
        near_y, far = after([near_y, far], up_mine)
        slabs = [slab, near_x, near_y, far]
        slabs = slabs + [swap(part, 1) for part in slabs]
        devices = 2 * (chip ^ offsets) + core
        positions = jnp.concatenate([devices, devices ^ 1]).astype(jnp.int32)
        up_positions = positions
        first_low, joined, heads_full, output_full, vectors, up_bias_half = call(
            functools.partial(project_kernel, len(slabs), rows, hidden),
            [
                ((length, width), BF16), ((length, 3 * width), BF16), ((width, 3 * width), BF16),
                ((width, width), BF16), ((VECTORS, width), F32), ((VECTORS, half), F32),
            ],
            (x, *slabs),
            positions,
            in_specs=[pl.BlockSpec(memory_space=pltpu.VMEM)]
            + [pl.BlockSpec(memory_space=pltpu.HBM)] * len(slabs),
            scratch=[
                pltpu.VMEM((len(slabs), VECTORS, LANES + hidden), BF16),
                pltpu.SemaphoreType.DMA((len(slabs), 3)),
            ],
            mib=20,
        )
    else:
        tail = jnp.concatenate([short.reshape(1, 8 * rows), up_bias[None]], axis=1)
        tail = jnp.pad(tail, ((0, 0), (0, 4 * width - tail.shape[1])))
        slab = jnp.concatenate(
            [jnp.concatenate([heads_weight, output_weight], axis=1), tail], axis=0
        )
        slabs = lax.all_gather(slab, "wide", axis=0)
        attend_full = slabs[:, :rows].reshape(width, 4 * width)
        heads_full = attend_full[:, : 3 * width]
        output_full = attend_full[:, 3 * width :]
        last = slabs[:, rows].astype(F32)
        vectors = last[:, : 8 * rows].reshape(wide, 8, rows).transpose(1, 0, 2).reshape(8, width)
        up_bias_half = mine_of(last[:, 8 * rows : 8 * rows + hidden].reshape(chips, 2, hidden), 1)
        up_bias_half = jnp.broadcast_to(up_bias_half.reshape(1, half), (VECTORS, half))
        positions = jnp.zeros((1,), jnp.int32)
        first_low, joined = call(
            functools.partial(project_kernel, 0, rows, hidden),
            [((length, width), BF16), ((length, 3 * width), BF16)],
            (x, heads_full, vectors),
            positions,
            mib=20,
        )
        up_view = up_weight.reshape(rows, chips, 2, hidden)
        up_pair = by_core(
            mine_of(up_view, 2).reshape(rows, half),
            swap(mine_of(up_view, 2, 1).reshape(rows, half), 1),
            0,
        ).reshape(2 * rows, half)
        up_parts = [spread_chips(up_pair).reshape(width, half)]
        down_parts = [spread_chips(down_weight).reshape(half, width)]
        up_positions = down_positions = positions

    attended, across, lse = attend(joined, column, segments)
    if square():
        passed_y, passed_x = after([mine_y, other_x], attended)
        up_parts = [
            up_mine, mine_x, mine_y, swap(passed_y, 2),
            swap(up_other, 1), other_x, other_y, swap(passed_x, 4),
        ]
        middle_row = hidden // 2
        upper, lower = after(
            [down_weight[:middle_row], down_weight[middle_row:]], mine_x, other_y, attended
        )
        lower_x, upper_y = swap(lower, 2), swap(upper, 4)
        upper_x, lower_y = swap(upper, 2), swap(lower, 4)
        down_parts = [
            down_weight, upper_x, lower_x, upper_y, lower_y
        ]
        at = jnp.arange(7, dtype=jnp.int32)
        down_positions = jnp.where(at == 0, chip, 2 * (chip ^ ((at + 1) // 2)) + (at + 1) % 2)
    middle, second_low = call(
        middle_kernel,
        [((length, width), F32), ((length, width), BF16)],
        (x, attended, output_full, vectors),
    )

    second_other = swap(second_low, 1)
    activated, slope, up_full = up_project(
        second_low, second_other, up_bias_half, up_parts, up_positions
    )
    if square():
        passed_x, passed_y = after([upper_y, lower_x], activated)
        down_parts = down_parts + [swap(passed_x, 2), swap(passed_y, 4)]
    outward, outward_other, down_full = down_project(activated, down_parts, down_positions)
    result_low, grad_down, grad_result, loss_sums = call(
        loss_kernel,
        [
            ((length, width), BF16), ((length, width), BF16), ((length, width), F32),
            ((SUBLANES, width), F32),
        ],
        (middle, outward, swap(outward_other, 1), vectors, readout.T, targets, loss_mask),
    )

    grad_down_other = swap(grad_down, 1)
    down_parts = down_grad(activated, grad_down, grad_down_other, chips, chip_position)
    if square():
        keep_dx, send_dx, keep_dy, send_dy = down_parts
        down_first = [swap(send_dx, 2), swap(send_dy, 4)]
        (grad_down_other,) = after([grad_down_other], send_dx)
    grad_up, up_bias_part, *up_parts = up_grad(
        grad_down, grad_down_other, slope, second_low, second_other, down_full, rows, chip_position
    )
    inward, inward_other = call(
        inward_kernel,
        [((length, width), F32), ((length, width), BF16)],
        (grad_up, up_full),
        mib=20,
    )
    got_inward = swap(inward_other, 1)
    if square():
        down_second = [
            add_low(keep_dx[1], down_first[0][1]), add_low(keep_dy[1], down_first[1][1])
        ]
        (got_inward,) = after([got_inward], down_second)
        keep_ux, send_ux, keep_uy, send_uy = up_parts
        send_ux, send_uy = after([send_ux, send_uy], down_second)
        down_got = [swap(down_second[0], 4), swap(down_second[1], 2)]
        up_first = [swap(send_ux, 2), swap(send_uy, 4)]
    grad_middle, grad_branch, grad_attended, branch_sums = call(
        branch_kernel,
        [
            ((length, width), F32), ((length, width), BF16), ((length, width), BF16),
            ((SUBLANES, width), F32),
        ],
        (got_inward, inward, middle, grad_result, output_full, vectors),
        in_specs=[vmem, far_away, far_away, far_away, vmem, vmem],
        scratch=[
            *[pltpu.VMEM((length, width), F32)] * 3,
            pltpu.SemaphoreType.DMA((length // ROWS, 3)),
        ],
        mib=24,
    )

    if square():
        attend_grads = attend_back(joined, column, segments, grad_attended, across, lse)
        down_narrow = [
            add_low(keep_dx[0], down_first[0][0], after([down_got[0]], attend_grads[0])[0]),
            add_low(keep_dy[0], down_first[1][0], after([down_got[1]], attend_grads[0])[0]),
        ]
        down_in = hop(down_narrow, INWARD)
        attend_grads = after(attend_grads, down_narrow)
    else:
        attend_grads = attend_back(joined, column, segments, grad_attended, across, lse)
    slab_shape = ((rows + VECTORS, 4 * width), BF16)
    *slabs, input_grad, short_sums, attend_part = call(
        functools.partial(last_kernel, 8 if square() else 0, rows, hidden, len(attend_grads) // 3),
        ([slab_shape] * 8 if square() else [])
        + [((length, width), F32), ((VECTORS, width), F32), ((width, 4 * width), BF16)],
        (
            x, first_low, *attend_grads, heads_full, attended, grad_branch,
            grad_middle, vectors, branch_sums, loss_sums, up_bias_part,
        ),
        positions,
        mib=40,
    )
    if square():
        slab_got = [swap(slabs[4 + at], 1) for at in (3, 1, 2, 0)]
        up_first = after(up_first, slabs[7])
        up_second = [add_low(keep_ux[1], up_first[0][1]), add_low(keep_uy[1], up_first[1][1])]
        up_got = [swap(up_second[0], 4), swap(up_second[1], 2)]

        down_half, down_mid = [], []
        gate = up_second
        for at in range(2):
            (came,) = after([down_in[at]], gate)
            down_half.append(add_low(down_narrow[at], came))
            down_mid += hop(down_half[-1:], ACROSS)
            gate = down_half[-1:]

        slab_got = after(slab_got, gate)
        both = [add_low(slabs[at], got) for at, got in zip((3, 1, 2, 0), slab_got)]
        slab_far = [swap(both[0], 6), swap(both[1], 2), swap(both[2], 4)]

        up_got = after(up_got, both)
        up_narrow = [
            add_low(keep_ux[0], up_first[0][0], up_got[0]),
            add_low(keep_uy[0], up_first[1][0], up_got[1]),
        ]
        up_in = hop(up_narrow, INWARD)

        gate = up_narrow
        down_total, down_out = [], []
        for at in range(2):
            (came,) = after([down_mid[at]], gate)
            down_total.append(add_low(down_half[at], came))
            down_out += hop(down_total[-1:], OUTWARD)
            gate = down_total[-1:]

        up_half, up_mid = [], []
        (came,) = after(up_in[:1], gate)
        up_half.append(add_low(up_narrow[0], came))
        up_mid += hop(up_half, ACROSS)

        slab_far = after(slab_far, up_half)
        cut = rows // 2 // SUBLANES * SUBLANES
        slab_narrow = [
            add_low(both[3][part], *[far[part] for far in slab_far])
            for part in (slice(0, cut), slice(cut, None))
        ]
        slab_in = hop(slab_narrow, INWARD)

        (came,) = after(up_in[1:], slab_narrow)
        up_half.append(add_low(up_narrow[1], came))
        up_mid += hop(up_half[1:], ACROSS)

        (came,) = after(up_mid[:1], up_half[1])
        up_total = [add_low(up_half[0], came)]
        up_out = hop(up_total, OUTWARD)

        gate = up_total
        slab_half, slab_mid = [], []
        for at in range(2):
            (came,) = after([slab_in[at]], gate)
            slab_half.append(add_low(slab_narrow[at], came))
            slab_mid += hop(slab_half[-1:], ACROSS)
            gate = slab_half[-1:]

        (came,) = after(up_mid[1:], gate)
        up_total.append(add_low(up_half[1], came))
        up_out += hop(up_total[1:], OUTWARD)

        gate = up_total[1]
        slab_total, slab_out = [], []
        for at in range(2):
            (came,) = after([slab_mid[at]], gate)
            slab_total.append(add_low(slab_half[at], came))
            slab_out += hop(slab_total[-1:], OUTWARD)
            gate = slab_total[-1:]

        down_out = after(down_out, gate)
        down_weight_sum = jnp.concatenate(
            [settle(*pair) for pair in zip(down_total, down_out)]
        ).astype(F32)
        up_out = after(up_out, gate)
        upper, lower = [settle(*pair) for pair in zip(up_total, up_out)]
        first = core == 0
        (up_weight_sum,) = call(
            functools.partial(join_kernel, hidden),
            [((rows, 2 * half), F32)],
            (jnp.where(first, upper, lower), swap(jnp.where(first, lower, upper), 1)),
            core_position,
        )
        slab_out = after(slab_out, up_weight_sum)
        heads_sum, output_sum, short = call(
            functools.partial(settle_kernel, cut, rows),
            [((rows, 3 * width), F32), ((rows, width), F32), ((VECTORS, 4 * width), F32)],
            (*slab_total, *slab_out),
            lax.axis_index("narrow").reshape(1).astype(jnp.int32),
        )
        vectors_sum = short[:, :rows]
        up_bias_grad = short[0, LANES : LANES + hidden]
        lanes_sum = short[:2, LANES + hidden : 2 * LANES + hidden]
        loss_sum = jnp.sum(lanes_sum[0])
        token_count = jnp.round(jnp.sum(lanes_sum[1])).astype(jnp.int32)
    else:
        down_weight_sum = collect_chips(down_parts[0].reshape(chips, hidden, width))
        down_weight_sum = sum_narrow(down_weight_sum).astype(F32)
        up_sum = sum_narrow(collect_chips(up_parts[0].reshape(chips, 2 * rows, half)))
        up_sum = up_sum.reshape(2, rows, chips, hidden)
        up_weight_sum = by_core(mine_of(up_sum, 0), swap(mine_of(up_sum, 0, 1), 1), 2)
        up_weight_sum = up_weight_sum.reshape(rows, 2 * half).astype(F32)
        short = short_sums.reshape(8, wide, rows).transpose(1, 0, 2).reshape(wide, 8 * rows)
        up_bias_rows = up_bias_part.reshape(chips, hidden)
        up_bias_rows = by_core(up_bias_rows, jnp.zeros_like(up_bias_rows), 1).reshape(wide, hidden)
        shared = jnp.broadcast_to(loss_sums[:1, :LANES], (wide, LANES))
        row = jnp.concatenate([short, up_bias_rows, shared], axis=1).astype(BF16)
        row = jnp.pad(row, ((0, 0), (0, 4 * width - row.shape[1])))
        slab = jnp.concatenate([attend_part.reshape(wide, rows, 4 * width), row[:, None]], axis=1)
        slab = sum_narrow(lax.psum_scatter(slab, "wide", scatter_dimension=0)).astype(F32)
        vectors_sum = slab[rows, : 8 * rows].reshape(8, rows)
        heads_sum, output_sum = slab[:rows, : 3 * width], slab[:rows, 3 * width :]
        up_bias_grad = slab[rows, 8 * rows : 8 * rows + hidden]
        loss_sum = jnp.sum(slab[rows, 8 * rows + hidden : 8 * rows + hidden + LANES])
        token_count = lax.psum(jnp.sum(loss_mask), ("narrow", "wide"))
    return (
        result_low[None],
        input_grad[None],
        vectors_sum[ATTEND_GAIN],
        vectors_sum[ATTEND_SHIFT],
        heads_sum,
        vectors_sum[QUERY_BIAS],
        vectors_sum[VALUE_BIAS],
        output_sum,
        vectors_sum[OUTPUT_BIAS],
        vectors_sum[FORWARD_GAIN],
        vectors_sum[FORWARD_SHIFT],
        up_weight_sum,
        up_bias_grad,
        down_weight_sum,
        vectors_sum[DOWN_BIAS],
        loss_sum,
        token_count,
    )


def solution(mesh):
    in_specs = (
        P(("narrow", "wide"), None, None),
        P(("narrow", "wide"), None),
        P(("narrow", "wide"), None),
        P(("narrow", "wide"), None),
        P(),
        P("wide"),
        P("wide"),
        P("wide", None),
        P("wide"),
        P("wide"),
        P("wide", None),
        P("wide"),
        P("wide"),
        P("wide"),
        P("wide", None),
        P("wide"),
        P("wide", None),
        P("wide"),
    )
    out_specs = (
        P(("narrow", "wide"), None, None),
        P(("narrow", "wide"), None, None),
        P("wide"),
        P("wide"),
        P("wide", None),
        P("wide"),
        P("wide"),
        P("wide", None),
        P("wide"),
        P("wide"),
        P("wide"),
        P("wide", None),
        P("wide"),
        P("wide", None),
        P("wide"),
        P(),
        P(),
    )
    return jax.shard_map(local, mesh=mesh, in_specs=in_specs, out_specs=out_specs, check_vma=False)
```

profile of v0, /device:TPU:0, one launch (start us, length us, event | category | flops | bytes accessed | tf_op | source)
XLA Modules:
  0.0 256.7 jit_solution(4835407516499861372)
XLA Ops:
  4.1 3.0 %collective-permute-start = (bf16[88,2560]{1,0:T(8,128)(2,1)S(1)}, bf16[88,2560]{1,0:T(8,128)(2,1)S(1)}, u32[]{:S(2)}, u32[]{:S(2)}) collective-permute-start(bf16[88,2560]{1,0:T(8,128)(2,1)S(1)} %shard_map.305.refs_0_), channel_id=1, source_target_pairs={{0,2},{1,3},{2,0},{3,1},{4,6},{5,7},{6,4},{7,5},{8,10},{9,11},{10,... | collective-permute-start | bytes 1351688 | tf_op jit(solution)/shard_map/ppermute | solution.py:704
  8.7 9.6 %collective-permute-done.refs_1_ = bf16[88,2560]{1,0:T(8,128)(2,1)S(1)} collective-permute-done((bf16[88,2560]{1,0:T(8,128)(2,1)S(1)}, bf16[88,2560]{1,0:T(8,128)(2,1)S(1)}, u32[]{:S(2)}, u32[]{:S(2)}) %collective-permute-start) | collective-permute-done | bytes 450592 | tf_op jit(solution)/shard_map/ppermute | solution.py:704
  20.6 8.0 %collective-permute-done.1.refs_2_ = bf16[88,2560]{1,0:T(8,128)(2,1)S(1)} collective-permute-done((bf16[88,2560]{1,0:T(8,128)(2,1)S(1)}, bf16[88,2560]{1,0:T(8,128)(2,1)S(1)}, u32[]{:S(2)}, u32[]{:S(2)}) %collective-permute-start.1) | collective-permute-done | bytes 450592 | tf_op jit(solution)/shard_map/ppermute | solution.py:704
  34.1 5.0 %shard_map.307 = (bf16[512,640]{1,0:T(8,128)(2,1)S(1)}, bf16[512,1920]{1,0:T(8,128)(2,1)S(1)}, bf16[640,1920]{1,0:T(8,128)(2,1)S(1)}, bf16[640,640]{1,0:T(8,128)...) custom-call(s32[8]{0:T(128)S(1)} %pad_add_fusion.position_ref, bf16[512,640]{1,0:T(8,128)(2,1)S(1)} %bitcast.56, ...), custom_call_target="tpu_custom_call" | custom-call | flops 1 | bytes 1 | tf_op jit(solution)/shard_map/pallas_call | solution.py:53
  40.5 7.9 %shard_map.308 = (bf16[512,640]{1,0:T(8,128)(2,1)S(1)}, f32[640,512]{1,0:T(8,128)S(1)}, f32[40,512]{1,0:T(8,128)S(1)}) custom-call(s32[512,1]{1,0:T(8,128)S(1)} %copy-done.7, s32[1,512]{1,0:T(1,128)S(1)} %copy-done.30, bf16[512,1920]{1,0:T(8,128)(2,1)S(1)} %get-tuple-element.122.q_ref.k_ref.v_ref, ...), custom_call_target="tpu_custom_call" | custom-call | flops 1 | bytes 1 | tf_op jit(solution)/shard_map/pallas_call | solution.py:53
  54.4 8.5 %collective-permute-done.11.refs_3_ = bf16[80,2560]{1,0:T(8,128)(2,1)S(1)} collective-permute-done((bf16[80,2560]{1,0:T(8,128)(2,1)}, bf16[80,2560]{1,0:T(8,128)(2,1)S(1)}, u32[]{:S(2)}, u32[]{:S(2)}) %collective-permute-start.11) | collective-permute-done | bytes 409632 | tf_op jit(solution)/shard_map/ppermute | solution.py:704
  64.9 9.0 %shard_map.310 = (bf16[1024,2560]{1,0:T(8,128)(2,1)S(1)}, bf16[1024,2560]{1,0:T(8,128)(2,1)S(1)}, bf16[640,2560]{1,0:T(8,128)(2,1)S(1)}) custom-call(s32[8]{0:T(128)S(1)} %pad_add_fusion.position_ref, bf16[512,640]{1,0:T(8,128)(2,1)S(1)} %get-tuple-element.127.own_ref.second_ref, bf16[512,640]{1,0:T(8,128)(2,1)S(1)} %collective-permute-done.7.other_ref.second_other_ref, ...), custom_call_target="tpu_custom_call" | custom-call | flops 1 | bytes 1 | tf_op jit(solution)/shard_map/pallas_call | solution.py:53
  74.0 1.6 collective-permute-start.19
  76.1 4.3 %collective-permute-done.15.refs_1_ = bf16[320,640]{1,0:T(8,128)(2,1)S(1)} collective-permute-done((bf16[320,640]{1,0:T(8,128)(2,1)S(1)}, bf16[320,640]{1,0:T(8,128)(2,1)S(1)}, u32[]{:S(2)}, u32[]{:S(2)}) %collective-permute-start.15) | collective-permute-done | bytes 409632 | tf_op jit(solution)/shard_map/ppermute | solution.py:704
  81.6 7.1 %collective-permute-done.19.refs_5_ = bf16[320,640]{1,0:T(8,128)(2,1)S(1)} collective-permute-done((bf16[320,640]{1,0:T(8,128)(2,1)S(1)}, bf16[320,640]{1,0:T(8,128)(2,1)S(1)}, u32[]{:S(2)}, u32[]{:S(2)}) %collective-permute-start.19) | collective-permute-done | bytes 409632 | tf_op jit(solution)/shard_map/ppermute | solution.py:704
  89.6 5.1 %shard_map.311 = (f32[512,640]{1,0:T(8,128)S(1)}, bf16[512,640]{1,0:T(8,128)(2,1)S(1)}, bf16[2560,640]{1,0:T(8,128)(2,1)S(1)}) custom-call(s32[7]{0:T(128)S(1)} %compare_select_fusion.position_ref, bf16[1024,2560]{1,0:T(8,128)(2,1)S(1)} %get-tuple-element.132.act_ref, bf16[640,640]{1,0:T(8,128)(2,1)S(1)} %copy-done.2, ...), custom_call_target="tpu_custom_call" | custom-call | flops 1 | bytes 1 | tf_op jit(solution)/shard_map/pallas_call | solution.py:53
  94.7 2.1 collective-permute-done.21.got_ref
  99.1 2.0 collective-permute-done.22.other_ref
  101.1 4.3 %shard_map.313 = (bf16[2,320,640]{2,1,0:T(8,128)(2,1)S(1)}, bf16[2,320,640]{2,1,0:T(8,128)(2,1)S(1)}, bf16[2,320,640]{2,1,0:T(8,128)(2,1)S(1)}, bf16[2,320,640]{2,1,0:T(8,128)(2,1)S(1)}) custom-call(s32[1]{0:T(128)} %bitcast.13.position_ref, bf16[1024,2560]{1,0:T(8,128)(2,1)S(1)} %get-tuple-element.132.act_ref, ...), custom_call_target="tpu_custom_call" | custom-call | flops 1 | bytes 1 | tf_op jit(solution)/shard_map/pallas_call | solution.py:53
  107.9 10.9 %shard_map.314 = (bf16[1024,2560]{1,0:T(8,128)(2,1)S(1)}, f32[1,2560]{1,0:T(1,128)S(1)}, bf16[2,80,2560]{2,1,0:T(8,128)(2,1)S(1)}, bf16[2,80,2560]{2,1,0:T(8,128...) custom-call(s32[1]{0:T(128)} %bitcast.13.position_ref, ...), custom_call_target="tpu_custom_call" | custom-call | flops 1 | bytes 1 | tf_op jit(solution)/shard_map/pallas_call | solution.py:53
  118.8 4.3 %shard_map.315 = (f32[512,640]{1,0:T(8,128)S(1)}, bf16[512,640]{1,0:T(8,128)(2,1)}) custom-call(bf16[1024,2560]{1,0:T(8,128)(2,1)S(1)} %get-tuple-element.146.grad_ref, bf16[640,2560]{1,0:T(8,128)(2,1)S(1)} %get-tuple-element.147.up_ref), custom_call_target="tpu_custom_call" | custom-call | flops 1 | bytes 1 | tf_op jit(solution)/shard_map/pallas_call | solution.py:53
  124.1 1.6 collective-permute-done.24
  131.8 5.2 %shard_map.316 = (f32[512,640]{1,0:T(8,128)S(1)}, bf16[512,640]{1,0:T(8,128)(2,1)S(1)}, bf16[512,640]{1,0:T(8,128)(2,1)S(1)}, f32[8,640]{1,0:T(8,128)S(1)}) custom-call(bf16[512,640]{1,0:T(8,128)(2,1)} %collective-permute-done.23.got_ref, f32[512,640]{1,0:T(8,128)} %copy-done.13, f32[512,640]{1,0:T(8,128)} %copy-done.1, f32[512,640]{1,0:T(8,128)} %copy-done.12, ...), custom_call_target="tpu_custom_call" | custom-call | flops 1 | bytes 1 | tf_op jit(solution)/shard_map/pallas_call | solution.py:53
  137.2 13.0 %shard_map.317 = (bf16[512,640]{1,0:T(8,128)(2,1)S(1)}, bf16[512,640]{1,0:T(8,128)(2,1)S(1)}, bf16[512,640]{1,0:T(8,128)(2,1)S(1)}) custom-call(s32[512,1]{1,0:T(8,128)S(1)} %copy-done.8, s32[1,512]{1,0:T(1,128)S(1)} %copy-done.30, bf16[512,1920]{1,0:T(8,128)(2,1)S(1)} %get-tuple-element.122.q_ref.k_ref.v_ref, ...), custom_call_target="tpu_custom_call" | custom-call | flops 1 | bytes 1 | tf_op jit(solution)/shard_map/pallas_call | solution.py:53
  151.6 3.5 %collective-permute-start.32 = (bf16[320,640]{1,0:T(8,128)(2,1)S(1)}, bf16[320,640]{1,0:T(8,128)(2,1)S(1)}, u32[]{:S(2)}, u32[]{:S(2)}) collective-permute-start(bf16[320,640]{1,0:T(8,128)(2,1)S(1)} %fusion.2), channel_id=1, source_target_pairs={{0,8},{24,16},{1,9},{25,17},{2,10},{26,18},{3,11},{27,19},{4,12},{... | collective-permute-start | bytes 1228808 | tf_op jit(solution)/shard_map/ppermute | solution.py:740
  156.3 1.6 collective-permute-start.33
  157.9 8.5 %shard_map.318 = (bf16[88,2560]{1,0:T(8,128)(2,1)S(1)}, bf16[88,2560]{1,0:T(8,128)(2,1)S(1)}, bf16[88,2560]{1,0:T(8,128)(2,1)S(1)}, bf16[88,2560]{1,0:T(8,128)(2...) custom-call(s32[8]{0:T(128)S(1)} %pad_add_fusion.position_ref, ...), custom_call_target="tpu_custom_call" | custom-call | flops 1 | bytes 1 | tf_op jit(solution)/shard_map/pallas_call | solution.py:53
  169.2 1.7 collective-permute-done.33
  172.1 1.6 collective-permute-start.40
  176.7 6.3 %collective-permute-done.39 = bf16[80,2560]{1,0:T(8,128)(2,1)S(1)} collective-permute-done((bf16[80,2560]{1,0:T(8,128)(2,1)S(1)}, bf16[80,2560]{1,0:T(8,128)(2,1)S(1)}, u32[]{:S(2)}, u32[]{:S(2)}) %collective-permute-start.39) | collective-permute-done | bytes 409632 | tf_op jit(solution)/shard_map/ppermute | solution.py:704
  188.0 4.4 %collective-permute-start.41 = (bf16[80,2560]{1,0:T(8,128)(2,1)S(1)}, bf16[80,2560]{1,0:T(8,128)(2,1)S(1)}, u32[]{:S(2)}, u32[]{:S(2)}) collective-permute-start(bf16[80,2560]{1,0:T(8,128)(2,1)S(1)} %fusion.1), channel_id=1, source_target_pairs={{0,8},{24,16},{1,9},{25,17},{2,10},{26,18},{3,11},{27,19},{4,12},{... | collective-permute-start | bytes 1228808 | tf_op jit(solution)/shard_map/ppermute | solution.py:740
  192.5 7.5 %collective-permute-start.46 = (bf16[80,2560]{1,0:T(8,128)(2,1)S(1)}, bf16[80,2560]{1,0:T(8,128)(2,1)S(1)}, u32[]{:S(2)}, u32[]{:S(2)}) collective-permute-start(bf16[80,2560]{1,0:T(8,128)(2,1)S(1)} %fusion), channel_id=1, source_target_pairs={{0,8},{24,16},{1,9},{25,17},{2,10},{26,18},{3,11},{27,19},{4,12},{... | collective-permute-start | bytes 1228808 | tf_op jit(solution)/shard_map/ppermute | solution.py:740
  204.4 7.4 %collective-permute-start.44 = (bf16[40,2560]{1,0:T(8,128)(2,1)S(1)}, bf16[40,2560]{1,0:T(8,128)(2,1)S(1)}, u32[]{:S(2)}, u32[]{:S(2)}) collective-permute-start(bf16[40,2560]{1,0:T(8,128)(2,1)S(1)} %add_convert_fusion.21), channel_id=1, source_target_pairs={{0,8},{24,16},{1,9},{25,17},{2,10},{26,18},{3,11},{27,19},{4,12},{... | collective-permute-start | bytes 614408 | tf_op jit(solution)/shard_map/ppermute | solution.py:740
  214.2 3.1 %collective-permute-done.44 = bf16[40,2560]{1,0:T(8,128)(2,1)S(1)} collective-permute-done((bf16[40,2560]{1,0:T(8,128)(2,1)S(1)}, bf16[40,2560]{1,0:T(8,128)(2,1)S(1)}, u32[]{:S(2)}, u32[]{:S(2)}) %collective-permute-start.44) | collective-permute-done | bytes 204832 | tf_op jit(solution)/shard_map/ppermute | solution.py:740
  225.6 4.7 %collective-permute-done.53 = bf16[80,2560]{1,0:T(8,128)(2,1)S(1)} collective-permute-done((bf16[80,2560]{1,0:T(8,128)(2,1)S(1)}, bf16[80,2560]{1,0:T(8,128)(2,1)S(1)}, u32[]{:S(2)}, u32[]{:S(2)}) %collective-permute-start.53) | collective-permute-done | bytes 409632 | tf_op jit(solution)/shard_map/ppermute | solution.py:740
  230.2 17.1 %collective-permute-done.54 = bf16[80,2560]{1,0:T(8,128)(2,1)S(1)} collective-permute-done((bf16[80,2560]{1,0:T(8,128)(2,1)S(1)}, bf16[80,2560]{1,0:T(8,128)(2,1)S(1)}, u32[]{:S(2)}, u32[]{:S(2)}) %collective-permute-start.54) | collective-permute-done | bytes 409632 | tf_op jit(solution)/shard_map/ppermute | solution.py:740
  250.6 1.6 collective-permute-done.52.refs_3_
  (227 shorter events, 71.8 us)
Async XLA Ops:
  7.2 21.5 %collective-permute-start.1 = (bf16[88,2560]{1,0:T(8,128)(2,1)S(1)}, bf16[88,2560]{1,0:T(8,128)(2,1)S(1)}, u32[]{:S(2)}, u32[]{:S(2)}) collective-permute-start(bf16[88,2560]{1,0:T(8,128)(2,1)S(1)} %shard_map.305.refs_0_), channel_id=1, source_target_pairs={{0,4},{1,5},{2,6},{3,7},{4,0},{5,1},{6,2},{7,3},{8,12},{9,13},{10,... | collective-permute-start | bytes 1351688 | tf_op jit(solution)/shard_map/ppermute | solution.py:704
  8.7 19.9 %collective-permute-start.2 = (bf16[88,2560]{1,0:T(8,128)(2,1)S(1)}, bf16[88,2560]{1,0:T(8,128)(2,1)S(1)}, u32[]{:S(2)}, u32[]{:S(2)}) collective-permute-start(bf16[88,2560]{1,0:T(8,128)(2,1)S(1)} %shard_map.305.refs_0_), channel_id=1, source_target_pairs={{0,6},{1,7},{2,4},{3,5},{4,2},{5,3},{6,0},{7,1},{8,14},{9,15},{10,... | collective-permute-start | bytes 1351688 | tf_op jit(solution)/shard_map/ppermute | solution.py:704
  8.7 22.0 %collective-permute-start.3 = (bf16[88,2560]{1,0:T(8,128)(2,1)S(1)}, bf16[88,2560]{1,0:T(8,128)(2,1)S(1)}, u32[]{:S(2)}, u32[]{:S(2)}) collective-permute-start(bf16[88,2560]{1,0:T(8,128)(2,1)S(1)} %shard_map.305.refs_0_), channel_id=1, source_target_pairs={{0,1},{1,0},{2,3},{3,2},{4,5},{5,4},{6,7},{7,6},{8,9},{9,8},{10,11... | collective-permute-start | bytes 1351688 | tf_op jit(solution)/shard_map/ppermute | solution.py:704
  29.2 20.3 %collective-permute-start.9 = (bf16[80,2560]{1,0:T(8,128)(2,1)}, bf16[80,2560]{1,0:T(8,128)(2,1)}, u32[]{:S(2)}, u32[]{:S(2)}) collective-permute-start(bf16[80,2560]{1,0:T(8,128)(2,1)} %get-tuple-element.119.refs_0_), channel_id=1, source_target_pairs={{0,4},{1,5},{2,6},{3,7},{4,0},{5,1},{6,2},{7,3},{8,12},{9,13},{10,... | collective-permute-start | bytes 1228808 | tf_op jit(solution)/shard_map/ppermute | solution.py:704
  30.7 20.8 %collective-permute-start.8 = (bf16[80,2560]{1,0:T(8,128)(2,1)}, bf16[80,2560]{1,0:T(8,128)(2,1)}, u32[]{:S(2)}, u32[]{:S(2)}) collective-permute-start(bf16[80,2560]{1,0:T(8,128)(2,1)} %get-tuple-element.119.refs_0_), channel_id=1, source_target_pairs={{0,2},{1,3},{2,0},{3,1},{4,6},{5,7},{6,4},{7,5},{8,10},{9,11},{10,... | collective-permute-start | bytes 1228808 | tf_op jit(solution)/shard_map/ppermute | solution.py:704
  31.3 19.0 %collective-permute-start.10 = (bf16[80,2560]{1,0:T(8,128)(2,1)}, bf16[80,2560]{1,0:T(8,128)(2,1)}, u32[]{:S(2)}, u32[]{:S(2)}) collective-permute-start(bf16[80,2560]{1,0:T(8,128)(2,1)} %get-tuple-element.129), channel_id=1, source_target_pairs={{0,3},{1,2},{2,1},{3,0},{4,7},{5,6},{6,5},{7,4},{8,11},{9,10},{10,... | collective-permute-start | bytes 1228808 | tf_op jit(solution)/shard_map/ppermute | solution.py:704
  31.9 22.0 %collective-permute-start.12 = (bf16[80,2560]{1,0:T(8,128)(2,1)}, bf16[80,2560]{1,0:T(8,128)(2,1)}, u32[]{:S(2)}, u32[]{:S(2)}) collective-permute-start(bf16[80,2560]{1,0:T(8,128)(2,1)} %get-tuple-element.129), channel_id=1, source_target_pairs={{0,1},{1,0},{2,3},{3,2},{4,5},{5,4},{6,7},{7,6},{8,9},{9,8},{10,11... | collective-permute-start | bytes 1228808 | tf_op jit(solution)/shard_map/ppermute | solution.py:704
  32.9 19.5 %collective-permute-start.13 = (bf16[80,2560]{1,0:T(8,128)(2,1)}, bf16[80,2560]{1,0:T(8,128)(2,1)}, u32[]{:S(2)}, u32[]{:S(2)}) collective-permute-start(bf16[80,2560]{1,0:T(8,128)(2,1)} %get-tuple-element.129), channel_id=1, source_target_pairs={{0,5},{1,4},{2,7},{3,6},{4,1},{5,0},{6,3},{7,2},{8,13},{9,12},{10,... | collective-permute-start | bytes 1228808 | tf_op jit(solution)/shard_map/ppermute | solution.py:704
  49.5 15.4 %collective-permute-start.7 = (bf16[512,640]{1,0:T(8,128)(2,1)S(1)}, bf16[512,640]{1,0:T(8,128)(2,1)S(1)}, u32[]{:S(2)}, u32[]{:S(2)}) collective-permute-start(bf16[512,640]{1,0:T(8,128)(2,1)S(1)} %get-tuple-element.127.own_ref.second_ref), channel_id=1, source_target_pairs={{0,1},{1,0},{2,3},{3,2},{4,5},{5,4},{6,7},{7,6},{8,9},{9,8},{10,11... | collective-permute-start | bytes 1966088 | tf_op jit(solution)/shard_map/ppermute | solution.py:704
  52.4 21.6 %collective-permute-start.16 = (bf16[320,640]{1,0:T(8,128)(2,1)S(1)}, bf16[320,640]{1,0:T(8,128)(2,1)S(1)}, u32[]{:S(2)}, u32[]{:S(2)}) collective-permute-start(bf16[320,640]{1,0:T(8,128)(2,1)S(1)} %get-tuple-element.134), channel_id=1, source_target_pairs={{0,2},{1,3},{2,0},{3,1},{4,6},{5,7},{6,4},{7,5},{8,10},{9,11},{10,... | collective-permute-start | bytes 1228808 | tf_op jit(solution)/shard_map/ppermute | solution.py:704
  53.9 20.1 %collective-permute-start.17 = (bf16[320,640]{1,0:T(8,128)(2,1)S(1)}, bf16[320,640]{1,0:T(8,128)(2,1)S(1)}, u32[]{:S(2)}, u32[]{:S(2)}) collective-permute-start(bf16[320,640]{1,0:T(8,128)(2,1)S(1)} %get-tuple-element.133), channel_id=1, source_target_pairs={{0,4},{1,5},{2,6},{3,7},{4,0},{5,1},{6,2},{7,3},{8,12},{9,13},{10,... | collective-permute-start | bytes 1228808 | tf_op jit(solution)/shard_map/ppermute | solution.py:704
  62.9 17.6 %collective-permute-start.15 = (bf16[320,640]{1,0:T(8,128)(2,1)S(1)}, bf16[320,640]{1,0:T(8,128)(2,1)S(1)}, u32[]{:S(2)}, u32[]{:S(2)}) collective-permute-start(bf16[320,640]{1,0:T(8,128)(2,1)S(1)} %get-tuple-element.133), channel_id=1, source_target_pairs={{0,2},{1,3},{2,0},{3,1},{4,6},{5,7},{6,4},{7,5},{8,10},{9,11},{10,... | collective-permute-start | bytes 1228808 | tf_op jit(solution)/shard_map/ppermute | solution.py:704
  64.0 17.6 %collective-permute-start.18 = (bf16[320,640]{1,0:T(8,128)(2,1)S(1)}, bf16[320,640]{1,0:T(8,128)(2,1)S(1)}, u32[]{:S(2)}, u32[]{:S(2)}) collective-permute-start(bf16[320,640]{1,0:T(8,128)(2,1)S(1)} %get-tuple-element.134), channel_id=1, source_target_pairs={{0,4},{1,5},{2,6},{3,7},{4,0},{5,1},{6,2},{7,3},{8,12},{9,13},{10,... | collective-permute-start | bytes 1228808 | tf_op jit(solution)/shard_map/ppermute | solution.py:704
  74.0 14.8 %collective-permute-start.19 = (bf16[320,640]{1,0:T(8,128)(2,1)S(1)}, bf16[320,640]{1,0:T(8,128)(2,1)S(1)}, u32[]{:S(2)}, u32[]{:S(2)}) collective-permute-start(bf16[320,640]{1,0:T(8,128)(2,1)S(1)} %collective-permute-done.17.refs_3_), channel_id=1, source_target_pairs={{0,2},{1,3},{2,0},{3,1},{4,6},{5,7},{6,4},{7,5},{8,10},{9,11},{10,... | collective-permute-start | bytes 1228808 | tf_op jit(solution)/shard_map/ppermute | solution.py:704
  105.4 20.3 %collective-permute-start.24 = (bf16[2,320,640]{2,1,0:T(8,128)(2,1)S(1)}, bf16[2,320,640]{2,1,0:T(8,128)(2,1)S(1)}, u32[]{:S(2)}, u32[]{:S(2)}) collective-permute-start(bf16[2,320,640]{2,1,0:T(8,128)(2,1)S(1)} %get-tuple-element.142), channel_id=1, source_target_pairs={{0,2},{1,3},{2,0},{3,1},{4,6},{5,7},{6,4},{7,5},{8,10},{9,11},{10,... | collective-permute-start | bytes 2457608 | tf_op jit(solution)/shard_map/ppermute | solution.py:704
  106.4 21.3 %collective-permute-start.25 = (bf16[2,320,640]{2,1,0:T(8,128)(2,1)S(1)}, bf16[2,320,640]{2,1,0:T(8,128)(2,1)S(1)}, u32[]{:S(2)}, u32[]{:S(2)}) collective-permute-start(bf16[2,320,640]{2,1,0:T(8,128)(2,1)S(1)} %get-tuple-element.151), channel_id=1, source_target_pairs={{0,4},{1,5},{2,6},{3,7},{4,0},{5,1},{6,2},{7,3},{8,12},{9,13},{10,... | collective-permute-start | bytes 2457608 | tf_op jit(solution)/shard_map/ppermute | solution.py:704
  126.8 23.4 %collective-permute-start.26 = (bf16[320,640]{1,0:T(8,128)(2,1)}, bf16[320,640]{1,0:T(8,128)(2,1)}, u32[]{:S(2)}, u32[]{:S(2)}) collective-permute-start(bf16[320,640]{1,0:T(8,128)(2,1)} %fusion.4), channel_id=1, source_target_pairs={{0,4},{1,5},{2,6},{3,7},{4,0},{5,1},{6,2},{7,3},{8,12},{9,13},{10,... | collective-permute-start | bytes 1228808 | tf_op jit(solution)/shard_map/ppermute | solution.py:704
  128.7 21.6 %collective-permute-start.27 = (bf16[320,640]{1,0:T(8,128)(2,1)}, bf16[320,640]{1,0:T(8,128)(2,1)}, u32[]{:S(2)}, u32[]{:S(2)}) collective-permute-start(bf16[320,640]{1,0:T(8,128)(2,1)} %fusion.5), channel_id=1, source_target_pairs={{0,2},{1,3},{2,0},{3,1},{4,6},{5,7},{6,4},{7,5},{8,10},{9,11},{10,... | collective-permute-start | bytes 1228808 | tf_op jit(solution)/shard_map/ppermute | solution.py:704
  130.2 36.3 %collective-permute-start.34 = (bf16[2,80,2560]{2,1,0:T(8,128)(2,1)}, bf16[2,80,2560]{2,1,0:T(8,128)(2,1)}, u32[]{:S(2)}, u32[]{:S(2)}) collective-permute-start(bf16[2,80,2560]{2,1,0:T(8,128)(2,1)} %get-tuple-element.181), channel_id=1, source_target_pairs={{0,2},{1,3},{2,0},{3,1},{4,6},{5,7},{6,4},{7,5},{8,10},{9,11},{10,... | collective-permute-start | bytes 2457608 | tf_op jit(solution)/shard_map/ppermute | solution.py:704
  130.7 36.2 %collective-permute-start.35 = (bf16[2,80,2560]{2,1,0:T(8,128)(2,1)}, bf16[2,80,2560]{2,1,0:T(8,128)(2,1)}, u32[]{:S(2)}, u32[]{:S(2)}) collective-permute-start(bf16[2,80,2560]{2,1,0:T(8,128)(2,1)} %get-tuple-element.182), channel_id=1, source_target_pairs={{0,4},{1,5},{2,6},{3,7},{4,0},{5,1},{6,2},{7,3},{8,12},{9,13},{10,... | collective-permute-start | bytes 2457608 | tf_op jit(solution)/shard_map/ppermute | solution.py:704
  151.6 19.4 %collective-permute-start.32 = (bf16[320,640]{1,0:T(8,128)(2,1)S(1)}, bf16[320,640]{1,0:T(8,128)(2,1)S(1)}, u32[]{:S(2)}, u32[]{:S(2)}) collective-permute-start(bf16[320,640]{1,0:T(8,128)(2,1)S(1)} %fusion.2), channel_id=1, source_target_pairs={{0,8},{24,16},{1,9},{25,17},{2,10},{26,18},{3,11},{27,19},{4,12},{... | collective-permute-start | bytes 1228808 | tf_op jit(solution)/shard_map/ppermute | solution.py:740
  156.3 14.6 %collective-permute-start.33 = (bf16[320,640]{1,0:T(8,128)(2,1)S(1)}, bf16[320,640]{1,0:T(8,128)(2,1)S(1)}, u32[]{:S(2)}, u32[]{:S(2)}) collective-permute-start(bf16[320,640]{1,0:T(8,128)(2,1)S(1)} %fusion.3), channel_id=1, source_target_pairs={{0,8},{24,16},{1,9},{25,17},{2,10},{26,18},{3,11},{27,19},{4,12},{... | collective-permute-start | bytes 1228808 | tf_op jit(solution)/shard_map/ppermute | solution.py:740
  174.3 18.2 %collective-permute-start.42 = (bf16[320,640]{1,0:T(8,128)(2,1)S(1)}, bf16[320,640]{1,0:T(8,128)(2,1)S(1)}, u32[]{:S(2)}, u32[]{:S(2)}) collective-permute-start(bf16[320,640]{1,0:T(8,128)(2,1)S(1)} %add_convert_fusion.10), channel_id=1, source_target_pairs={{8,16},{16,8},{9,17},{17,9},{10,18},{18,10},{11,19},{19,11},{12,20... | collective-permute-start | bytes 1228808 | tf_op jit(solution)/shard_map/ppermute | solution.py:740
  175.2 27.1 %collective-permute-start.36 = (bf16[88,2560]{1,0:T(8,128)(2,1)S(1)}, bf16[88,2560]{1,0:T(8,128)(2,1)S(1)}, u32[]{:S(2)}, u32[]{:S(2)}) collective-permute-start(bf16[88,2560]{1,0:T(8,128)(2,1)S(1)} %add_convert_fusion.2), channel_id=1, source_target_pairs={{0,6},{1,7},{2,4},{3,5},{4,2},{5,3},{6,0},{7,1},{8,14},{9,15},{10,... | collective-permute-start | bytes 1351688 | tf_op jit(solution)/shard_map/ppermute | solution.py:704
  182.9 20.6 %collective-permute-start.37 = (bf16[88,2560]{1,0:T(8,128)(2,1)S(1)}, bf16[88,2560]{1,0:T(8,128)(2,1)S(1)}, u32[]{:S(2)}, u32[]{:S(2)}) collective-permute-start(bf16[88,2560]{1,0:T(8,128)(2,1)S(1)} %add_convert_fusion.1), channel_id=1, source_target_pairs={{0,2},{1,3},{2,0},{3,1},{4,6},{5,7},{6,4},{7,5},{8,10},{9,11},{10,... | collective-permute-start | bytes 1351688 | tf_op jit(solution)/shard_map/ppermute | solution.py:704
  184.5 19.8 %collective-permute-start.38 = (bf16[88,2560]{1,0:T(8,128)(2,1)S(1)}, bf16[88,2560]{1,0:T(8,128)(2,1)S(1)}, u32[]{:S(2)}, u32[]{:S(2)}) collective-permute-start(bf16[88,2560]{1,0:T(8,128)(2,1)S(1)} %add_convert_fusion), channel_id=1, source_target_pairs={{0,4},{1,5},{2,6},{3,7},{4,0},{5,1},{6,2},{7,3},{8,12},{9,13},{10,... | collective-permute-start | bytes 1351688 | tf_op jit(solution)/shard_map/ppermute | solution.py:704
  192.5 19.5 %collective-permute-start.46 = (bf16[80,2560]{1,0:T(8,128)(2,1)S(1)}, bf16[80,2560]{1,0:T(8,128)(2,1)S(1)}, u32[]{:S(2)}, u32[]{:S(2)}) collective-permute-start(bf16[80,2560]{1,0:T(8,128)(2,1)S(1)} %fusion), channel_id=1, source_target_pairs={{0,8},{24,16},{1,9},{25,17},{2,10},{26,18},{3,11},{27,19},{4,12},{... | collective-permute-start | bytes 1228808 | tf_op jit(solution)/shard_map/ppermute | solution.py:740
  200.9 23.4 %collective-permute-start.56 = (bf16[320,640]{1,0:T(8,128)(2,1)S(1)}, bf16[320,640]{1,0:T(8,128)(2,1)S(1)}, u32[]{:S(2)}, u32[]{:S(2)}) collective-permute-start(bf16[320,640]{1,0:T(8,128)(2,1)S(1)} %add_convert_fusion.9), channel_id=1, source_target_pairs={{8,0},{16,24},{9,1},{17,25},{10,2},{18,26},{11,3},{19,27},{12,4},{... | collective-permute-start | bytes 1228808 | tf_op jit(solution)/shard_map/ppermute | solution.py:740
  202.3 23.3 %collective-permute-start.57 = (bf16[320,640]{1,0:T(8,128)(2,1)S(1)}, bf16[320,640]{1,0:T(8,128)(2,1)S(1)}, u32[]{:S(2)}, u32[]{:S(2)}) collective-permute-start(bf16[320,640]{1,0:T(8,128)(2,1)S(1)} %add_convert_fusion.8), channel_id=1, source_target_pairs={{8,0},{16,24},{9,1},{17,25},{10,2},{18,26},{11,3},{19,27},{12,4},{... | collective-permute-start | bytes 1228808 | tf_op jit(solution)/shard_map/ppermute | solution.py:740
  221.5 25.9 %collective-permute-start.54 = (bf16[80,2560]{1,0:T(8,128)(2,1)S(1)}, bf16[80,2560]{1,0:T(8,128)(2,1)S(1)}, u32[]{:S(2)}, u32[]{:S(2)}) collective-permute-start(bf16[80,2560]{1,0:T(8,128)(2,1)S(1)} %add_convert_fusion.4), channel_id=1, source_target_pairs={{8,0},{16,24},{9,1},{17,25},{10,2},{18,26},{11,3},{19,27},{12,4},{... | collective-permute-start | bytes 1228808 | tf_op jit(solution)/shard_map/ppermute | solution.py:740
  222.9 27.7 %collective-permute-start.51 = (bf16[40,2560]{1,0:T(8,128)(2,1)S(1)}, bf16[40,2560]{1,0:T(8,128)(2,1)S(1)}, u32[]{:S(2)}, u32[]{:S(2)}) collective-permute-start(bf16[40,2560]{1,0:T(8,128)(2,1)S(1)} %add_convert_fusion.19.refs_0_), channel_id=1, source_target_pairs={{8,0},{16,24},{9,1},{17,25},{10,2},{18,26},{11,3},{19,27},{12,4},{... | collective-permute-start | bytes 614408 | tf_op jit(solution)/shard_map/ppermute | solution.py:740
  224.2 28.0 %collective-permute-start.52 = (bf16[48,2560]{1,0:T(8,128)(2,1)S(1)}, bf16[48,2560]{1,0:T(8,128)(2,1)S(1)}, u32[]{:S(2)}, u32[]{:S(2)}) collective-permute-start(bf16[48,2560]{1,0:T(8,128)(2,1)S(1)} %add_convert_fusion.16.refs_1_), channel_id=1, source_target_pairs={{8,0},{16,24},{9,1},{17,25},{10,2},{18,26},{11,3},{19,27},{12,4},{... | collective-permute-start | bytes 737288 | tf_op jit(solution)/shard_map/ppermute | solution.py:740
  (70 other events, 687.3 us)
where the time goes:
time: 258 us; the launch traced here: 257 us
  waiting for transfers between devices  82.9 us (32%)
  Pallas kernels  78.6 us (30%)
  starting transfers between devices  68.3 us (26%)
  other arithmetic  12.9 us (5%)
  local copies, waits for them, and re-layouts  10.6 us (4%)
  between operations  3.42 us (1%)
    pallas_call x16, Pallas kernels, call(): pl.pallas_call(kernel, out_shape=shapes, grid_spec=pltpu.PrefetchScalarGr...  78.6 us
    ppermute x40, waiting for transfers between devices, swap(): lax.ppermute(values, 'wide', [(i, i ^ bit) for i in range(lax.axis_size('...  52.6 us
    ppermute x18, starting transfers between devices, hop(): return [lax.ppermute(part, 'narrow', pairs) for part in parts]  37.5 us
    ppermute x40, starting transfers between devices, swap(): lax.ppermute(values, 'wide', [(i, i ^ bit) for i in range(lax.axis_size('...  30.8 us
    ppermute x18, waiting for transfers between devices, hop(): return [lax.ppermute(part, 'narrow', pairs) for part in parts]  30.3 us
    convert_element_type x26, other arithmetic, add_low(): return sum((part.astype(F32) for part in parts)).astype(BF16)  10.7 us
    unnamed x88, local copies, waits for them, and re-layouts  6.94 us
  transfers between devices with their start and end apart: 58, of which 20 were waited for; matrix products, arithmetic and copies ran while one was open for 5% of the time, Pallas kernels for 26%

commit v1 on v0

--- a/solution.py
+++ b/solution.py
@@ -640,7 +640,7 @@
     grad_refs, refs = refs[: 3 * pieces], refs[3 * pieces :]
     heads_ref, attended_ref, branch_ref, grad_ref, vector_ref, *refs = refs
     sums_ref, loss_ref, up_ref, *refs = refs
-    slabs, (input_ref, vectors_ref, full_ref) = refs[:count], refs[count:]
+    stacks, (input_ref, vectors_ref, full_ref) = refs[:-3], refs[-3:]
     width = x_ref.shape[1]
 
     def grads(which, here):
@@ -672,7 +672,8 @@
     vectors_ref[...] = vectors
     blank = jnp.zeros((VECTORS - 1, hidden), F32)
     lanes = jnp.concatenate([loss_ref[:2, :LANES], jnp.zeros((VECTORS - 2, LANES), F32)], axis=0)
-    for at, slab in enumerate(slabs):
+    for at in range(count):
+        slab = stacks[at // (count // 2)].at[at % (count // 2)]
         place_at = position_ref[at]
         begin = pl.multiple_of(place_at * rows, SUBLANES)
         slab[:rows, :] = full_ref[pl.ds(begin, rows), :]
@@ -687,8 +688,9 @@
         slab[rows:, :] = jnp.concatenate([row, pad], axis=1)
 
 
-def settle_kernel(cut, rows, place_ref, *refs):
-    totals, outers, (heads_ref, out_ref, short_ref) = refs[:2], refs[2:4], refs[4:]
+def settle_kernel(cut, rows, hidden, place_ref, *refs):
+    totals, outers, refs = refs[:2], refs[2:4], refs[4:]
+    heads_ref, out_ref, short_ref, loss_ref, count_ref = refs
     width = out_ref.shape[1]
     inner = (place_ref[0] == 1) | (place_ref[0] == 2)
     chosen = [
@@ -697,7 +699,11 @@
     for begin, end, values in ((0, cut, chosen[0]), (cut, rows, chosen[1])):
         heads_ref[begin:end, :] = values[: end - begin, : 3 * width]
         out_ref[begin:end, :] = values[: end - begin, 3 * width :]
-    short_ref[...] = chosen[1][rows - cut :]
+    short = chosen[1][rows - cut :]
+    short_ref[...] = short
+    lanes = short[:, LANES + hidden : 2 * LANES + hidden]
+    loss_ref[0] = jnp.sum(lanes[0:1])
+    count_ref[0] = jnp.sum(lanes[1:2]).astype(jnp.int32)
 
 
 def swap(values, bit):
@@ -800,7 +806,10 @@
             (heads_weight, output_weight, short, up_bias[None]),
         )
         near_x, near_y, far = swap(slab, 2), swap(slab, 4), swap(slab, 6)
-        (up_weight,) = after([up_weight], near_x)
+        devices = 2 * (chip ^ offsets) + core
+        positions = jnp.concatenate([devices, devices ^ 1]).astype(jnp.int32)
+        up_positions = positions
+        up_weight, column, positions = after([up_weight, column, positions], near_x)
         up_mine, up_other = call(
             functools.partial(halves_kernel, hidden),
             [((rows, half), BF16)] * 2,
@@ -809,12 +818,9 @@
         )
         other_x, mine_y = swap(up_other, 3), swap(up_mine, 4)
         mine_x, other_y = swap(up_mine, 2), swap(up_other, 5)
-        near_y, far = after([near_y, far], up_mine)
-        slabs = [slab, near_x, near_y, far]
-        slabs = slabs + [swap(part, 1) for part in slabs]
-        devices = 2 * (chip ^ offsets) + core
-        positions = jnp.concatenate([devices, devices ^ 1]).astype(jnp.int32)
-        up_positions = positions
+        swapped = [swap(slab, 1), swap(near_x, 1)]
+        near_y, far = after([near_y, far], up_mine, swapped)
+        slabs = [slab, near_x, near_y, far, *swapped, swap(near_y, 1), swap(far, 1)]
         first_low, joined, heads_full, output_full, vectors, up_bias_half = call(
             functools.partial(project_kernel, len(slabs), rows, hidden),
             [
@@ -946,18 +952,19 @@
 
     if square():
         attend_grads = attend_back(joined, column, segments, grad_attended, across, lse)
+        down_got = after(down_got, attend_grads[0])
         down_narrow = [
-            add_low(keep_dx[0], down_first[0][0], after([down_got[0]], attend_grads[0])[0]),
-            add_low(keep_dy[0], down_first[1][0], after([down_got[1]], attend_grads[0])[0]),
+            add_low(keep_dx[0], down_first[0][0], down_got[0]),
+            add_low(keep_dy[0], down_first[1][0], down_got[1]),
         ]
         down_in = hop(down_narrow, INWARD)
         attend_grads = after(attend_grads, down_narrow)
     else:
         attend_grads = attend_back(joined, column, segments, grad_attended, across, lse)
-    slab_shape = ((rows + VECTORS, 4 * width), BF16)
-    *slabs, input_grad, short_sums, attend_part = call(
+    stack_shape = ((4, rows + VECTORS, 4 * width), BF16)
+    *stacks, input_grad, short_sums, attend_part = call(
         functools.partial(last_kernel, 8 if square() else 0, rows, hidden, len(attend_grads) // 3),
-        ([slab_shape] * 8 if square() else [])
+        ([stack_shape] * 2 if square() else [])
         + [((length, width), F32), ((VECTORS, width), F32), ((width, 4 * width), BF16)],
         (
             x, first_low, *attend_grads, heads_full, attended, grad_branch,
@@ -967,22 +974,19 @@
         mib=40,
     )
     if square():
-        slab_got = [swap(slabs[4 + at], 1) for at in (3, 1, 2, 0)]
-        up_first = after(up_first, slabs[7])
+        mine, others = stacks
+        mine_got = swap(others, 1)
+        up_first = after(up_first, mine)
         up_second = [add_low(keep_ux[1], up_first[0][1]), add_low(keep_uy[1], up_first[1][1])]
         up_got = [swap(up_second[0], 4), swap(up_second[1], 2)]
 
-        down_half, down_mid = [], []
-        gate = up_second
-        for at in range(2):
-            (came,) = after([down_in[at]], gate)
-            down_half.append(add_low(down_narrow[at], came))
-            down_mid += hop(down_half[-1:], ACROSS)
-            gate = down_half[-1:]
-
-        slab_got = after(slab_got, gate)
-        both = [add_low(slabs[at], got) for at, got in zip((3, 1, 2, 0), slab_got)]
-        slab_far = [swap(both[0], 6), swap(both[1], 2), swap(both[2], 4)]
+        down_in = after(down_in, up_second)
+        down_half = jnp.concatenate(add_each(down_narrow, down_in))
+        (down_mid,) = hop([down_half], ACROSS)
+
+        (mine_got,) = after([mine_got], down_half)
+        both = [add_low(mine[at], mine_got[at]) for at in range(4)]
+        slab_far = [swap(both[3], 6), swap(both[1], 2), swap(both[2], 4)]
 
         up_got = after(up_got, both)
         up_narrow = [
@@ -991,48 +995,43 @@
         ]
         up_in = hop(up_narrow, INWARD)
 
-        gate = up_narrow
-        down_total, down_out = [], []
-        for at in range(2):
-            (came,) = after([down_mid[at]], gate)
-            down_total.append(add_low(down_half[at], came))
-            down_out += hop(down_total[-1:], OUTWARD)
-            gate = down_total[-1:]
-
-        up_half, up_mid = [], []
-        (came,) = after(up_in[:1], gate)
-        up_half.append(add_low(up_narrow[0], came))
-        up_mid += hop(up_half, ACROSS)
-
-        slab_far = after(slab_far, up_half)
+        (came,) = after(up_in[:1], up_narrow)
+        up_half = [add_low(up_narrow[0], came)]
+        up_mid = hop(up_half, ACROSS)
+
+        (down_mid,) = after([down_mid], up_half)
+        down_total = add_low(down_half, down_mid)
+        (down_out,) = hop([down_total], OUTWARD)
+
+        (came,) = after(up_in[1:], down_total)
+        up_half.append(add_low(up_narrow[1], came))
+        up_mid += hop(up_half[1:], ACROSS)
+
+        slab_far = after(slab_far, up_half[1])
         cut = rows // 2 // SUBLANES * SUBLANES
         slab_narrow = [
-            add_low(both[3][part], *[far[part] for far in slab_far])
+            add_low(both[0][part], *[far[part] for far in slab_far])
             for part in (slice(0, cut), slice(cut, None))
         ]
         slab_in = hop(slab_narrow, INWARD)
 
-        (came,) = after(up_in[1:], slab_narrow)
-        up_half.append(add_low(up_narrow[1], came))
-        up_mid += hop(up_half[1:], ACROSS)
-
-        (came,) = after(up_mid[:1], up_half[1])
+        (came,) = after(up_mid[:1], slab_narrow)
         up_total = [add_low(up_half[0], came)]
         up_out = hop(up_total, OUTWARD)
 
-        gate = up_total
-        slab_half, slab_mid = [], []
-        for at in range(2):
-            (came,) = after([slab_in[at]], gate)
-            slab_half.append(add_low(slab_narrow[at], came))
-            slab_mid += hop(slab_half[-1:], ACROSS)
-            gate = slab_half[-1:]
-
-        (came,) = after(up_mid[1:], gate)
+        (came,) = after(slab_in[:1], up_total)
+        slab_half = [add_low(slab_narrow[0], came)]
+        slab_mid = hop(slab_half, ACROSS)
+
+        (came,) = after(up_mid[1:], slab_half)
         up_total.append(add_low(up_half[1], came))
         up_out += hop(up_total[1:], OUTWARD)
 
-        gate = up_total[1]
+        (came,) = after(slab_in[1:], up_total[1])
+        slab_half.append(add_low(slab_narrow[1], came))
+        slab_mid += hop(slab_half[1:], ACROSS)
+
+        gate = slab_half[1]
         slab_total, slab_out = [], []
         for at in range(2):
             (came,) = after([slab_mid[at]], gate)
@@ -1040,10 +1039,8 @@
             slab_out += hop(slab_total[-1:], OUTWARD)
             gate = slab_total[-1:]
 
-        down_out = after(down_out, gate)
-        down_weight_sum = jnp.concatenate(
-            [settle(*pair) for pair in zip(down_total, down_out)]
-        ).astype(F32)
+        (down_out,) = after([down_out], gate)
+        down_weight_sum = settle(down_total, down_out).astype(F32)
         up_out = after(up_out, gate)
         upper, lower = [settle(*pair) for pair in zip(up_total, up_out)]
         first = core == 0
@@ -1054,17 +1051,20 @@
             core_position,
         )
         slab_out = after(slab_out, up_weight_sum)
-        heads_sum, output_sum, short = call(
-            functools.partial(settle_kernel, cut, rows),
-            [((rows, 3 * width), F32), ((rows, width), F32), ((VECTORS, 4 * width), F32)],
+        scalar = pl.BlockSpec(memory_space=pltpu.SMEM)
+        heads_sum, output_sum, short, loss_sum, token_count = call(
+            functools.partial(settle_kernel, cut, rows, hidden),
+            [
+                ((rows, 3 * width), F32), ((rows, width), F32), ((VECTORS, 4 * width), F32),
+                ((1,), F32), ((1,), jnp.int32),
+            ],
             (*slab_total, *slab_out),
             lax.axis_index("narrow").reshape(1).astype(jnp.int32),
+            out_specs=[vmem, vmem, vmem, scalar, scalar],
         )
         vectors_sum = short[:, :rows]
         up_bias_grad = short[0, LANES : LANES + hidden]
-        lanes_sum = short[:2, LANES + hidden : 2 * LANES + hidden]
-        loss_sum = jnp.sum(lanes_sum[0])
-        token_count = jnp.round(jnp.sum(lanes_sum[1])).astype(jnp.int32)
+        loss_sum, token_count = loss_sum.reshape(()), token_count.reshape(())
     else:
         down_weight_sum = collect_chips(down_parts[0].reshape(chips, hidden, width))
         down_weight_sum = sum_narrow(down_weight_sum).astype(F32)

time: 258 us -> 259 us (level)
  waiting for transfers between devices: 82.9 us -> 94.4 us
  starting transfers between devices: 68.3 us -> 59.1 us
    ppermute x18 -> x16, waiting for transfers between devices: 30.3 us -> 43.2 us  [hop(): return [lax.ppermute(part, 'narrow', pairs) for part in parts]]
    ppermute x18 -> x16, starting transfers between devices: 37.5 us -> 29.4 us  [hop(): return [lax.ppermute(part, 'narrow', pairs) for part in parts]]
    ppermute x40 -> x37, waiting for transfers between devices: 52.6 us -> 51.1 us  [swap(): lax.ppermute(values, 'wide', [(i, i ^ bit) for i in range(lax.axis_size('...]
    unnamed x88 -> x92, local copies, waits for them, and re-layouts: 6.94 us -> 8.32 us
    ppermute x40 -> x37, starting transfers between devices: 30.8 us -> 29.7 us  [swap(): lax.ppermute(values, 'wide', [(i, i ^ bit) for i in range(lax.axis_size('...]
    convert_element_type x26 -> x21, other arithmetic: 10.7 us -> 10.7 us  [add_low(): return sum((part.astype(F32) for part in parts)).astype(BF16)]
  transfers between devices with their start and end apart: 58 -> 53, of which waited for: 20 -> 20; matrix products, arithmetic and copies ran while one was open for 5% -> 5% of each run, Pallas kernels for 26% -> 26%
where the time goes in v1:
time: 259 us; the launch traced here: 258 us
  waiting for transfers between devices  94.4 us (36%)
  Pallas kernels  78.6 us (30%)
  starting transfers between devices  59.1 us (23%)
  other arithmetic  12.2 us (5%)
  local copies, waits for them, and re-layouts  11.9 us (5%)
    pallas_call x16, Pallas kernels, call(): pl.pallas_call(kernel, out_shape=shapes, grid_spec=pltpu.PrefetchScalarGr...  78.6 us
    ppermute x37, waiting for transfers between devices, swap(): lax.ppermute(values, 'wide', [(i, i ^ bit) for i in range(lax.axis_size('...  51.1 us
    ppermute x16, waiting for transfers between devices, hop(): return [lax.ppermute(part, 'narrow', pairs) for part in parts]  43.2 us
    ppermute x37, starting transfers between devices, swap(): lax.ppermute(values, 'wide', [(i, i ^ bit) for i in range(lax.axis_size('...  29.7 us
    ppermute x16, starting transfers between devices, hop(): return [lax.ppermute(part, 'narrow', pairs) for part in parts]  29.4 us
    convert_element_type x21, other arithmetic, add_low(): return sum((part.astype(F32) for part in parts)).astype(BF16)  10.7 us
    unnamed x92, local copies, waits for them, and re-layouts  8.32 us
  transfers between devices with their start and end apart: 53, of which 20 were waited for; matrix products, arithmetic and copies ran while one was open for 5% of the time, Pallas kernels for 26%

profile of v1, /device:TPU:0, one launch (start us, length us, event | category | flops | bytes accessed | tf_op | source)
XLA Modules:
  0.0 257.9 jit_solution(14958990968995371603)
XLA Ops:
  4.1 3.0 %collective-permute-start = (bf16[88,2560]{1,0:T(8,128)(2,1)S(1)}, bf16[88,2560]{1,0:T(8,128)(2,1)S(1)}, u32[]{:S(2)}, u32[]{:S(2)}) collective-permute-start(bf16[88,2560]{1,0:T(8,128)(2,1)S(1)} %shard_map.305.refs_0_), channel_id=1, source_target_pairs={{0,2},{1,3},{2,0},{3,1},{4,6},{5,7},{6,4},{7,5},{8,10},{9,11},{10,... | collective-permute-start | bytes 1351688 | tf_op jit(solution)/shard_map/ppermute | solution.py:710
  8.7 9.6 %collective-permute-done.refs_1_ = bf16[88,2560]{1,0:T(8,128)(2,1)S(1)} collective-permute-done((bf16[88,2560]{1,0:T(8,128)(2,1)S(1)}, bf16[88,2560]{1,0:T(8,128)(2,1)S(1)}, u32[]{:S(2)}, u32[]{:S(2)}) %collective-permute-start) | collective-permute-done | bytes 450592 | tf_op jit(solution)/shard_map/ppermute | solution.py:710
  20.6 8.0 %collective-permute-done.1.refs_2_ = bf16[88,2560]{1,0:T(8,128)(2,1)S(1)} collective-permute-done((bf16[88,2560]{1,0:T(8,128)(2,1)S(1)}, bf16[88,2560]{1,0:T(8,128)(2,1)S(1)}, u32[]{:S(2)}, u32[]{:S(2)}) %collective-permute-start.1) | collective-permute-done | bytes 450592 | tf_op jit(solution)/shard_map/ppermute | solution.py:710
  35.1 5.0 %shard_map.307 = (bf16[512,640]{1,0:T(8,128)(2,1)S(1)}, bf16[512,1920]{1,0:T(8,128)(2,1)S(1)}, bf16[640,1920]{1,0:T(8,128)(2,1)S(1)}, bf16[640,640]{1,0:T(8,128)...) custom-call(s32[8]{0:T(128)S(1)} %pad_add_fusion.position_ref, bf16[512,640]{1,0:T(8,128)(2,1)S(1)} %bitcast.74, ...), custom_call_target="tpu_custom_call" | custom-call | flops 1 | bytes 1 | tf_op jit(solution)/shard_map/pallas_call | solution.py:53
  41.5 7.9 %shard_map.308 = (bf16[512,640]{1,0:T(8,128)(2,1)S(1)}, f32[640,512]{1,0:T(8,128)S(1)}, f32[40,512]{1,0:T(8,128)S(1)}) custom-call(s32[512,1]{1,0:T(8,128)S(1)} %copy-done.7, s32[1,512]{1,0:T(1,128)S(1)} %copy-done.30, bf16[512,1920]{1,0:T(8,128)(2,1)S(1)} %get-tuple-element.117.q_ref.k_ref.v_ref, ...), custom_call_target="tpu_custom_call" | custom-call | flops 1 | bytes 1 | tf_op jit(solution)/shard_map/pallas_call | solution.py:53
  55.4 8.5 %collective-permute-done.11.refs_3_ = bf16[80,2560]{1,0:T(8,128)(2,1)S(1)} collective-permute-done((bf16[80,2560]{1,0:T(8,128)(2,1)}, bf16[80,2560]{1,0:T(8,128)(2,1)S(1)}, u32[]{:S(2)}, u32[]{:S(2)}) %collective-permute-start.11) | collective-permute-done | bytes 409632 | tf_op jit(solution)/shard_map/ppermute | solution.py:710
  65.6 9.0 %shard_map.310 = (bf16[1024,2560]{1,0:T(8,128)(2,1)S(1)}, bf16[1024,2560]{1,0:T(8,128)(2,1)S(1)}, bf16[640,2560]{1,0:T(8,128)(2,1)S(1)}) custom-call(s32[8]{0:T(128)S(1)} %pad_add_fusion.position_ref, bf16[512,640]{1,0:T(8,128)(2,1)S(1)} %get-tuple-element.122.own_ref.second_ref, bf16[512,640]{1,0:T(8,128)(2,1)S(1)} %collective-permute-done.7.other_ref.second_other_ref, ...), custom_call_target="tpu_custom_call" | custom-call | flops 1 | bytes 1 | tf_op jit(solution)/shard_map/pallas_call | solution.py:53
  77.1 4.3 %collective-permute-done.15.refs_1_ = bf16[320,640]{1,0:T(8,128)(2,1)S(1)} collective-permute-done((bf16[320,640]{1,0:T(8,128)(2,1)S(1)}, bf16[320,640]{1,0:T(8,128)(2,1)S(1)}, u32[]{:S(2)}, u32[]{:S(2)}) %collective-permute-start.15) | collective-permute-done | bytes 409632 | tf_op jit(solution)/shard_map/ppermute | solution.py:710
  82.1 7.2 %collective-permute-done.19.refs_5_ = bf16[320,640]{1,0:T(8,128)(2,1)S(1)} collective-permute-done((bf16[320,640]{1,0:T(8,128)(2,1)S(1)}, bf16[320,640]{1,0:T(8,128)(2,1)S(1)}, u32[]{:S(2)}, u32[]{:S(2)}) %collective-permute-start.19) | collective-permute-done | bytes 409632 | tf_op jit(solution)/shard_map/ppermute | solution.py:710
  90.1 5.1 %shard_map.311 = (f32[512,640]{1,0:T(8,128)S(1)}, bf16[512,640]{1,0:T(8,128)(2,1)S(1)}, bf16[2560,640]{1,0:T(8,128)(2,1)S(1)}) custom-call(s32[7]{0:T(128)S(1)} %compare_select_fusion.position_ref, bf16[1024,2560]{1,0:T(8,128)(2,1)S(1)} %get-tuple-element.127.act_ref, bf16[640,640]{1,0:T(8,128)(2,1)S(1)} %copy-done.2, ...), custom_call_target="tpu_custom_call" | custom-call | flops 1 | bytes 1 | tf_op jit(solution)/shard_map/pallas_call | solution.py:53
  95.2 2.1 collective-permute-done.21.got_ref
  99.6 2.0 collective-permute-done.22.other_ref
  101.6 4.3 %shard_map.313 = (bf16[2,320,640]{2,1,0:T(8,128)(2,1)S(1)}, bf16[2,320,640]{2,1,0:T(8,128)(2,1)S(1)}, bf16[2,320,640]{2,1,0:T(8,128)(2,1)S(1)}, bf16[2,320,640]{2,1,0:T(8,128)(2,1)S(1)}) custom-call(s32[1]{0:T(128)} %bitcast.13.position_ref, bf16[1024,2560]{1,0:T(8,128)(2,1)S(1)} %get-tuple-element.127.act_ref, ...), custom_call_target="tpu_custom_call" | custom-call | flops 1 | bytes 1 | tf_op jit(solution)/shard_map/pallas_call | solution.py:53
  108.3 10.9 %shard_map.314 = (bf16[1024,2560]{1,0:T(8,128)(2,1)S(1)}, f32[1,2560]{1,0:T(1,128)S(1)}, bf16[2,80,2560]{2,1,0:T(8,128)(2,1)S(1)}, bf16[2,80,2560]{2,1,0:T(8,128...) custom-call(s32[1]{0:T(128)} %bitcast.13.position_ref, ...), custom_call_target="tpu_custom_call" | custom-call | flops 1 | bytes 1 | tf_op jit(solution)/shard_map/pallas_call | solution.py:53
  119.3 4.3 %shard_map.315 = (f32[512,640]{1,0:T(8,128)S(1)}, bf16[512,640]{1,0:T(8,128)(2,1)}) custom-call(bf16[1024,2560]{1,0:T(8,128)(2,1)S(1)} %get-tuple-element.141.grad_ref, bf16[640,2560]{1,0:T(8,128)(2,1)S(1)} %get-tuple-element.142.up_ref), custom_call_target="tpu_custom_call" | custom-call | flops 1 | bytes 1 | tf_op jit(solution)/shard_map/pallas_call | solution.py:53
  124.6 1.7 collective-permute-done.24
  132.5 5.2 %shard_map.316 = (f32[512,640]{1,0:T(8,128)S(1)}, bf16[512,640]{1,0:T(8,128)(2,1)S(1)}, bf16[512,640]{1,0:T(8,128)(2,1)S(1)}, f32[8,640]{1,0:T(8,128)S(1)}) custom-call(bf16[512,640]{1,0:T(8,128)(2,1)} %collective-permute-done.23.got_ref, f32[512,640]{1,0:T(8,128)} %copy-done.13, f32[512,640]{1,0:T(8,128)} %copy-done.1, f32[512,640]{1,0:T(8,128)} %copy-done.12, ...), custom_call_target="tpu_custom_call" | custom-call | flops 1 | bytes 1 | tf_op jit(solution)/shard_map/pallas_call | solution.py:53
  137.8 13.0 %shard_map.317 = (bf16[512,640]{1,0:T(8,128)(2,1)S(1)}, bf16[512,640]{1,0:T(8,128)(2,1)S(1)}, bf16[512,640]{1,0:T(8,128)(2,1)S(1)}) custom-call(s32[512,1]{1,0:T(8,128)S(1)} %copy-done.8, s32[1,512]{1,0:T(1,128)S(1)} %copy-done.30, bf16[512,1920]{1,0:T(8,128)(2,1)S(1)} %get-tuple-element.117.q_ref.k_ref.v_ref, ...), custom_call_target="tpu_custom_call" | custom-call | flops 1 | bytes 1 | tf_op jit(solution)/shard_map/pallas_call | solution.py:53
  152.2 3.5 %collective-permute-start.29 = (bf16[320,640]{1,0:T(8,128)(2,1)S(1)}, bf16[320,640]{1,0:T(8,128)(2,1)S(1)}, u32[]{:S(2)}, u32[]{:S(2)}) collective-permute-start(bf16[320,640]{1,0:T(8,128)(2,1)S(1)} %fusion.3), channel_id=1, source_target_pairs={{0,8},{24,16},{1,9},{25,17},{2,10},{26,18},{3,11},{27,19},{4,12},{... | collective-permute-start | bytes 1228808 | tf_op jit(solution)/shard_map/ppermute | solution.py:746
  156.9 1.6 collective-permute-start.30
  158.6 8.4 %shard_map.318 = (bf16[4,88,2560]{2,1,0:T(8,128)(2,1)S(1)}, bf16[4,88,2560]{2,1,0:T(8,128)(2,1)S(1)}, f32[512,640]{1,0:T(8,128)}, f32[8,640]{1,0:T(8,128)}, bf16[640,2560]{1,0:T(8,128)(2,1)}) custom-call(s32[8]{0:T(128)S(1)} %pad_add_fusion.position_ref, bf16[512,640]{1,0:T(8,128)(2,1)S(1)} %bitcast.76, bf16[512,640]{1,0:T(8,128)(2,1)S(1)} %copy-done.24, ...), custom_call_target="tpu_custom_call" | custom-call | flops 1 | bytes 1 | tf_op jit(solution)/shard_map/pallas_call | solution.py:53
  173.2 1.6 collective-permute-start.33
  175.4 4.7 %collective-permute-done.36 = bf16[80,2560]{1,0:T(8,128)(2,1)S(1)} collective-permute-done((bf16[80,2560]{1,0:T(8,128)(2,1)S(1)}, bf16[80,2560]{1,0:T(8,128)(2,1)S(1)}, u32[]{:S(2)}, u32[]{:S(2)}) %collective-permute-start.36) | collective-permute-done | bytes 409632 | tf_op jit(solution)/shard_map/ppermute | solution.py:710
  180.9 1.6 collective-permute-done.37
  186.2 6.6 %collective-permute-done.40 = bf16[80,2560]{1,0:T(8,128)(2,1)S(1)} collective-permute-done((bf16[80,2560]{1,0:T(8,128)(2,1)S(1)}, bf16[80,2560]{1,0:T(8,128)(2,1)S(1)}, u32[]{:S(2)}, u32[]{:S(2)}) %collective-permute-start.40) | collective-permute-done | bytes 409632 | tf_op jit(solution)/shard_map/ppermute | solution.py:746
  192.8 4.4 %collective-permute-start.38 = (bf16[80,2560]{1,0:T(8,128)(2,1)S(1)}, bf16[80,2560]{1,0:T(8,128)(2,1)S(1)}, u32[]{:S(2)}, u32[]{:S(2)}) collective-permute-start(bf16[80,2560]{1,0:T(8,128)(2,1)S(1)} %fusion.1), channel_id=1, source_target_pairs={{0,8},{24,16},{1,9},{25,17},{2,10},{26,18},{3,11},{27,19},{4,12},{... | collective-permute-start | bytes 1228808 | tf_op jit(solution)/shard_map/ppermute | solution.py:746
  198.2 5.9 %collective-permute-done.38 = bf16[80,2560]{1,0:T(8,128)(2,1)S(1)} collective-permute-done((bf16[80,2560]{1,0:T(8,128)(2,1)S(1)}, bf16[80,2560]{1,0:T(8,128)(2,1)S(1)}, u32[]{:S(2)}, u32[]{:S(2)}) %collective-permute-start.38) | collective-permute-done | bytes 409632 | tf_op jit(solution)/shard_map/ppermute | solution.py:746
  206.3 7.4 %collective-permute-start.41 = (bf16[40,2560]{1,0:T(8,128)(2,1)S(1)}, bf16[40,2560]{1,0:T(8,128)(2,1)S(1)}, u32[]{:S(2)}, u32[]{:S(2)}) collective-permute-start(bf16[40,2560]{1,0:T(8,128)(2,1)S(1)} %fusion.16), channel_id=1, source_target_pairs={{0,8},{24,16},{1,9},{25,17},{2,10},{26,18},{3,11},{27,19},{4,12},{... | collective-permute-start | bytes 614408 | tf_op jit(solution)/shard_map/ppermute | solution.py:746
  221.1 14.7 %collective-permute-done.49 = bf16[80,2560]{1,0:T(8,128)(2,1)S(1)} collective-permute-done((bf16[80,2560]{1,0:T(8,128)(2,1)S(1)}, bf16[80,2560]{1,0:T(8,128)(2,1)S(1)}, u32[]{:S(2)}, u32[]{:S(2)}) %collective-permute-start.49) | collective-permute-done | bytes 409632 | tf_op jit(solution)/shard_map/ppermute | solution.py:746
  235.8 5.1 %collective-permute-done.50 = bf16[80,2560]{1,0:T(8,128)(2,1)S(1)} collective-permute-done((bf16[80,2560]{1,0:T(8,128)(2,1)S(1)}, bf16[80,2560]{1,0:T(8,128)(2,1)S(1)}, u32[]{:S(2)}, u32[]{:S(2)}) %collective-permute-start.50) | collective-permute-done | bytes 409632 | tf_op jit(solution)/shard_map/ppermute | solution.py:746
  246.3 4.7 %collective-permute-done.47.refs_2_ = bf16[40,2560]{1,0:T(8,128)(2,1)S(1)} collective-permute-done((bf16[40,2560]{1,0:T(8,128)(2,1)S(1)}, bf16[40,2560]{1,0:T(8,128)(2,1)S(1)}, u32[]{:S(2)}, u32[]{:S(2)}) %collective-permute-start.47) | collective-permute-done | bytes 204832 | tf_op jit(solution)/shard_map/ppermute | solution.py:746
  251.0 4.8 %collective-permute-done.48.refs_3_ = bf16[48,2560]{1,0:T(8,128)(2,1)S(1)} collective-permute-done((bf16[48,2560]{1,0:T(8,128)(2,1)S(1)}, bf16[48,2560]{1,0:T(8,128)(2,1)S(1)}, u32[]{:S(2)}, u32[]{:S(2)}) %collective-permute-start.48) | collective-permute-done | bytes 245792 | tf_op jit(solution)/shard_map/ppermute | solution.py:746
  (215 shorter events, 70.1 us)
Async XLA Ops:
  4.1 14.2 %collective-permute-start = (bf16[88,2560]{1,0:T(8,128)(2,1)S(1)}, bf16[88,2560]{1,0:T(8,128)(2,1)S(1)}, u32[]{:S(2)}, u32[]{:S(2)}) collective-permute-start(bf16[88,2560]{1,0:T(8,128)(2,1)S(1)} %shard_map.305.refs_0_), channel_id=1, source_target_pairs={{0,2},{1,3},{2,0},{3,1},{4,6},{5,7},{6,4},{7,5},{8,10},{9,11},{10,... | collective-permute-start | bytes 1351688 | tf_op jit(solution)/shard_map/ppermute | solution.py:710
  7.2 21.5 %collective-permute-start.1 = (bf16[88,2560]{1,0:T(8,128)(2,1)S(1)}, bf16[88,2560]{1,0:T(8,128)(2,1)S(1)}, u32[]{:S(2)}, u32[]{:S(2)}) collective-permute-start(bf16[88,2560]{1,0:T(8,128)(2,1)S(1)} %shard_map.305.refs_0_), channel_id=1, source_target_pairs={{0,4},{1,5},{2,6},{3,7},{4,0},{5,1},{6,2},{7,3},{8,12},{9,13},{10,... | collective-permute-start | bytes 1351688 | tf_op jit(solution)/shard_map/ppermute | solution.py:710
  8.7 19.9 %collective-permute-start.2 = (bf16[88,2560]{1,0:T(8,128)(2,1)S(1)}, bf16[88,2560]{1,0:T(8,128)(2,1)S(1)}, u32[]{:S(2)}, u32[]{:S(2)}) collective-permute-start(bf16[88,2560]{1,0:T(8,128)(2,1)S(1)} %shard_map.305.refs_0_), channel_id=1, source_target_pairs={{0,6},{1,7},{2,4},{3,5},{4,2},{5,3},{6,0},{7,1},{8,14},{9,15},{10,... | collective-permute-start | bytes 1351688 | tf_op jit(solution)/shard_map/ppermute | solution.py:710
  8.7 19.9 %collective-permute-start.3 = (bf16[88,2560]{1,0:T(8,128)(2,1)S(1)}, bf16[88,2560]{1,0:T(8,128)(2,1)S(1)}, u32[]{:S(2)}, u32[]{:S(2)}) collective-permute-start(bf16[88,2560]{1,0:T(8,128)(2,1)S(1)} %shard_map.305.refs_0_), channel_id=1, source_target_pairs={{0,1},{1,0},{2,3},{3,2},{4,5},{5,4},{6,7},{7,6},{8,9},{9,8},{10,11... | collective-permute-start | bytes 1351688 | tf_op jit(solution)/shard_map/ppermute | solution.py:710
  29.2 21.3 %collective-permute-start.9 = (bf16[80,2560]{1,0:T(8,128)(2,1)}, bf16[80,2560]{1,0:T(8,128)(2,1)}, u32[]{:S(2)}, u32[]{:S(2)}) collective-permute-start(bf16[80,2560]{1,0:T(8,128)(2,1)} %get-tuple-element.114.refs_0_), channel_id=1, source_target_pairs={{0,4},{1,5},{2,6},{3,7},{4,0},{5,1},{6,2},{7,3},{8,12},{9,13},{10,... | collective-permute-start | bytes 1228808 | tf_op jit(solution)/shard_map/ppermute | solution.py:710
  30.8 20.5 %collective-permute-start.10 = (bf16[80,2560]{1,0:T(8,128)(2,1)}, bf16[80,2560]{1,0:T(8,128)(2,1)}, u32[]{:S(2)}, u32[]{:S(2)}) collective-permute-start(bf16[80,2560]{1,0:T(8,128)(2,1)} %get-tuple-element.124), channel_id=1, source_target_pairs={{0,3},{1,2},{2,1},{3,0},{4,7},{5,6},{6,5},{7,4},{8,11},{9,10},{10,... | collective-permute-start | bytes 1228808 | tf_op jit(solution)/shard_map/ppermute | solution.py:710
  30.8 21.2 %collective-permute-start.8 = (bf16[80,2560]{1,0:T(8,128)(2,1)}, bf16[80,2560]{1,0:T(8,128)(2,1)}, u32[]{:S(2)}, u32[]{:S(2)}) collective-permute-start(bf16[80,2560]{1,0:T(8,128)(2,1)} %get-tuple-element.114.refs_0_), channel_id=1, source_target_pairs={{0,2},{1,3},{2,0},{3,1},{4,6},{5,7},{6,4},{7,5},{8,10},{9,11},{10,... | collective-permute-start | bytes 1228808 | tf_op jit(solution)/shard_map/ppermute | solution.py:710
  32.2 20.9 %collective-permute-start.13 = (bf16[80,2560]{1,0:T(8,128)(2,1)}, bf16[80,2560]{1,0:T(8,128)(2,1)}, u32[]{:S(2)}, u32[]{:S(2)}) collective-permute-start(bf16[80,2560]{1,0:T(8,128)(2,1)} %get-tuple-element.124), channel_id=1, source_target_pairs={{0,5},{1,4},{2,7},{3,6},{4,1},{5,0},{6,3},{7,2},{8,13},{9,12},{10,... | collective-permute-start | bytes 1228808 | tf_op jit(solution)/shard_map/ppermute | solution.py:710
  33.7 20.6 %collective-permute-start.12 = (bf16[80,2560]{1,0:T(8,128)(2,1)}, bf16[80,2560]{1,0:T(8,128)(2,1)}, u32[]{:S(2)}, u32[]{:S(2)}) collective-permute-start(bf16[80,2560]{1,0:T(8,128)(2,1)} %get-tuple-element.124), channel_id=1, source_target_pairs={{0,1},{1,0},{2,3},{3,2},{4,5},{5,4},{6,7},{7,6},{8,9},{9,8},{10,11... | collective-permute-start | bytes 1228808 | tf_op jit(solution)/shard_map/ppermute | solution.py:710
  50.6 15.1 %collective-permute-start.7 = (bf16[512,640]{1,0:T(8,128)(2,1)S(1)}, bf16[512,640]{1,0:T(8,128)(2,1)S(1)}, u32[]{:S(2)}, u32[]{:S(2)}) collective-permute-start(bf16[512,640]{1,0:T(8,128)(2,1)S(1)} %get-tuple-element.122.own_ref.second_ref), channel_id=1, source_target_pairs={{0,1},{1,0},{2,3},{3,2},{4,5},{5,4},{6,7},{7,6},{8,9},{9,8},{10,11... | collective-permute-start | bytes 1966088 | tf_op jit(solution)/shard_map/ppermute | solution.py:710
  53.1 21.6 %collective-permute-start.16 = (bf16[320,640]{1,0:T(8,128)(2,1)S(1)}, bf16[320,640]{1,0:T(8,128)(2,1)S(1)}, u32[]{:S(2)}, u32[]{:S(2)}) collective-permute-start(bf16[320,640]{1,0:T(8,128)(2,1)S(1)} %get-tuple-element.129), channel_id=1, source_target_pairs={{0,2},{1,3},{2,0},{3,1},{4,6},{5,7},{6,4},{7,5},{8,10},{9,11},{10,... | collective-permute-start | bytes 1228808 | tf_op jit(solution)/shard_map/ppermute | solution.py:710
  54.3 20.3 %collective-permute-start.17 = (bf16[320,640]{1,0:T(8,128)(2,1)S(1)}, bf16[320,640]{1,0:T(8,128)(2,1)S(1)}, u32[]{:S(2)}, u32[]{:S(2)}) collective-permute-start(bf16[320,640]{1,0:T(8,128)(2,1)S(1)} %get-tuple-element.128), channel_id=1, source_target_pairs={{0,4},{1,5},{2,6},{3,7},{4,0},{5,1},{6,2},{7,3},{8,12},{9,13},{10,... | collective-permute-start | bytes 1228808 | tf_op jit(solution)/shard_map/ppermute | solution.py:710
  63.9 17.6 %collective-permute-start.15 = (bf16[320,640]{1,0:T(8,128)(2,1)S(1)}, bf16[320,640]{1,0:T(8,128)(2,1)S(1)}, u32[]{:S(2)}, u32[]{:S(2)}) collective-permute-start(bf16[320,640]{1,0:T(8,128)(2,1)S(1)} %get-tuple-element.128), channel_id=1, source_target_pairs={{0,2},{1,3},{2,0},{3,1},{4,6},{5,7},{6,4},{7,5},{8,10},{9,11},{10,... | collective-permute-start | bytes 1228808 | tf_op jit(solution)/shard_map/ppermute | solution.py:710
  64.6 17.6 %collective-permute-start.18 = (bf16[320,640]{1,0:T(8,128)(2,1)S(1)}, bf16[320,640]{1,0:T(8,128)(2,1)S(1)}, u32[]{:S(2)}, u32[]{:S(2)}) collective-permute-start(bf16[320,640]{1,0:T(8,128)(2,1)S(1)} %get-tuple-element.129), channel_id=1, source_target_pairs={{0,4},{1,5},{2,6},{3,7},{4,0},{5,1},{6,2},{7,3},{8,12},{9,13},{10,... | collective-permute-start | bytes 1228808 | tf_op jit(solution)/shard_map/ppermute | solution.py:710
  74.7 14.7 %collective-permute-start.19 = (bf16[320,640]{1,0:T(8,128)(2,1)S(1)}, bf16[320,640]{1,0:T(8,128)(2,1)S(1)}, u32[]{:S(2)}, u32[]{:S(2)}) collective-permute-start(bf16[320,640]{1,0:T(8,128)(2,1)S(1)} %collective-permute-done.17.refs_3_), channel_id=1, source_target_pairs={{0,2},{1,3},{2,0},{3,1},{4,6},{5,7},{6,4},{7,5},{8,10},{9,11},{10,... | collective-permute-start | bytes 1228808 | tf_op jit(solution)/shard_map/ppermute | solution.py:710
  76.0 14.1 %collective-permute-start.20 = (bf16[320,640]{1,0:T(8,128)(2,1)S(1)}, bf16[320,640]{1,0:T(8,128)(2,1)S(1)}, u32[]{:S(2)}, u32[]{:S(2)}) collective-permute-start(bf16[320,640]{1,0:T(8,128)(2,1)S(1)} %collective-permute-done.16.refs_2_), channel_id=1, source_target_pairs={{0,4},{1,5},{2,6},{3,7},{4,0},{5,1},{6,2},{7,3},{8,12},{9,13},{10,... | collective-permute-start | bytes 1228808 | tf_op jit(solution)/shard_map/ppermute | solution.py:710
  105.9 20.3 %collective-permute-start.24 = (bf16[2,320,640]{2,1,0:T(8,128)(2,1)S(1)}, bf16[2,320,640]{2,1,0:T(8,128)(2,1)S(1)}, u32[]{:S(2)}, u32[]{:S(2)}) collective-permute-start(bf16[2,320,640]{2,1,0:T(8,128)(2,1)S(1)} %get-tuple-element.137), channel_id=1, source_target_pairs={{0,2},{1,3},{2,0},{3,1},{4,6},{5,7},{6,4},{7,5},{8,10},{9,11},{10,... | collective-permute-start | bytes 2457608 | tf_op jit(solution)/shard_map/ppermute | solution.py:710
  107.0 21.2 %collective-permute-start.25 = (bf16[2,320,640]{2,1,0:T(8,128)(2,1)S(1)}, bf16[2,320,640]{2,1,0:T(8,128)(2,1)S(1)}, u32[]{:S(2)}, u32[]{:S(2)}) collective-permute-start(bf16[2,320,640]{2,1,0:T(8,128)(2,1)S(1)} %get-tuple-element.146), channel_id=1, source_target_pairs={{0,4},{1,5},{2,6},{3,7},{4,0},{5,1},{6,2},{7,3},{8,12},{9,13},{10,... | collective-permute-start | bytes 2457608 | tf_op jit(solution)/shard_map/ppermute | solution.py:710
  127.4 23.5 %collective-permute-start.26 = (bf16[320,640]{1,0:T(8,128)(2,1)}, bf16[320,640]{1,0:T(8,128)(2,1)}, u32[]{:S(2)}, u32[]{:S(2)}) collective-permute-start(bf16[320,640]{1,0:T(8,128)(2,1)} %fusion.10), channel_id=1, source_target_pairs={{0,4},{1,5},{2,6},{3,7},{4,0},{5,1},{6,2},{7,3},{8,12},{9,13},{10,... | collective-permute-start | bytes 1228808 | tf_op jit(solution)/shard_map/ppermute | solution.py:710
  129.2 21.6 %collective-permute-start.27 = (bf16[320,640]{1,0:T(8,128)(2,1)}, bf16[320,640]{1,0:T(8,128)(2,1)}, u32[]{:S(2)}, u32[]{:S(2)}) collective-permute-start(bf16[320,640]{1,0:T(8,128)(2,1)} %fusion.11), channel_id=1, source_target_pairs={{0,2},{1,3},{2,0},{3,1},{4,6},{5,7},{6,4},{7,5},{8,10},{9,11},{10,... | collective-permute-start | bytes 1228808 | tf_op jit(solution)/shard_map/ppermute | solution.py:710
  130.7 36.3 %collective-permute-start.31 = (bf16[2,80,2560]{2,1,0:T(8,128)(2,1)}, bf16[2,80,2560]{2,1,0:T(8,128)(2,1)}, u32[]{:S(2)}, u32[]{:S(2)}) collective-permute-start(bf16[2,80,2560]{2,1,0:T(8,128)(2,1)} %get-tuple-element.173), channel_id=1, source_target_pairs={{0,2},{1,3},{2,0},{3,1},{4,6},{5,7},{6,4},{7,5},{8,10},{9,11},{10,... | collective-permute-start | bytes 2457608 | tf_op jit(solution)/shard_map/ppermute | solution.py:710
  131.3 35.8 %collective-permute-start.32 = (bf16[2,80,2560]{2,1,0:T(8,128)(2,1)}, bf16[2,80,2560]{2,1,0:T(8,128)(2,1)}, u32[]{:S(2)}, u32[]{:S(2)}) collective-permute-start(bf16[2,80,2560]{2,1,0:T(8,128)(2,1)} %get-tuple-element.174), channel_id=1, source_target_pairs={{0,4},{1,5},{2,6},{3,7},{4,0},{5,1},{6,2},{7,3},{8,12},{9,13},{10,... | collective-permute-start | bytes 2457608 | tf_op jit(solution)/shard_map/ppermute | solution.py:710
  152.2 19.5 %collective-permute-start.29 = (bf16[320,640]{1,0:T(8,128)(2,1)S(1)}, bf16[320,640]{1,0:T(8,128)(2,1)S(1)}, u32[]{:S(2)}, u32[]{:S(2)}) collective-permute-start(bf16[320,640]{1,0:T(8,128)(2,1)S(1)} %fusion.3), channel_id=1, source_target_pairs={{0,8},{24,16},{1,9},{25,17},{2,10},{26,18},{3,11},{27,19},{4,12},{... | collective-permute-start | bytes 1228808 | tf_op jit(solution)/shard_map/ppermute | solution.py:746
  156.9 14.8 %collective-permute-start.30 = (bf16[320,640]{1,0:T(8,128)(2,1)S(1)}, bf16[320,640]{1,0:T(8,128)(2,1)S(1)}, u32[]{:S(2)}, u32[]{:S(2)}) collective-permute-start(bf16[320,640]{1,0:T(8,128)(2,1)S(1)} %fusion.2), channel_id=1, source_target_pairs={{0,8},{24,16},{1,9},{25,17},{2,10},{26,18},{3,11},{27,19},{4,12},{... | collective-permute-start | bytes 1228808 | tf_op jit(solution)/shard_map/ppermute | solution.py:746
  172.0 25.3 %collective-permute-start.39 = (bf16[640,640]{1,0:T(8,128)(2,1)S(1)}, bf16[640,640]{1,0:T(8,128)(2,1)S(1)}, u32[]{:S(2)}, u32[]{:S(2)}) collective-permute-start(bf16[640,640]{1,0:T(8,128)(2,1)S(1)} %pad_maximum_fusion), channel_id=1, source_target_pairs={{8,16},{16,8},{9,17},{17,9},{10,18},{18,10},{11,19},{19,11},{12,20... | collective-permute-start | bytes 2457608 | tf_op jit(solution)/shard_map/ppermute | solution.py:746
  173.2 32.3 %collective-permute-start.33 = (bf16[88,2560]{1,0:T(8,128)(2,1)S(1)}, bf16[88,2560]{1,0:T(8,128)(2,1)S(1)}, u32[]{:S(2)}, u32[]{:S(2)}) collective-permute-start(bf16[88,2560]{1,0:T(8,128)(2,1)S(1)} %get-tuple-element.209), channel_id=1, source_target_pairs={{0,6},{1,7},{2,4},{3,5},{4,2},{5,3},{6,0},{7,1},{8,14},{9,15},{10,... | collective-permute-start | bytes 1351688 | tf_op jit(solution)/shard_map/ppermute | solution.py:710
  174.8 31.4 %collective-permute-start.34 = (bf16[88,2560]{1,0:T(8,128)(2,1)S(1)}, bf16[88,2560]{1,0:T(8,128)(2,1)S(1)}, u32[]{:S(2)}, u32[]{:S(2)}) collective-permute-start(bf16[88,2560]{1,0:T(8,128)(2,1)S(1)} %get-tuple-element.208), channel_id=1, source_target_pairs={{0,2},{1,3},{2,0},{3,1},{4,6},{5,7},{6,4},{7,5},{8,10},{9,11},{10,... | collective-permute-start | bytes 1351688 | tf_op jit(solution)/shard_map/ppermute | solution.py:710
  180.1 26.1 %collective-permute-start.35 = (bf16[88,2560]{1,0:T(8,128)(2,1)S(1)}, bf16[88,2560]{1,0:T(8,128)(2,1)S(1)}, u32[]{:S(2)}, u32[]{:S(2)}) collective-permute-start(bf16[88,2560]{1,0:T(8,128)(2,1)S(1)} %get-tuple-element.207), channel_id=1, source_target_pairs={{0,4},{1,5},{2,6},{3,7},{4,0},{5,1},{6,2},{7,3},{8,12},{9,13},{10,... | collective-permute-start | bytes 1351688 | tf_op jit(solution)/shard_map/ppermute | solution.py:710
  197.3 17.9 %collective-permute-start.42 = (bf16[80,2560]{1,0:T(8,128)(2,1)S(1)}, bf16[80,2560]{1,0:T(8,128)(2,1)S(1)}, u32[]{:S(2)}, u32[]{:S(2)}) collective-permute-start(bf16[80,2560]{1,0:T(8,128)(2,1)S(1)} %add_convert_fusion.8), channel_id=1, source_target_pairs={{8,16},{16,8},{9,17},{17,9},{10,18},{18,10},{11,19},{19,11},{12,20... | collective-permute-start | bytes 1228808 | tf_op jit(solution)/shard_map/ppermute | solution.py:746
  204.1 39.7 %collective-permute-start.52 = (bf16[640,640]{1,0:T(8,128)(2,1)S(1)}, bf16[640,640]{1,0:T(8,128)(2,1)S(1)}, u32[]{:S(2)}, u32[]{:S(2)}) collective-permute-start(bf16[640,640]{1,0:T(8,128)(2,1)S(1)} %add_convert_fusion), channel_id=1, source_target_pairs={{8,0},{16,24},{9,1},{17,25},{10,2},{18,26},{11,3},{19,27},{12,4},{... | collective-permute-start | bytes 2457608 | tf_op jit(solution)/shard_map/ppermute | solution.py:746
  215.3 20.5 %collective-permute-start.49 = (bf16[80,2560]{1,0:T(8,128)(2,1)S(1)}, bf16[80,2560]{1,0:T(8,128)(2,1)S(1)}, u32[]{:S(2)}, u32[]{:S(2)}) collective-permute-start(bf16[80,2560]{1,0:T(8,128)(2,1)S(1)} %add_convert_fusion.6), channel_id=1, source_target_pairs={{8,0},{16,24},{9,1},{17,25},{10,2},{18,26},{11,3},{19,27},{12,4},{... | collective-permute-start | bytes 1228808 | tf_op jit(solution)/shard_map/ppermute | solution.py:746
  218.4 22.5 %collective-permute-start.50 = (bf16[80,2560]{1,0:T(8,128)(2,1)S(1)}, bf16[80,2560]{1,0:T(8,128)(2,1)S(1)}, u32[]{:S(2)}, u32[]{:S(2)}) collective-permute-start(bf16[80,2560]{1,0:T(8,128)(2,1)S(1)} %add_convert_fusion.5), channel_id=1, source_target_pairs={{8,0},{16,24},{9,1},{17,25},{10,2},{18,26},{11,3},{19,27},{12,4},{... | collective-permute-start | bytes 1228808 | tf_op jit(solution)/shard_map/ppermute | solution.py:746
  (67 other events, 650.7 us)

commit v2 on v1

--- a/solution.py
+++ b/solution.py
@@ -48,7 +48,10 @@
         for arg, spec in zip(args, in_specs)
     ]
     out_specs = out_specs or [whole] * len(outs)
-    shapes = [jax.ShapeDtypeStruct(shape, dtype) for shape, dtype in outs]
+    shapes = [
+        pltpu.HBM(*out) if spec.memory_space == pltpu.HBM else jax.ShapeDtypeStruct(*out)
+        for out, spec in zip(outs, out_specs)
+    ]
     extra = [] if positions is None else [positions]
     return pl.pallas_call(
         kernel,
@@ -94,10 +97,10 @@
     return [first, second, rest - second]
 
 
-def key_marks(segment_column):
-    lane = lax.broadcasted_iota(jnp.int32, (segment_column.shape[0], LANES), 1)
-    ones = (lane >= SEGMENTS) & (lane < SEGMENTS + 3)
-    return jnp.where((lane == segment_column) | ones, 1.0, 0.0).astype(BF16)
+def key_marks(segment_row):
+    at = lax.broadcasted_iota(jnp.int32, (LANES, segment_row.shape[1]), 0)
+    ones = (at >= SEGMENTS) & (at < SEGMENTS + 3)
+    return jnp.where((at == segment_row) | ones, 1.0, 0.0).astype(BF16).T
 
 
 def query_marks(segment_row):
@@ -115,10 +118,10 @@
     return jnp.concatenate(parts, axis=0)
 
 
-def attend_kernel(column_ref, row_ref, q_ref, k_ref, v_ref, out_ref, across_ref, lse_ref, marks_ref):
+def attend_kernel(row_ref, q_ref, k_ref, v_ref, out_ref, across_ref, lse_ref, marks_ref):
     @pl.when(pl.program_id(0) == 0)
     def _():
-        marks_ref[...] = key_marks(column_ref[...])
+        marks_ref[...] = key_marks(row_ref[...])
 
     length = q_ref.shape[0]
     heads = LANES // HEAD_DIM
@@ -163,12 +166,12 @@
 
 
 def attend_back_kernel(
-    column_ref, row_ref, q_ref, k_ref, v_ref, grad_ref, across_ref, lse_ref,
+    row_ref, q_ref, k_ref, v_ref, grad_ref, across_ref, lse_ref,
     gq_ref, gk_ref, gv_ref, marks_ref, turned_ref,
 ):
     @pl.when(pl.program_id(0) == 0)
     def _():
-        marks_ref[...] = key_marks(column_ref[...])
+        marks_ref[...] = key_marks(row_ref[...])
 
     length = q_ref.shape[0]
     grad = grad_ref[...]
@@ -255,40 +258,39 @@
     return (
         tiles,
         tile,
-        pl.BlockSpec((length, 1), lambda i: (0, 0)),
         pl.BlockSpec((1, length), lambda i: (0, 0)),
         pl.BlockSpec((LANES, length), lambda i: (begin + i, 0)),
         pl.BlockSpec((SUBLANES, length), lambda i: (begin + i, 0)),
     )
 
 
-def attend(joined, column, row):
+def attend(joined, row):
     length = joined.shape[0]
     width = joined.shape[1] // 3
-    tiles, tile, column_spec, row_spec, across_spec, lse_spec = attention_specs(length, width)
+    tiles, tile, row_spec, across_spec, lse_spec = attention_specs(length, width)
     return call(
         attend_kernel,
         [((length, width), BF16), ((width, length), F32), ((SUBLANES * tiles, length), F32)],
-        (column, row, joined, joined, joined),
+        (row, joined, joined, joined),
         grid=(tiles,),
-        in_specs=[column_spec, row_spec, tile(0), tile(tiles), tile(2 * tiles)],
+        in_specs=[row_spec, tile(0), tile(tiles), tile(2 * tiles)],
         out_specs=[tile(0), across_spec, lse_spec],
         scratch=[pltpu.VMEM((length, LANES), BF16)],
     )
 
 
-def attend_back(joined, column, row, grad, across, lse, begin=0, end=None):
+def attend_back(joined, row, grad, across, lse, begin=0, end=None):
     length = joined.shape[0]
     width = joined.shape[1] // 3
     specs = attention_specs(length, width, begin)
-    tiles, tile, column_spec, row_spec, across_spec, lse_spec = specs
+    tiles, tile, row_spec, across_spec, lse_spec = specs
     count = (end or tiles) - begin
     return call(
         attend_back_kernel,
         [((length, count * LANES), BF16)] * 3,
-        (column, row, joined, joined, joined, grad, across, lse),
+        (row, joined, joined, joined, grad, across, lse),
         grid=(count,),
-        in_specs=[column_spec, row_spec, tile(0), tile(tiles), tile(2 * tiles), tile(0), across_spec, lse_spec],
+        in_specs=[row_spec, tile(0), tile(tiles), tile(2 * tiles), tile(0), across_spec, lse_spec],
         out_specs=[tile(0, 0)] * 3,
         scratch=[pltpu.VMEM((length, LANES), BF16), pltpu.VMEM((LANES, length), F32)],
         mib=24,
@@ -485,9 +487,8 @@
     lanes = jnp.concatenate([loss_lanes, count_lanes], axis=0)
     lanes = jnp.concatenate([lanes, jnp.zeros((2, result.shape[1] - LANES), F32)], axis=1)
     grad_logits = (weight * (shifted / total - onehot.astype(F32))).astype(BF16)
-    grad = tn(grad_logits, readout_ref[...])
-    grad_ref[...] = grad
-    low = grad.astype(BF16)
+    grad_ref[...] = grad_logits
+    low = tn(grad_logits, readout_ref[...]).astype(BF16)
     down_ref[...] = low
     sums = jnp.sum(low.astype(F32), axis=0, keepdims=True)
     blank = jnp.zeros((SUBLANES - 3, result.shape[1]), F32)
@@ -584,10 +585,13 @@
     )
 
 
-def inward_kernel(grad_ref, up_ref, own_ref, other_ref):
-    length = own_ref.shape[0]
+def inward_kernel(grad_ref, up_ref, own_far, other_ref, own_ref, sem):
+    length = other_ref.shape[0]
+    own_ref[...] = nt(grad_ref[:length, :], up_ref[...])
+    copy = pltpu.make_async_copy(own_ref, own_far, sem)
+    copy.start()
     other_ref[...] = nt(grad_ref[length:, :], up_ref[...]).astype(BF16)
-    own_ref[...] = nt(grad_ref[:length, :], up_ref[...])
+    copy.wait()
 
 
 def join_kernel(hidden, position_ref, mine_ref, other_ref, out_ref):
@@ -599,8 +603,8 @@
 
 
 def branch_kernel(
-    got_ref, own_far, middle_far, result_far, out_ref, vector_ref,
-    grad_ref, branch_ref, attended_ref, sums_ref, own_ref, middle_ref, result_ref, sems,
+    got_ref, own_far, middle_far, logits_ref, classes_ref, out_ref, vector_ref,
+    grad_ref, branch_ref, attended_ref, sums_ref, own_ref, middle_ref, sems,
 ):
     width = own_ref.shape[1]
     blocks = range(0, own_ref.shape[0], ROWS)
@@ -610,9 +614,7 @@
         copies.append(
             [
                 pltpu.make_async_copy(far.at[here], ref.at[here], sems.at[at // ROWS, which])
-                for which, (far, ref) in enumerate(
-                    ((own_far, own_ref), (middle_far, middle_ref), (result_far, result_ref))
-                )
+                for which, (far, ref) in enumerate(((own_far, own_ref), (middle_far, middle_ref)))
             ]
         )
         for copy in copies[-1]:
@@ -625,7 +627,8 @@
         here = slice(at, at + ROWS)
         grad = own_ref[here, :] + got_ref[here, :].astype(F32)
         normal, inverse = unit(middle_ref[here, :])
-        middle = result_ref[here, :] + unit_back(grad, normal, inverse, gain)
+        result = tn(logits_ref[:, here], classes_ref[...])
+        middle = result + unit_back(grad, normal, inverse, gain)
         grad_ref[here, :] = middle
         branch = middle.astype(BF16)
         branch_ref[here, :] = branch
@@ -673,10 +676,15 @@
     blank = jnp.zeros((VECTORS - 1, hidden), F32)
     lanes = jnp.concatenate([loss_ref[:2, :LANES], jnp.zeros((VECTORS - 2, LANES), F32)], axis=0)
     for at in range(count):
-        slab = stacks[at // (count // 2)].at[at % (count // 2)]
+        stack = stacks[at // (count // 2)]
         place_at = position_ref[at]
         begin = pl.multiple_of(place_at * rows, SUBLANES)
-        slab[:rows, :] = full_ref[pl.ds(begin, rows), :]
+        cuts = [
+            (pick, slice(2 * width * side, 2 * width * (side + 1)))
+            for side, pick in enumerate(((0, 2, 1, 3)[at % 4], 4 + at % 4))
+        ]
+        for pick, here in cuts:
+            stack[pick, :rows, :] = full_ref[pl.ds(begin, rows), here]
         short = pltpu.roll(vectors, width - begin, 1)[:, :LANES]
         if at < count // 2:
             hidden_at = pl.multiple_of(lax.div(place_at, 2) * hidden, LANES)
@@ -685,23 +693,24 @@
             bias = jnp.zeros((VECTORS, hidden), F32)
         row = jnp.concatenate([short, bias, lanes], axis=1).astype(BF16)
         pad = jnp.zeros((VECTORS, 4 * width - row.shape[1]), BF16)
-        slab[rows:, :] = jnp.concatenate([row, pad], axis=1)
-
-
-def settle_kernel(cut, rows, hidden, place_ref, *refs):
+        row = jnp.concatenate([row, pad], axis=1)
+        for pick, here in cuts:
+            stack[pick, rows:, :] = row[:, here]
+
+
+def settle_kernel(rows, hidden, place_ref, *refs):
     totals, outers, refs = refs[:2], refs[2:4], refs[4:]
     heads_ref, out_ref, short_ref, loss_ref, count_ref = refs
     width = out_ref.shape[1]
     inner = (place_ref[0] == 1) | (place_ref[0] == 2)
-    chosen = [
+    left, right = [
         jnp.where(inner, total[...], outer[...]).astype(F32) for total, outer in zip(totals, outers)
     ]
-    for begin, end, values in ((0, cut, chosen[0]), (cut, rows, chosen[1])):
-        heads_ref[begin:end, :] = values[: end - begin, : 3 * width]
-        out_ref[begin:end, :] = values[: end - begin, 3 * width :]
-    short = chosen[1][rows - cut :]
-    short_ref[...] = short
-    lanes = short[:, LANES + hidden : 2 * LANES + hidden]
+    heads_ref[:, : 2 * width] = left[:rows]
+    heads_ref[:, 2 * width :] = right[:rows, :width]
+    out_ref[...] = right[:rows, width:]
+    short_ref[...] = left[rows:]
+    lanes = left[rows:, LANES + hidden : 2 * LANES + hidden]
     loss_ref[0] = jnp.sum(lanes[0:1])
     count_ref[0] = jnp.sum(lanes[1:2]).astype(jnp.int32)
 
@@ -778,9 +787,9 @@
     hidden = up_bias.shape[0]
     half = chips * hidden
     x = layer_input[0]
+    classes = readout.T
     vmem = pl.BlockSpec(memory_space=pltpu.VMEM)
     far_away = pl.BlockSpec(memory_space=pltpu.HBM)
-    column = segments.reshape(length, 1)
 
     def by_core(mine, other, axis):
         return jnp.where(
@@ -809,7 +818,7 @@
         devices = 2 * (chip ^ offsets) + core
         positions = jnp.concatenate([devices, devices ^ 1]).astype(jnp.int32)
         up_positions = positions
-        up_weight, column, positions = after([up_weight, column, positions], near_x)
+        up_weight, positions = after([up_weight, positions], near_x)
         up_mine, up_other = call(
             functools.partial(halves_kernel, hidden),
             [((rows, half), BF16)] * 2,
@@ -869,7 +878,7 @@
         down_parts = [spread_chips(down_weight).reshape(half, width)]
         up_positions = down_positions = positions
 
-    attended, across, lse = attend(joined, column, segments)
+    attended, across, lse = attend(joined, segments)
     if square():
         passed_y, passed_x = after([mine_y, other_x], attended)
         up_parts = [
@@ -901,13 +910,13 @@
         passed_x, passed_y = after([upper_y, lower_x], activated)
         down_parts = down_parts + [swap(passed_x, 2), swap(passed_y, 4)]
     outward, outward_other, down_full = down_project(activated, down_parts, down_positions)
-    result_low, grad_down, grad_result, loss_sums = call(
+    result_low, grad_down, grad_logits, loss_sums = call(
         loss_kernel,
         [
-            ((length, width), BF16), ((length, width), BF16), ((length, width), F32),
+            ((length, width), BF16), ((length, width), BF16), (classes.shape[:1] + (length,), BF16),
             ((SUBLANES, width), F32),
         ],
-        (middle, outward, swap(outward_other, 1), vectors, readout.T, targets, loss_mask),
+        (middle, outward, swap(outward_other, 1), vectors, classes, targets, loss_mask),
     )
 
     grad_down_other = swap(grad_down, 1)
@@ -923,6 +932,8 @@
         inward_kernel,
         [((length, width), F32), ((length, width), BF16)],
         (grad_up, up_full),
+        out_specs=[far_away, vmem],
+        scratch=[pltpu.VMEM((length, width), F32), pltpu.SemaphoreType.DMA],
         mib=20,
     )
     got_inward = swap(inward_other, 1)
@@ -941,17 +952,17 @@
             ((length, width), F32), ((length, width), BF16), ((length, width), BF16),
             ((SUBLANES, width), F32),
         ],
-        (got_inward, inward, middle, grad_result, output_full, vectors),
-        in_specs=[vmem, far_away, far_away, far_away, vmem, vmem],
+        (got_inward, inward, middle, grad_logits, classes, output_full, vectors),
+        in_specs=[vmem, far_away, far_away, vmem, vmem, vmem, vmem],
         scratch=[
-            *[pltpu.VMEM((length, width), F32)] * 3,
-            pltpu.SemaphoreType.DMA((length // ROWS, 3)),
+            *[pltpu.VMEM((length, width), F32)] * 2,
+            pltpu.SemaphoreType.DMA((length // ROWS, 2)),
         ],
         mib=24,
     )
 
     if square():
-        attend_grads = attend_back(joined, column, segments, grad_attended, across, lse)
+        attend_grads = attend_back(joined, segments, grad_attended, across, lse)
         down_got = after(down_got, attend_grads[0])
         down_narrow = [
             add_low(keep_dx[0], down_first[0][0], down_got[0]),
@@ -960,8 +971,8 @@
         down_in = hop(down_narrow, INWARD)
         attend_grads = after(attend_grads, down_narrow)
     else:
-        attend_grads = attend_back(joined, column, segments, grad_attended, across, lse)
-    stack_shape = ((4, rows + VECTORS, 4 * width), BF16)
+        attend_grads = attend_back(joined, segments, grad_attended, across, lse)
+    stack_shape = ((8, rows + VECTORS, 2 * width), BF16)
     *stacks, input_grad, short_sums, attend_part = call(
         functools.partial(last_kernel, 8 if square() else 0, rows, hidden, len(attend_grads) // 3),
         ([stack_shape] * 2 if square() else [])
@@ -985,8 +996,8 @@
         (down_mid,) = hop([down_half], ACROSS)
 
         (mine_got,) = after([mine_got], down_half)
-        both = [add_low(mine[at], mine_got[at]) for at in range(4)]
-        slab_far = [swap(both[3], 6), swap(both[1], 2), swap(both[2], 4)]
+        both = add_low(mine, mine_got)
+        side_first = [swap(both[2:4], 2), swap(both[6:8], 4)]
 
         up_got = after(up_got, both)
         up_narrow = [
@@ -995,27 +1006,30 @@
         ]
         up_in = hop(up_narrow, INWARD)
 
-        (came,) = after(up_in[:1], up_narrow)
+        side_first = after(side_first, up_narrow)
+        side_second = [add_low(both[1], side_first[0][1]), add_low(both[5], side_first[1][1])]
+        side_got = [swap(side_second[0], 4), swap(side_second[1], 2)]
+
+        (came,) = after(up_in[:1], side_second)
         up_half = [add_low(up_narrow[0], came)]
         up_mid = hop(up_half, ACROSS)
 
-        (down_mid,) = after([down_mid], up_half)
+        (came,) = after(up_in[1:], up_half)
+        up_half.append(add_low(up_narrow[1], came))
+        up_mid += hop(up_half[1:], ACROSS)
+
+        side_got = after(side_got, up_half[1])
+        slab_narrow = [
+            add_low(both[0], side_first[0][0], side_got[0]),
+            add_low(both[4], side_first[1][0], side_got[1]),
+        ]
+        slab_in = hop(slab_narrow, INWARD)
+
+        (down_mid,) = after([down_mid], slab_narrow)
         down_total = add_low(down_half, down_mid)
         (down_out,) = hop([down_total], OUTWARD)
 
-        (came,) = after(up_in[1:], down_total)
-        up_half.append(add_low(up_narrow[1], came))
-        up_mid += hop(up_half[1:], ACROSS)
-
-        slab_far = after(slab_far, up_half[1])
-        cut = rows // 2 // SUBLANES * SUBLANES
-        slab_narrow = [
-            add_low(both[0][part], *[far[part] for far in slab_far])
-            for part in (slice(0, cut), slice(cut, None))
-        ]
-        slab_in = hop(slab_narrow, INWARD)
-
-        (came,) = after(up_mid[:1], slab_narrow)
+        (came,) = after(up_mid[:1], down_total)
         up_total = [add_low(up_half[0], came)]
         up_out = hop(up_total, OUTWARD)
 
@@ -1041,7 +1055,7 @@
 
         (down_out,) = after([down_out], gate)
         down_weight_sum = settle(down_total, down_out).astype(F32)
-        up_out = after(up_out, gate)
+        up_out = after(up_out, down_weight_sum, slab_out[0])
         upper, lower = [settle(*pair) for pair in zip(up_total, up_out)]
         first = core == 0
         (up_weight_sum,) = call(
@@ -1050,12 +1064,12 @@
             (jnp.where(first, upper, lower), swap(jnp.where(first, lower, upper), 1)),
             core_position,
         )
-        slab_out = after(slab_out, up_weight_sum)
+        slab_out = after(slab_out, upper, lower)
         scalar = pl.BlockSpec(memory_space=pltpu.SMEM)
         heads_sum, output_sum, short, loss_sum, token_count = call(
-            functools.partial(settle_kernel, cut, rows, hidden),
+            functools.partial(settle_kernel, rows, hidden),
             [
-                ((rows, 3 * width), F32), ((rows, width), F32), ((VECTORS, 4 * width), F32),
+                ((rows, 3 * width), F32), ((rows, width), F32), ((VECTORS, 2 * width), F32),
                 ((1,), F32), ((1,), jnp.int32),
             ],
             (*slab_total, *slab_out),

time: 259 us -> 262 us (1.012)
  waiting for transfers between devices: 94.4 us -> 103 us
  local copies, waits for them, and re-layouts: 11.9 us -> 8.67 us
    ppermute x37 -> x38, waiting for transfers between devices: 51.1 us -> 58.5 us  [swap(): lax.ppermute(values, 'wide', [(i, i ^ bit) for i in range(lax.axis_size('...]
    unnamed x92 -> x90, local copies, waits for them, and re-layouts: 8.32 us -> 5.85 us
    ppermute x37 -> x38, starting transfers between devices: 29.7 us -> 28.9 us  [swap(): lax.ppermute(values, 'wide', [(i, i ^ bit) for i in range(lax.axis_size('...]
  transfers between devices with their start and end apart: 53 -> 54, of which waited for: 20 -> 24; matrix products, arithmetic and copies ran while one was open for 5% -> 5% of each run, Pallas kernels for 26% -> 26%
where the time goes in v2:
time: 262 us; the launch traced here: 261 us
  waiting for transfers between devices  103 us (39%)
  Pallas kernels  78.3 us (30%)
  starting transfers between devices  56.7 us (22%)
  other arithmetic  12.4 us (5%)
  local copies, waits for them, and re-layouts  8.67 us (3%)
    pallas_call x16, Pallas kernels, call(): pl.pallas_call(kernel, out_shape=shapes, grid_spec=pltpu.PrefetchScalarGr...  78.3 us
    ppermute x38, waiting for transfers between devices, swap(): lax.ppermute(values, 'wide', [(i, i ^ bit) for i in range(lax.axis_size('...  58.5 us
    ppermute x16, waiting for transfers between devices, hop(): return [lax.ppermute(part, 'narrow', pairs) for part in parts]  44.8 us
    ppermute x38, starting transfers between devices, swap(): lax.ppermute(values, 'wide', [(i, i ^ bit) for i in range(lax.axis_size('...  28.9 us
    ppermute x16, starting transfers between devices, hop(): return [lax.ppermute(part, 'narrow', pairs) for part in parts]  27.8 us
    convert_element_type x21, other arithmetic, add_low(): return sum((part.astype(F32) for part in parts)).astype(BF16)  10.8 us
    unnamed x90, local copies, waits for them, and re-layouts  5.85 us
  transfers between devices with their start and end apart: 54, of which 24 were waited for; matrix products, arithmetic and copies ran while one was open for 5% of the time, Pallas kernels for 26%

profile of v2, /device:TPU:0, one launch (start us, length us, event | category | flops | bytes accessed | tf_op | source)
XLA Modules:
  0.0 261.0 jit_solution(12528666349895360614)
XLA Ops:
  4.1 3.0 %collective-permute-start = (bf16[88,2560]{1,0:T(8,128)(2,1)S(1)}, bf16[88,2560]{1,0:T(8,128)(2,1)S(1)}, u32[]{:S(2)}, u32[]{:S(2)}) collective-permute-start(bf16[88,2560]{1,0:T(8,128)(2,1)S(1)} %shard_map.305.refs_0_), channel_id=1, source_target_pairs={{0,2},{1,3},{2,0},{3,1},{4,6},{5,7},{6,4},{7,5},{8,10},{9,11},{10,... | collective-permute-start | bytes 1351688 | tf_op jit(solution)/shard_map/ppermute | solution.py:719
  8.7 9.6 %collective-permute-done.refs_1_ = bf16[88,2560]{1,0:T(8,128)(2,1)S(1)} collective-permute-done((bf16[88,2560]{1,0:T(8,128)(2,1)S(1)}, bf16[88,2560]{1,0:T(8,128)(2,1)S(1)}, u32[]{:S(2)}, u32[]{:S(2)}) %collective-permute-start) | collective-permute-done | bytes 450592 | tf_op jit(solution)/shard_map/ppermute | solution.py:719
  19.7 8.9 %collective-permute-done.1.refs_2_ = bf16[88,2560]{1,0:T(8,128)(2,1)S(1)} collective-permute-done((bf16[88,2560]{1,0:T(8,128)(2,1)S(1)}, bf16[88,2560]{1,0:T(8,128)(2,1)S(1)}, u32[]{:S(2)}, u32[]{:S(2)}) %collective-permute-start.1) | collective-permute-done | bytes 450592 | tf_op jit(solution)/shard_map/ppermute | solution.py:719
  33.5 5.0 %shard_map.307 = (bf16[512,640]{1,0:T(8,128)(2,1)S(1)}, bf16[512,1920]{1,0:T(8,128)(2,1)S(1)}, bf16[640,1920]{1,0:T(8,128)(2,1)S(1)}, bf16[640,640]{1,0:T(8,128)...) custom-call(s32[8]{0:T(128)S(1)} %pad_add_fusion.position_ref, bf16[512,640]{1,0:T(8,128)(2,1)S(1)} %bitcast.69, ...), custom_call_target="tpu_custom_call" | custom-call | flops 1 | bytes 1 | tf_op jit(solution)/shard_map/pallas_call | solution.py:56
  39.9 7.9 %shard_map.308 = (bf16[512,640]{1,0:T(8,128)(2,1)S(1)}, f32[640,512]{1,0:T(8,128)S(1)}, f32[40,512]{1,0:T(8,128)S(1)}) custom-call(s32[1,512]{1,0:T(1,128)S(1)} %copy-done.28, bf16[512,1920]{1,0:T(8,128)(2,1)S(1)} %get-tuple-element.116.q_ref.k_ref.v_ref, bf16[512,1920]{1,0:T(8,128)(2,1)S(1)} %get-tuple-element.116.q_ref.k_ref.v_ref, ...), custom_call_target="tpu_custom_call" | custom-call | flops 1 | bytes 1 | tf_op jit(solution)/shard_map/pallas_call | solution.py:56
  53.9 8.3 %collective-permute-done.11.refs_3_ = bf16[80,2560]{1,0:T(8,128)(2,1)S(1)} collective-permute-done((bf16[80,2560]{1,0:T(8,128)(2,1)S(1)}, bf16[80,2560]{1,0:T(8,128)(2,1)S(1)}, u32[]{:S(2)}, u32[]{:S(2)}) %collective-permute-start.11) | collective-permute-done | bytes 409632 | tf_op jit(solution)/shard_map/ppermute | solution.py:719
  64.2 8.1 %shard_map.310 = (bf16[1024,2560]{1,0:T(8,128)(2,1)S(1)}, bf16[1024,2560]{1,0:T(8,128)(2,1)S(1)}, bf16[640,2560]{1,0:T(8,128)(2,1)S(1)}) custom-call(s32[8]{0:T(128)S(1)} %pad_add_fusion.position_ref, bf16[512,640]{1,0:T(8,128)(2,1)S(1)} %get-tuple-element.121.own_ref.second_ref, bf16[512,640]{1,0:T(8,128)(2,1)S(1)} %collective-permute-done.7.other_ref.second_other_ref, ...), custom_call_target="tpu_custom_call" | custom-call | flops 1 | bytes 1 | tf_op jit(solution)/shard_map/pallas_call | solution.py:56
  74.5 5.2 %collective-permute-done.15.refs_1_ = bf16[320,640]{1,0:T(8,128)(2,1)S(1)} collective-permute-done((bf16[320,640]{1,0:T(8,128)(2,1)S(1)}, bf16[320,640]{1,0:T(8,128)(2,1)S(1)}, u32[]{:S(2)}, u32[]{:S(2)}) %collective-permute-start.15) | collective-permute-done | bytes 409632 | tf_op jit(solution)/shard_map/ppermute | solution.py:719
  81.1 6.4 %collective-permute-done.19.refs_5_ = bf16[320,640]{1,0:T(8,128)(2,1)S(1)} collective-permute-done((bf16[320,640]{1,0:T(8,128)(2,1)S(1)}, bf16[320,640]{1,0:T(8,128)(2,1)S(1)}, u32[]{:S(2)}, u32[]{:S(2)}) %collective-permute-start.19) | collective-permute-done | bytes 409632 | tf_op jit(solution)/shard_map/ppermute | solution.py:719
  89.1 5.1 %shard_map.311 = (f32[512,640]{1,0:T(8,128)S(1)}, bf16[512,640]{1,0:T(8,128)(2,1)S(1)}, bf16[2560,640]{1,0:T(8,128)(2,1)S(1)}) custom-call(s32[7]{0:T(128)S(1)} %compare_select_fusion.position_ref, bf16[1024,2560]{1,0:T(8,128)(2,1)S(1)} %get-tuple-element.126.act_ref, bf16[640,640]{1,0:T(8,128)(2,1)S(1)} %copy-done.2, ...), custom_call_target="tpu_custom_call" | custom-call | flops 1 | bytes 1 | tf_op jit(solution)/shard_map/pallas_call | solution.py:56
  94.2 2.1 collective-permute-done.21.got_ref
  97.5 2.0 collective-permute-done.22.other_ref
  99.5 4.3 %shard_map.313 = (bf16[2,320,640]{2,1,0:T(8,128)(2,1)S(1)}, bf16[2,320,640]{2,1,0:T(8,128)(2,1)S(1)}, bf16[2,320,640]{2,1,0:T(8,128)(2,1)S(1)}, bf16[2,320,640]{2,1,0:T(8,128)(2,1)S(1)}) custom-call(s32[1]{0:T(128)} %bitcast.12.position_ref, bf16[1024,2560]{1,0:T(8,128)(2,1)S(1)} %get-tuple-element.126.act_ref, ...), custom_call_target="tpu_custom_call" | custom-call | flops 1 | bytes 1 | tf_op jit(solution)/shard_map/pallas_call | solution.py:56
  105.7 10.9 %shard_map.314 = (bf16[1024,2560]{1,0:T(8,128)(2,1)S(1)}, f32[1,2560]{1,0:T(1,128)S(1)}, bf16[2,80,2560]{2,1,0:T(8,128)(2,1)S(1)}, bf16[2,80,2560]{2,1,0:T(8,128...) custom-call(s32[1]{0:T(128)} %bitcast.12.position_ref, ...), custom_call_target="tpu_custom_call" | custom-call | flops 1 | bytes 1 | tf_op jit(solution)/shard_map/pallas_call | solution.py:56
  116.5 6.0 %shard_map.315 = (f32[512,640]{1,0:T(8,128)}, bf16[512,640]{1,0:T(8,128)(2,1)}) custom-call(bf16[1024,2560]{1,0:T(8,128)(2,1)S(1)} %get-tuple-element.140.grad_ref, bf16[640,2560]{1,0:T(8,128)(2,1)S(1)} %get-tuple-element.141.up_ref), custom_call_target="tpu_custom_call" | custom-call | flops 1 | bytes 1 | tf_op jit(solution)/shard_map/pallas_call | solution.py:56
  128.8 1.5 collective-permute-start.32
  130.3 5.1 %shard_map.316 = (f32[512,640]{1,0:T(8,128)S(1)}, bf16[512,640]{1,0:T(8,128)(2,1)S(1)}, bf16[512,640]{1,0:T(8,128)(2,1)S(1)}, f32[8,640]{1,0:T(8,128)S(1)}) custom-call(bf16[512,640]{1,0:T(8,128)(2,1)} %collective-permute-done.23.got_ref, f32[512,640]{1,0:T(8,128)} %get-tuple-element.147.own_far, f32[512,640]{1,0:T(8,128)} %copy-done.1, ...), custom_call_target="tpu_custom_call" | custom-call | flops 1 | bytes 1 | tf_op jit(solution)/shard_map/pallas_call | solution.py:56
  135.5 13.0 %shard_map.317 = (bf16[512,640]{1,0:T(8,128)(2,1)S(1)}, bf16[512,640]{1,0:T(8,128)(2,1)S(1)}, bf16[512,640]{1,0:T(8,128)(2,1)S(1)}) custom-call(s32[1,512]{1,0:T(1,128)S(1)} %copy-done.29, bf16[512,1920]{1,0:T(8,128)(2,1)S(1)} %get-tuple-element.116.q_ref.k_ref.v_ref, bf16[512,1920]{1,0:T(8,128)(2,1)S(1)} %get-tuple-element.116.q_ref.k_ref.v_ref, ...), custom_call_target="tpu_custom_call" | custom-call | flops 1 | bytes 1 | tf_op jit(solution)/shard_map/pallas_call | solution.py:56
  149.9 3.5 %collective-permute-start.29 = (bf16[320,640]{1,0:T(8,128)(2,1)S(1)}, bf16[320,640]{1,0:T(8,128)(2,1)S(1)}, u32[]{:S(2)}, u32[]{:S(2)}) collective-permute-start(bf16[320,640]{1,0:T(8,128)(2,1)S(1)} %fusion.3), channel_id=1, source_target_pairs={{0,8},{24,16},{1,9},{25,17},{2,10},{26,18},{3,11},{27,19},{4,12},{... | collective-permute-start | bytes 1228808 | tf_op jit(solution)/shard_map/ppermute | solution.py:755
  154.6 1.6 collective-permute-start.30
  156.3 8.5 %shard_map.318 = (bf16[8,88,1280]{2,1,0:T(8,128)(2,1)S(1)}, bf16[8,88,1280]{2,1,0:T(8,128)(2,1)S(1)}, f32[512,640]{1,0:T(8,128)}, f32[8,640]{1,0:T(8,128)}, bf16[640,2560]{1,0:T(8,128)(2,1)}) custom-call(s32[8]{0:T(128)S(1)} %copy-done.31, bf16[512,640]{1,0:T(8,128)(2,1)S(1)} %bitcast.71, bf16[512,640]{1,0:T(8,128)(2,1)S(1)} %copy-done.20, ...), custom_call_target="tpu_custom_call" | custom-call | flops 1 | bytes 1 | tf_op jit(solution)/shard_map/pallas_call | solution.py:56
  172.9 5.4 %collective-permute-done.35 = bf16[80,2560]{1,0:T(8,128)(2,1)S(1)} collective-permute-done((bf16[80,2560]{1,0:T(8,128)(2,1)S(1)}, bf16[80,2560]{1,0:T(8,128)(2,1)S(1)}, u32[]{:S(2)}, u32[]{:S(2)}) %collective-permute-start.35) | collective-permute-done | bytes 409632 | tf_op jit(solution)/shard_map/ppermute | solution.py:719
  178.3 1.7 collective-permute-done.36
  184.9 4.0 %collective-permute-done.33 = bf16[2,88,1280]{2,1,0:T(8,128)(2,1)S(1)} collective-permute-done((bf16[2,88,1280]{2,1,0:T(8,128)(2,1)S(1)}, bf16[2,88,1280]{2,1,0:T(8,128)(2,1)S(1)}, u32[]{:S(2)}, u32[]{:S(2)}) %collective-permute-start.33) | collective-permute-done | bytes 450592 | tf_op jit(solution)/shard_map/ppermute | solution.py:719
  189.0 1.6 collective-permute-start.37
  191.1 7.8 %collective-permute-done.40 = bf16[80,2560]{1,0:T(8,128)(2,1)S(1)} collective-permute-done((bf16[80,2560]{1,0:T(8,128)(2,1)S(1)}, bf16[80,2560]{1,0:T(8,128)(2,1)S(1)}, u32[]{:S(2)}, u32[]{:S(2)}) %collective-permute-start.40) | collective-permute-done | bytes 409632 | tf_op jit(solution)/shard_map/ppermute | solution.py:755
  200.7 8.9 %collective-permute-start.41 = (bf16[88,1280]{1,0:T(8,128)(2,1)S(1)}, bf16[88,1280]{1,0:T(8,128)(2,1)S(1)}, u32[]{:S(2)}, u32[]{:S(2)}) collective-permute-start(bf16[88,1280]{1,0:T(8,128)(2,1)S(1)} %get-tuple-element.211), channel_id=1, source_target_pairs={{0,8},{24,16},{1,9},{25,17},{2,10},{26,18},{3,11},{27,19},{4,12},{... | collective-permute-start | bytes 675848 | tf_op jit(solution)/shard_map/ppermute | solution.py:755
  220.3 13.8 %collective-permute-done.52 = bf16[640,640]{1,0:T(8,128)(2,1)S(1)} collective-permute-done((bf16[640,640]{1,0:T(8,128)(2,1)S(1)}, bf16[640,640]{1,0:T(8,128)(2,1)S(1)}, u32[]{:S(2)}, u32[]{:S(2)}) %collective-permute-start.52) | collective-permute-done | bytes 819232 | tf_op jit(solution)/shard_map/ppermute | solution.py:755
  235.4 7.5 %collective-permute-done.50 = bf16[80,2560]{1,0:T(8,128)(2,1)S(1)} collective-permute-done((bf16[80,2560]{1,0:T(8,128)(2,1)S(1)}, bf16[80,2560]{1,0:T(8,128)(2,1)S(1)}, u32[]{:S(2)}, u32[]{:S(2)}) %collective-permute-start.50) | collective-permute-done | bytes 409632 | tf_op jit(solution)/shard_map/ppermute | solution.py:755
  242.9 8.8 %collective-permute-done.51 = bf16[80,2560]{1,0:T(8,128)(2,1)S(1)} collective-permute-done((bf16[80,2560]{1,0:T(8,128)(2,1)S(1)}, bf16[80,2560]{1,0:T(8,128)(2,1)S(1)}, u32[]{:S(2)}, u32[]{:S(2)}) %collective-permute-start.51) | collective-permute-done | bytes 409632 | tf_op jit(solution)/shard_map/ppermute | solution.py:755
  251.7 3.5 %collective-permute-done.48.refs_2_ = bf16[88,1280]{1,0:T(8,128)(2,1)S(1)} collective-permute-done((bf16[88,1280]{1,0:T(8,128)(2,1)S(1)}, bf16[88,1280]{1,0:T(8,128)(2,1)S(1)}, u32[]{:S(2)}, u32[]{:S(2)}) %collective-permute-start.48) | collective-permute-done | bytes 225312 | tf_op jit(solution)/shard_map/ppermute | solution.py:755
  255.4 2.2 collective-permute-done.49.refs_3_
  (216 shorter events, 68.5 us)
Async XLA Ops:
  7.2 21.5 %collective-permute-start.1 = (bf16[88,2560]{1,0:T(8,128)(2,1)S(1)}, bf16[88,2560]{1,0:T(8,128)(2,1)S(1)}, u32[]{:S(2)}, u32[]{:S(2)}) collective-permute-start(bf16[88,2560]{1,0:T(8,128)(2,1)S(1)} %shard_map.305.refs_0_), channel_id=1, source_target_pairs={{0,4},{1,5},{2,6},{3,7},{4,0},{5,1},{6,2},{7,3},{8,12},{9,13},{10,... | collective-permute-start | bytes 1351688 | tf_op jit(solution)/shard_map/ppermute | solution.py:719
  8.7 19.9 %collective-permute-start.2 = (bf16[88,2560]{1,0:T(8,128)(2,1)S(1)}, bf16[88,2560]{1,0:T(8,128)(2,1)S(1)}, u32[]{:S(2)}, u32[]{:S(2)}) collective-permute-start(bf16[88,2560]{1,0:T(8,128)(2,1)S(1)} %shard_map.305.refs_0_), channel_id=1, source_target_pairs={{0,6},{1,7},{2,4},{3,5},{4,2},{5,3},{6,0},{7,1},{8,14},{9,15},{10,... | collective-permute-start | bytes 1351688 | tf_op jit(solution)/shard_map/ppermute | solution.py:719
  8.7 19.9 %collective-permute-start.3 = (bf16[88,2560]{1,0:T(8,128)(2,1)S(1)}, bf16[88,2560]{1,0:T(8,128)(2,1)S(1)}, u32[]{:S(2)}, u32[]{:S(2)}) collective-permute-start(bf16[88,2560]{1,0:T(8,128)(2,1)S(1)} %shard_map.305.refs_0_), channel_id=1, source_target_pairs={{0,1},{1,0},{2,3},{3,2},{4,5},{5,4},{6,7},{7,6},{8,9},{9,8},{10,11... | collective-permute-start | bytes 1351688 | tf_op jit(solution)/shard_map/ppermute | solution.py:719
  29.2 19.8 %collective-permute-start.9 = (bf16[80,2560]{1,0:T(8,128)(2,1)S(1)}, bf16[80,2560]{1,0:T(8,128)(2,1)S(1)}, u32[]{:S(2)}, u32[]{:S(2)}) collective-permute-start(bf16[80,2560]{1,0:T(8,128)(2,1)S(1)} %get-tuple-element.113.refs_0_), channel_id=1, source_target_pairs={{0,4},{1,5},{2,6},{3,7},{4,0},{5,1},{6,2},{7,3},{8,12},{9,13},{10,... | collective-permute-start | bytes 1228808 | tf_op jit(solution)/shard_map/ppermute | solution.py:719
  30.8 19.0 %collective-permute-start.10 = (bf16[80,2560]{1,0:T(8,128)(2,1)S(1)}, bf16[80,2560]{1,0:T(8,128)(2,1)S(1)}, u32[]{:S(2)}, u32[]{:S(2)}) collective-permute-start(bf16[80,2560]{1,0:T(8,128)(2,1)S(1)} %get-tuple-element.123), channel_id=1, source_target_pairs={{0,3},{1,2},{2,1},{3,0},{4,7},{5,6},{6,5},{7,4},{8,11},{9,10},{10,... | collective-permute-start | bytes 1228808 | tf_op jit(solution)/shard_map/ppermute | solution.py:719
  30.8 20.5 %collective-permute-start.8 = (bf16[80,2560]{1,0:T(8,128)(2,1)S(1)}, bf16[80,2560]{1,0:T(8,128)(2,1)S(1)}, u32[]{:S(2)}, u32[]{:S(2)}) collective-permute-start(bf16[80,2560]{1,0:T(8,128)(2,1)S(1)} %get-tuple-element.113.refs_0_), channel_id=1, source_target_pairs={{0,2},{1,3},{2,0},{3,1},{4,6},{5,7},{6,4},{7,5},{8,10},{9,11},{10,... | collective-permute-start | bytes 1228808 | tf_op jit(solution)/shard_map/ppermute | solution.py:719
  32.2 19.7 %collective-permute-start.13 = (bf16[80,2560]{1,0:T(8,128)(2,1)S(1)}, bf16[80,2560]{1,0:T(8,128)(2,1)S(1)}, u32[]{:S(2)}, u32[]{:S(2)}) collective-permute-start(bf16[80,2560]{1,0:T(8,128)(2,1)S(1)} %get-tuple-element.123), channel_id=1, source_target_pairs={{0,5},{1,4},{2,7},{3,6},{4,1},{5,0},{6,3},{7,2},{8,13},{9,12},{10,... | collective-permute-start | bytes 1228808 | tf_op jit(solution)/shard_map/ppermute | solution.py:719
  32.7 20.6 %collective-permute-start.12 = (bf16[80,2560]{1,0:T(8,128)(2,1)S(1)}, bf16[80,2560]{1,0:T(8,128)(2,1)S(1)}, u32[]{:S(2)}, u32[]{:S(2)}) collective-permute-start(bf16[80,2560]{1,0:T(8,128)(2,1)S(1)} %get-tuple-element.123), channel_id=1, source_target_pairs={{0,1},{1,0},{2,3},{3,2},{4,5},{5,4},{6,7},{7,6},{8,9},{9,8},{10,11... | collective-permute-start | bytes 1228808 | tf_op jit(solution)/shard_map/ppermute | solution.py:719
  51.8 20.5 %collective-permute-start.16 = (bf16[320,640]{1,0:T(8,128)(2,1)S(1)}, bf16[320,640]{1,0:T(8,128)(2,1)S(1)}, u32[]{:S(2)}, u32[]{:S(2)}) collective-permute-start(bf16[320,640]{1,0:T(8,128)(2,1)S(1)} %get-tuple-element.128), channel_id=1, source_target_pairs={{0,2},{1,3},{2,0},{3,1},{4,6},{5,7},{6,4},{7,5},{8,10},{9,11},{10,... | collective-permute-start | bytes 1228808 | tf_op jit(solution)/shard_map/ppermute | solution.py:719
  53.3 19.0 %collective-permute-start.17 = (bf16[320,640]{1,0:T(8,128)(2,1)S(1)}, bf16[320,640]{1,0:T(8,128)(2,1)S(1)}, u32[]{:S(2)}, u32[]{:S(2)}) collective-permute-start(bf16[320,640]{1,0:T(8,128)(2,1)S(1)} %get-tuple-element.127), channel_id=1, source_target_pairs={{0,4},{1,5},{2,6},{3,7},{4,0},{5,1},{6,2},{7,3},{8,12},{9,13},{10,... | collective-permute-start | bytes 1228808 | tf_op jit(solution)/shard_map/ppermute | solution.py:719
  62.1 17.6 %collective-permute-start.15 = (bf16[320,640]{1,0:T(8,128)(2,1)S(1)}, bf16[320,640]{1,0:T(8,128)(2,1)S(1)}, u32[]{:S(2)}, u32[]{:S(2)}) collective-permute-start(bf16[320,640]{1,0:T(8,128)(2,1)S(1)} %get-tuple-element.127), channel_id=1, source_target_pairs={{0,2},{1,3},{2,0},{3,1},{4,6},{5,7},{6,4},{7,5},{8,10},{9,11},{10,... | collective-permute-start | bytes 1228808 | tf_op jit(solution)/shard_map/ppermute | solution.py:719
  63.6 17.6 %collective-permute-start.18 = (bf16[320,640]{1,0:T(8,128)(2,1)S(1)}, bf16[320,640]{1,0:T(8,128)(2,1)S(1)}, u32[]{:S(2)}, u32[]{:S(2)}) collective-permute-start(bf16[320,640]{1,0:T(8,128)(2,1)S(1)} %get-tuple-element.128), channel_id=1, source_target_pairs={{0,4},{1,5},{2,6},{3,7},{4,0},{5,1},{6,2},{7,3},{8,12},{9,13},{10,... | collective-permute-start | bytes 1228808 | tf_op jit(solution)/shard_map/ppermute | solution.py:719
  72.4 15.2 %collective-permute-start.19 = (bf16[320,640]{1,0:T(8,128)(2,1)S(1)}, bf16[320,640]{1,0:T(8,128)(2,1)S(1)}, u32[]{:S(2)}, u32[]{:S(2)}) collective-permute-start(bf16[320,640]{1,0:T(8,128)(2,1)S(1)} %collective-permute-done.17.refs_3_), channel_id=1, source_target_pairs={{0,2},{1,3},{2,0},{3,1},{4,6},{5,7},{6,4},{7,5},{8,10},{9,11},{10,... | collective-permute-start | bytes 1228808 | tf_op jit(solution)/shard_map/ppermute | solution.py:719
  73.9 15.2 %collective-permute-start.20 = (bf16[320,640]{1,0:T(8,128)(2,1)S(1)}, bf16[320,640]{1,0:T(8,128)(2,1)S(1)}, u32[]{:S(2)}, u32[]{:S(2)}) collective-permute-start(bf16[320,640]{1,0:T(8,128)(2,1)S(1)} %collective-permute-done.16.refs_2_), channel_id=1, source_target_pairs={{0,4},{1,5},{2,6},{3,7},{4,0},{5,1},{6,2},{7,3},{8,12},{9,13},{10,... | collective-permute-start | bytes 1228808 | tf_op jit(solution)/shard_map/ppermute | solution.py:719
  103.8 20.4 %collective-permute-start.24 = (bf16[2,320,640]{2,1,0:T(8,128)(2,1)S(1)}, bf16[2,320,640]{2,1,0:T(8,128)(2,1)S(1)}, u32[]{:S(2)}, u32[]{:S(2)}) collective-permute-start(bf16[2,320,640]{2,1,0:T(8,128)(2,1)S(1)} %get-tuple-element.136), channel_id=1, source_target_pairs={{0,2},{1,3},{2,0},{3,1},{4,6},{5,7},{6,4},{7,5},{8,10},{9,11},{10,... | collective-permute-start | bytes 2457608 | tf_op jit(solution)/shard_map/ppermute | solution.py:719
  104.4 21.2 %collective-permute-start.25 = (bf16[2,320,640]{2,1,0:T(8,128)(2,1)S(1)}, bf16[2,320,640]{2,1,0:T(8,128)(2,1)S(1)}, u32[]{:S(2)}, u32[]{:S(2)}) collective-permute-start(bf16[2,320,640]{2,1,0:T(8,128)(2,1)S(1)} %get-tuple-element.145), channel_id=1, source_target_pairs={{0,4},{1,5},{2,6},{3,7},{4,0},{5,1},{6,2},{7,3},{8,12},{9,13},{10,... | collective-permute-start | bytes 2457608 | tf_op jit(solution)/shard_map/ppermute | solution.py:719
  125.2 23.4 %collective-permute-start.26 = (bf16[320,640]{1,0:T(8,128)(2,1)}, bf16[320,640]{1,0:T(8,128)(2,1)}, u32[]{:S(2)}, u32[]{:S(2)}) collective-permute-start(bf16[320,640]{1,0:T(8,128)(2,1)} %fusion.6), channel_id=1, source_target_pairs={{0,4},{1,5},{2,6},{3,7},{4,0},{5,1},{6,2},{7,3},{8,12},{9,13},{10,... | collective-permute-start | bytes 1228808 | tf_op jit(solution)/shard_map/ppermute | solution.py:719
  126.7 21.9 %collective-permute-start.27 = (bf16[320,640]{1,0:T(8,128)(2,1)}, bf16[320,640]{1,0:T(8,128)(2,1)}, u32[]{:S(2)}, u32[]{:S(2)}) collective-permute-start(bf16[320,640]{1,0:T(8,128)(2,1)} %fusion.7), channel_id=1, source_target_pairs={{0,2},{1,3},{2,0},{3,1},{4,6},{5,7},{6,4},{7,5},{8,10},{9,11},{10,... | collective-permute-start | bytes 1228808 | tf_op jit(solution)/shard_map/ppermute | solution.py:719
  128.0 36.8 %collective-permute-start.31 = (bf16[2,80,2560]{2,1,0:T(8,128)(2,1)}, bf16[2,80,2560]{2,1,0:T(8,128)(2,1)}, u32[]{:S(2)}, u32[]{:S(2)}) collective-permute-start(bf16[2,80,2560]{2,1,0:T(8,128)(2,1)} %get-tuple-element.172), channel_id=1, source_target_pairs={{0,2},{1,3},{2,0},{3,1},{4,6},{5,7},{6,4},{7,5},{8,10},{9,11},{10,... | collective-permute-start | bytes 2457608 | tf_op jit(solution)/shard_map/ppermute | solution.py:719
  128.8 36.0 %collective-permute-start.32 = (bf16[2,80,2560]{2,1,0:T(8,128)(2,1)}, bf16[2,80,2560]{2,1,0:T(8,128)(2,1)}, u32[]{:S(2)}, u32[]{:S(2)}) collective-permute-start(bf16[2,80,2560]{2,1,0:T(8,128)(2,1)} %get-tuple-element.173), channel_id=1, source_target_pairs={{0,4},{1,5},{2,6},{3,7},{4,0},{5,1},{6,2},{7,3},{8,12},{9,13},{10,... | collective-permute-start | bytes 2457608 | tf_op jit(solution)/shard_map/ppermute | solution.py:719
  149.9 18.9 %collective-permute-start.29 = (bf16[320,640]{1,0:T(8,128)(2,1)S(1)}, bf16[320,640]{1,0:T(8,128)(2,1)S(1)}, u32[]{:S(2)}, u32[]{:S(2)}) collective-permute-start(bf16[320,640]{1,0:T(8,128)(2,1)S(1)} %fusion.3), channel_id=1, source_target_pairs={{0,8},{24,16},{1,9},{25,17},{2,10},{26,18},{3,11},{27,19},{4,12},{... | collective-permute-start | bytes 1228808 | tf_op jit(solution)/shard_map/ppermute | solution.py:755
  169.5 41.4 %collective-permute-start.43 = (bf16[640,640]{1,0:T(8,128)(2,1)S(1)}, bf16[640,640]{1,0:T(8,128)(2,1)S(1)}, u32[]{:S(2)}, u32[]{:S(2)}) collective-permute-start(bf16[640,640]{1,0:T(8,128)(2,1)S(1)} %pad_maximum_fusion), channel_id=1, source_target_pairs={{8,16},{16,8},{9,17},{17,9},{10,18},{18,10},{11,19},{19,11},{12,20... | collective-permute-start | bytes 2457608 | tf_op jit(solution)/shard_map/ppermute | solution.py:755
  170.8 18.0 %collective-permute-start.33 = (bf16[2,88,1280]{2,1,0:T(8,128)(2,1)S(1)}, bf16[2,88,1280]{2,1,0:T(8,128)(2,1)S(1)}, u32[]{:S(2)}, u32[]{:S(2)}) collective-permute-start(bf16[2,88,1280]{2,1,0:T(8,128)(2,1)S(1)} %get-tuple-element.215), channel_id=1, source_target_pairs={{0,2},{1,3},{2,0},{3,1},{4,6},{5,7},{6,4},{7,5},{8,10},{9,11},{10,... | collective-permute-start | bytes 1351688 | tf_op jit(solution)/shard_map/ppermute | solution.py:719
  171.4 17.4 %collective-permute-start.34 = (bf16[2,88,1280]{2,1,0:T(8,128)(2,1)S(1)}, bf16[2,88,1280]{2,1,0:T(8,128)(2,1)S(1)}, u32[]{:S(2)}, u32[]{:S(2)}) collective-permute-start(bf16[2,88,1280]{2,1,0:T(8,128)(2,1)S(1)} %get-tuple-element.214), channel_id=1, source_target_pairs={{0,4},{1,5},{2,6},{3,7},{4,0},{5,1},{6,2},{7,3},{8,12},{9,13},{10,... | collective-permute-start | bytes 1351688 | tf_op jit(solution)/shard_map/ppermute | solution.py:719
  181.1 18.6 %collective-permute-start.39 = (bf16[80,2560]{1,0:T(8,128)(2,1)S(1)}, bf16[80,2560]{1,0:T(8,128)(2,1)S(1)}, u32[]{:S(2)}, u32[]{:S(2)}) collective-permute-start(bf16[80,2560]{1,0:T(8,128)(2,1)S(1)} %fusion), channel_id=1, source_target_pairs={{0,8},{24,16},{1,9},{25,17},{2,10},{26,18},{3,11},{27,19},{4,12},{... | collective-permute-start | bytes 1228808 | tf_op jit(solution)/shard_map/ppermute | solution.py:755
  183.6 15.4 %collective-permute-start.40 = (bf16[80,2560]{1,0:T(8,128)(2,1)S(1)}, bf16[80,2560]{1,0:T(8,128)(2,1)S(1)}, u32[]{:S(2)}, u32[]{:S(2)}) collective-permute-start(bf16[80,2560]{1,0:T(8,128)(2,1)S(1)} %fusion.1), channel_id=1, source_target_pairs={{0,8},{24,16},{1,9},{25,17},{2,10},{26,18},{3,11},{27,19},{4,12},{... | collective-permute-start | bytes 1228808 | tf_op jit(solution)/shard_map/ppermute | solution.py:755
  199.8 15.3 %collective-permute-start.46 = (bf16[80,2560]{1,0:T(8,128)(2,1)S(1)}, bf16[80,2560]{1,0:T(8,128)(2,1)S(1)}, u32[]{:S(2)}, u32[]{:S(2)}) collective-permute-start(bf16[80,2560]{1,0:T(8,128)(2,1)S(1)} %add_convert_fusion.4), channel_id=1, source_target_pairs={{8,16},{16,8},{9,17},{17,9},{10,18},{18,10},{11,19},{19,11},{12,20... | collective-permute-start | bytes 1228808 | tf_op jit(solution)/shard_map/ppermute | solution.py:755
  211.1 23.0 %collective-permute-start.52 = (bf16[640,640]{1,0:T(8,128)(2,1)S(1)}, bf16[640,640]{1,0:T(8,128)(2,1)S(1)}, u32[]{:S(2)}, u32[]{:S(2)}) collective-permute-start(bf16[640,640]{1,0:T(8,128)(2,1)S(1)} %add_convert_fusion.1), channel_id=1, source_target_pairs={{8,0},{16,24},{9,1},{17,25},{10,2},{18,26},{11,3},{19,27},{12,4},{... | collective-permute-start | bytes 2457608 | tf_op jit(solution)/shard_map/ppermute | solution.py:755
  212.5 30.4 %collective-permute-start.50 = (bf16[80,2560]{1,0:T(8,128)(2,1)S(1)}, bf16[80,2560]{1,0:T(8,128)(2,1)S(1)}, u32[]{:S(2)}, u32[]{:S(2)}) collective-permute-start(bf16[80,2560]{1,0:T(8,128)(2,1)S(1)} %add_convert_fusion.3), channel_id=1, source_target_pairs={{8,0},{16,24},{9,1},{17,25},{10,2},{18,26},{11,3},{19,27},{12,4},{... | collective-permute-start | bytes 1228808 | tf_op jit(solution)/shard_map/ppermute | solution.py:755
  215.3 36.4 %collective-permute-start.51 = (bf16[80,2560]{1,0:T(8,128)(2,1)S(1)}, bf16[80,2560]{1,0:T(8,128)(2,1)S(1)}, u32[]{:S(2)}, u32[]{:S(2)}) collective-permute-start(bf16[80,2560]{1,0:T(8,128)(2,1)S(1)} %add_convert_fusion.2), channel_id=1, source_target_pairs={{8,0},{16,24},{9,1},{17,25},{10,2},{18,26},{11,3},{19,27},{12,4},{... | collective-permute-start | bytes 1228808 | tf_op jit(solution)/shard_map/ppermute | solution.py:755
  217.6 37.5 %collective-permute-start.48 = (bf16[88,1280]{1,0:T(8,128)(2,1)S(1)}, bf16[88,1280]{1,0:T(8,128)(2,1)S(1)}, u32[]{:S(2)}, u32[]{:S(2)}) collective-permute-start(bf16[88,1280]{1,0:T(8,128)(2,1)S(1)} %add_convert_fusion.13.refs_0_), channel_id=1, source_target_pairs={{8,0},{16,24},{9,1},{17,25},{10,2},{18,26},{11,3},{19,27},{12,4},{... | collective-permute-start | bytes 675848 | tf_op jit(solution)/shard_map/ppermute | solution.py:755
  219.0 38.6 %collective-permute-start.49 = (bf16[88,1280]{1,0:T(8,128)(2,1)S(1)}, bf16[88,1280]{1,0:T(8,128)(2,1)S(1)}, u32[]{:S(2)}, u32[]{:S(2)}) collective-permute-start(bf16[88,1280]{1,0:T(8,128)(2,1)S(1)} %add_convert_fusion.12.refs_1_), channel_id=1, source_target_pairs={{8,0},{16,24},{9,1},{17,25},{10,2},{18,26},{11,3},{19,27},{12,4},{... | collective-permute-start | bytes 675848 | tf_op jit(solution)/shard_map/ppermute | solution.py:755
  (67 other events, 686.5 us)

commit v3 on v2

--- a/solution.py
+++ b/solution.py
@@ -307,14 +307,6 @@
     slab_ref[rows:, LANES : LANES + up_ref.shape[1]] = jnp.broadcast_to(
         up_ref[...], (VECTORS, up_ref.shape[1])
     )
-
-
-def halves_kernel(hidden, position_ref, up_ref, mine_ref, other_ref):
-    for at in range(mine_ref.shape[1] // hidden):
-        here = slice(hidden * at, hidden * (at + 1))
-        for core, ref in enumerate((mine_ref, other_ref)):
-            begin = (2 * at + (position_ref[0] + core) % 2) * hidden
-            ref[:, here] = up_ref[:, pl.ds(pl.multiple_of(begin, LANES), hidden)]
 
 
 def project_kernel(count, rows, hidden, position_ref, x_ref, *refs):
@@ -419,18 +411,25 @@
     return pl.BlockSpec(shape, lambda i, at: (0,) * len(shape))
 
 
-def up_project(own, other, bias, parts, positions):
+def up_project(own, other, bias, parts, positions, hidden):
     length, width = own.shape
-    half = parts[0].shape[1]
-    steps, _, column = column_specs(half, 512)
+    half = bias.shape[1]
+    paired = parts[0].shape[1] > half
+    steps, block, column = column_specs(half, hidden if paired else 512)
     whole = whole_spec((length, width))
+
+    def part_spec(part):
+        if paired:
+            return pl.BlockSpec((part.shape[0], block), lambda i, at: (0, 2 * i + at[len(parts)]))
+        return column(part.shape[0])
+
     return call(
         up_kernel,
         [((2 * length, half), BF16), ((2 * length, half), BF16), ((width, half), BF16)],
         (own, other, bias, *parts),
         positions,
         grid=(steps,),
-        in_specs=[whole, whole, column(bias.shape[0])] + [column(part.shape[0]) for part in parts],
+        in_specs=[whole, whole, column(bias.shape[0])] + [part_spec(part) for part in parts],
         out_specs=[column(2 * length), column(2 * length), column(width)],
     )
 
@@ -815,21 +814,14 @@
             (heads_weight, output_weight, short, up_bias[None]),
         )
         near_x, near_y, far = swap(slab, 2), swap(slab, 4), swap(slab, 6)
+        swapped = swap(slab, 1)
         devices = 2 * (chip ^ offsets) + core
         positions = jnp.concatenate([devices, devices ^ 1]).astype(jnp.int32)
-        up_positions = positions
-        up_weight, positions = after([up_weight, positions], near_x)
-        up_mine, up_other = call(
-            functools.partial(halves_kernel, hidden),
-            [((rows, half), BF16)] * 2,
-            (up_weight,),
-            core_position,
-        )
-        other_x, mine_y = swap(up_other, 3), swap(up_mine, 4)
-        mine_x, other_y = swap(up_mine, 2), swap(up_other, 5)
-        swapped = [swap(slab, 1), swap(near_x, 1)]
-        near_y, far = after([near_y, far], up_mine, swapped)
-        slabs = [slab, near_x, near_y, far, *swapped, swap(near_y, 1), swap(far, 1)]
+        up_weight, positions = after([up_weight, positions], near_x, swapped)
+        up_x, up_y = swap(up_weight, 2), swap(up_weight, 4)
+        swapped_x = swap(near_x, 1)
+        near_y, far = after([near_y, far], swapped_x)
+        slabs = [slab, near_x, near_y, far, swapped, swapped_x, swap(near_y, 1), swap(far, 1)]
         first_low, joined, heads_full, output_full, vectors, up_bias_half = call(
             functools.partial(project_kernel, len(slabs), rows, hidden),
             [
@@ -880,14 +872,20 @@
 
     attended, across, lse = attend(joined, segments)
     if square():
-        passed_y, passed_x = after([mine_y, other_x], attended)
+        up_x, up_y = after([up_x, up_y], attended)
+        middle_row = rows // 2
         up_parts = [
-            up_mine, mine_x, mine_y, swap(passed_y, 2),
-            swap(up_other, 1), other_x, other_y, swap(passed_x, 4),
+            up_weight, up_x, up_y, swap(up_y[:middle_row], 2), swap(up_x[middle_row:], 4)
         ]
+        up_parts = up_parts + [swap(part, 1) for part in up_parts]
+        at = jnp.arange(11, dtype=jnp.int32)
+        part = at % 5
+        device = 2 * (chip ^ jnp.minimum(part, 3)) + (core ^ (at // 5))
+        up_positions = jnp.where(part < 3, device, 2 * device + part - 3)
+        up_positions = jnp.where(at < 10, up_positions, core).astype(jnp.int32)
         middle_row = hidden // 2
         upper, lower = after(
-            [down_weight[:middle_row], down_weight[middle_row:]], mine_x, other_y, attended
+            [down_weight[:middle_row], down_weight[middle_row:]], up_x, up_y
         )
         lower_x, upper_y = swap(lower, 2), swap(upper, 4)
         upper_x, lower_y = swap(upper, 2), swap(lower, 4)
@@ -904,7 +902,7 @@
 
     second_other = swap(second_low, 1)
     activated, slope, up_full = up_project(
-        second_low, second_other, up_bias_half, up_parts, up_positions
+        second_low, second_other, up_bias_half, up_parts, up_positions, hidden
     )
     if square():
         passed_x, passed_y = after([upper_y, lower_x], activated)
@@ -1010,26 +1008,26 @@
         side_second = [add_low(both[1], side_first[0][1]), add_low(both[5], side_first[1][1])]
         side_got = [swap(side_second[0], 4), swap(side_second[1], 2)]
 
-        (came,) = after(up_in[:1], side_second)
-        up_half = [add_low(up_narrow[0], came)]
-        up_mid = hop(up_half, ACROSS)
-
-        (came,) = after(up_in[1:], up_half)
-        up_half.append(add_low(up_narrow[1], came))
-        up_mid += hop(up_half[1:], ACROSS)
-
-        side_got = after(side_got, up_half[1])
+        (down_mid,) = after([down_mid], side_second)
+        down_total = add_low(down_half, down_mid)
+        (down_out,) = hop([down_total], OUTWARD)
+
+        side_got = after(side_got, down_total)
         slab_narrow = [
             add_low(both[0], side_first[0][0], side_got[0]),
             add_low(both[4], side_first[1][0], side_got[1]),
         ]
         slab_in = hop(slab_narrow, INWARD)
 
-        (down_mid,) = after([down_mid], slab_narrow)
-        down_total = add_low(down_half, down_mid)
-        (down_out,) = hop([down_total], OUTWARD)
-
-        (came,) = after(up_mid[:1], down_total)
+        (came,) = after(up_in[:1], slab_narrow)
+        up_half = [add_low(up_narrow[0], came)]
+        up_mid = hop(up_half, ACROSS)
+
+        (came,) = after(up_in[1:], up_half)
+        up_half.append(add_low(up_narrow[1], came))
+        up_mid += hop(up_half[1:], ACROSS)
+
+        (came,) = after(up_mid[:1], up_half[1])
         up_total = [add_low(up_half[0], came)]
         up_out = hop(up_total, OUTWARD)
 

time: 262 us -> 246 us (0.939)
  waiting for transfers between devices: 103 us -> 94.7 us
  starting transfers between devices: 56.7 us -> 51.1 us
    ppermute x16, waiting for transfers between devices: 44.8 us -> 29.9 us  [hop(): return [lax.ppermute(part, 'narrow', pairs) for part in parts]]
    ppermute x16, starting transfers between devices: 27.8 us -> 20.2 us  [hop(): return [lax.ppermute(part, 'narrow', pairs) for part in parts]]
    ppermute x38 -> x40, waiting for transfers between devices: 58.5 us -> 64.9 us  [swap(): lax.ppermute(values, 'wide', [(i, i ^ bit) for i in range(lax.axis_size('...]
    ppermute x38 -> x40, starting transfers between devices: 28.9 us -> 30.9 us  [swap(): lax.ppermute(values, 'wide', [(i, i ^ bit) for i in range(lax.axis_size('...]
    unnamed x90 -> x96, local copies, waits for them, and re-layouts: 5.85 us -> 4 us
    pallas_call x16 -> x15, Pallas kernels: 78.3 us -> 78.6 us  [call(): pl.pallas_call(kernel, out_shape=shapes, grid_spec=pltpu.PrefetchScalarGr...]
  transfers between devices with their start and end apart: 54 -> 56, of which waited for: 24 -> 27; matrix products, arithmetic and copies ran while one was open for 5% -> 6% of each run, Pallas kernels for 26% -> 27%
where the time goes in v3:
time: 246 us; the launch traced here: 245 us
  waiting for transfers between devices  94.7 us (38%)
  Pallas kernels  78.6 us (32%)
  starting transfers between devices  51.1 us (21%)
  other arithmetic  12.3 us (5%)
  local copies, waits for them, and re-layouts  6.81 us (3%)
    pallas_call x15, Pallas kernels, call(): pl.pallas_call(kernel, out_shape=shapes, grid_spec=pltpu.PrefetchScalarGr...  78.6 us
    ppermute x40, waiting for transfers between devices, swap(): lax.ppermute(values, 'wide', [(i, i ^ bit) for i in range(lax.axis_size('...  64.9 us
    ppermute x40, starting transfers between devices, swap(): lax.ppermute(values, 'wide', [(i, i ^ bit) for i in range(lax.axis_size('...  30.9 us
    ppermute x16, waiting for transfers between devices, hop(): return [lax.ppermute(part, 'narrow', pairs) for part in parts]  29.9 us
    ppermute x16, starting transfers between devices, hop(): return [lax.ppermute(part, 'narrow', pairs) for part in parts]  20.2 us
    convert_element_type x21, other arithmetic, add_low(): return sum((part.astype(F32) for part in parts)).astype(BF16)  10.7 us
  transfers between devices with their start and end apart: 56, of which 27 were waited for; matrix products, arithmetic and copies ran while one was open for 6% of the time, Pallas kernels for 27%

profile of v3, /device:TPU:0, one launch (start us, length us, event | category | flops | bytes accessed | tf_op | source)
XLA Modules:
  0.0 245.2 jit_solution(976928914727737213)
XLA Ops:
  4.1 3.0 %collective-permute-start = (bf16[88,2560]{1,0:T(8,128)(2,1)S(1)}, bf16[88,2560]{1,0:T(8,128)(2,1)S(1)}, u32[]{:S(2)}, u32[]{:S(2)}) collective-permute-start(bf16[88,2560]{1,0:T(8,128)(2,1)S(1)} %shard_map.305.refs_0_), channel_id=1, source_target_pairs={{0,2},{1,3},{2,0},{3,1},{4,6},{5,7},{6,4},{7,5},{8,10},{9,11},{10,... | collective-permute-start | bytes 1351688 | tf_op jit(solution)/shard_map/ppermute | solution.py:718
  8.7 9.6 %collective-permute-done.refs_1_ = bf16[88,2560]{1,0:T(8,128)(2,1)S(1)} collective-permute-done((bf16[88,2560]{1,0:T(8,128)(2,1)S(1)}, bf16[88,2560]{1,0:T(8,128)(2,1)S(1)}, u32[]{:S(2)}, u32[]{:S(2)}) %collective-permute-start) | collective-permute-done | bytes 450592 | tf_op jit(solution)/shard_map/ppermute | solution.py:718
  18.4 2.1 collective-permute-start.8
  22.0 8.0 %collective-permute-done.2.refs_2_ = bf16[88,2560]{1,0:T(8,128)(2,1)S(1)} collective-permute-done((bf16[88,2560]{1,0:T(8,128)(2,1)S(1)}, bf16[88,2560]{1,0:T(8,128)(2,1)S(1)}, u32[]{:S(2)}, u32[]{:S(2)}) %collective-permute-start.2) | collective-permute-done | bytes 450592 | tf_op jit(solution)/shard_map/ppermute | solution.py:718
  34.4 5.0 %shard_map.306 = (bf16[512,640]{1,0:T(8,128)(2,1)S(1)}, bf16[512,1920]{1,0:T(8,128)(2,1)S(1)}, bf16[640,1920]{1,0:T(8,128)(2,1)S(1)}, bf16[640,640]{1,0:T(8,128)...) custom-call(s32[8]{0:T(128)S(1)} %pad_add_fusion.position_ref, bf16[512,640]{1,0:T(8,128)(2,1)S(1)} %bitcast.69, ...), custom_call_target="tpu_custom_call" | custom-call | flops 1 | bytes 1 | tf_op jit(solution)/shard_map/pallas_call | solution.py:56
  39.4 7.9 %shard_map.307 = (bf16[512,640]{1,0:T(8,128)(2,1)S(1)}, f32[640,512]{1,0:T(8,128)S(1)}, f32[40,512]{1,0:T(8,128)S(1)}) custom-call(s32[1,512]{1,0:T(1,128)S(1)} %copy-done.31, bf16[512,1920]{1,0:T(8,128)(2,1)S(1)} %get-tuple-element.112.q_ref.k_ref.v_ref, bf16[512,1920]{1,0:T(8,128)(2,1)S(1)} %get-tuple-element.112.q_ref.k_ref.v_ref, ...), custom_call_target="tpu_custom_call" | custom-call | flops 1 | bytes 1 | tf_op jit(solution)/shard_map/pallas_call | solution.py:56
  51.6 9.6 %collective-permute-done.10.refs_3_ = bf16[40,5120]{1,0:T(8,128)(2,1)S(1)} collective-permute-done((bf16[40,5120]{1,0:T(8,128)(2,1)S(1)}, bf16[40,5120]{1,0:T(8,128)(2,1)S(1)}, u32[]{:S(2)}, u32[]{:S(2)}) %collective-permute-start.10) | collective-permute-done | bytes 409632 | tf_op jit(solution)/shard_map/ppermute | solution.py:718
  66.1 9.5 %shard_map.309 = (bf16[1024,2560]{1,0:T(8,128)(2,1)S(1)}, bf16[1024,2560]{1,0:T(8,128)(2,1)S(1)}, bf16[640,2560]{1,0:T(8,128)(2,1)S(1)}) custom-call(s32[11]{0:T(128)S(1)} %compare_select_fusion.1.position_ref, bf16[512,640]{1,0:T(8,128)(2,1)S(1)} %get-tuple-element.117.own_ref.second_ref, ...), custom_call_target="tpu_custom_call" | custom-call | flops 1 | bytes 1 | tf_op jit(solution)/shard_map/pallas_call | solution.py:56
  78.3 4.7 %collective-permute-done.17.refs_1_ = bf16[320,640]{1,0:T(8,128)(2,1)S(1)} collective-permute-done((bf16[320,640]{1,0:T(8,128)(2,1)S(1)}, bf16[320,640]{1,0:T(8,128)(2,1)S(1)}, u32[]{:S(2)}, u32[]{:S(2)}) %collective-permute-start.17) | collective-permute-done | bytes 409632 | tf_op jit(solution)/shard_map/ppermute | solution.py:718
  84.1 7.3 %collective-permute-done.21.refs_5_ = bf16[320,640]{1,0:T(8,128)(2,1)S(1)} collective-permute-done((bf16[320,640]{1,0:T(8,128)(2,1)S(1)}, bf16[320,640]{1,0:T(8,128)(2,1)S(1)}, u32[]{:S(2)}, u32[]{:S(2)}) %collective-permute-start.21) | collective-permute-done | bytes 409632 | tf_op jit(solution)/shard_map/ppermute | solution.py:718
  92.1 5.0 %shard_map.310 = (f32[512,640]{1,0:T(8,128)S(1)}, bf16[512,640]{1,0:T(8,128)(2,1)S(1)}, bf16[2560,640]{1,0:T(8,128)(2,1)S(1)}) custom-call(s32[7]{0:T(128)S(1)} %compare_select_fusion.2.position_ref, bf16[1024,2560]{1,0:T(8,128)(2,1)S(1)} %get-tuple-element.122.act_ref, bf16[640,640]{1,0:T(8,128)(2,1)S(1)} %copy-done.3, ...), custom_call_target="tpu_custom_call" | custom-call | flops 1 | bytes 1 | tf_op jit(solution)/shard_map/pallas_call | solution.py:56
  97.2 2.1 collective-permute-done.23.got_ref
  100.5 2.0 collective-permute-done.24.other_ref
  102.5 4.3 %shard_map.312 = (bf16[2,320,640]{2,1,0:T(8,128)(2,1)S(1)}, bf16[2,320,640]{2,1,0:T(8,128)(2,1)S(1)}, bf16[2,320,640]{2,1,0:T(8,128)(2,1)S(1)}, bf16[2,320,640]{2,1,0:T(8,128)(2,1)S(1)}) custom-call(s32[1]{0:T(128)} %bitcast.11.position_ref, bf16[1024,2560]{1,0:T(8,128)(2,1)S(1)} %get-tuple-element.122.act_ref, ...), custom_call_target="tpu_custom_call" | custom-call | flops 1 | bytes 1 | tf_op jit(solution)/shard_map/pallas_call | solution.py:56
  109.0 10.9 %shard_map.313 = (bf16[1024,2560]{1,0:T(8,128)(2,1)S(1)}, f32[1,2560]{1,0:T(1,128)S(1)}, bf16[2,80,2560]{2,1,0:T(8,128)(2,1)S(1)}, bf16[2,80,2560]{2,1,0:T(8,128...) custom-call(s32[1]{0:T(128)} %bitcast.11.position_ref, ...), custom_call_target="tpu_custom_call" | custom-call | flops 1 | bytes 1 | tf_op jit(solution)/shard_map/pallas_call | solution.py:56
  119.9 6.0 %shard_map.314 = (f32[512,640]{1,0:T(8,128)}, bf16[512,640]{1,0:T(8,128)(2,1)}) custom-call(bf16[1024,2560]{1,0:T(8,128)(2,1)S(1)} %get-tuple-element.136.grad_ref, bf16[640,2560]{1,0:T(8,128)(2,1)S(1)} %get-tuple-element.137.up_ref), custom_call_target="tpu_custom_call" | custom-call | flops 1 | bytes 1 | tf_op jit(solution)/shard_map/pallas_call | solution.py:56
  133.3 4.1 %shard_map.315 = (f32[512,640]{1,0:T(8,128)S(1)}, bf16[512,640]{1,0:T(8,128)(2,1)S(1)}, bf16[512,640]{1,0:T(8,128)(2,1)S(1)}, f32[8,640]{1,0:T(8,128)S(1)}) custom-call(bf16[512,640]{1,0:T(8,128)(2,1)S(1)} %collective-permute-done.25.got_ref, f32[512,640]{1,0:T(8,128)} %get-tuple-element.143.own_far, f32[512,640]{1,0:T(8,128)} %copy-done.2, ...), custom_call_target="tpu_custom_call" | custom-call | flops 1 | bytes 1 | tf_op jit(solution)/shard_map/pallas_call | solution.py:56
  137.5 13.0 %shard_map.316 = (bf16[512,640]{1,0:T(8,128)(2,1)S(1)}, bf16[512,640]{1,0:T(8,128)(2,1)S(1)}, bf16[512,640]{1,0:T(8,128)(2,1)S(1)}) custom-call(s32[1,512]{1,0:T(1,128)S(1)} %copy-done.32, bf16[512,1920]{1,0:T(8,128)(2,1)S(1)} %get-tuple-element.112.q_ref.k_ref.v_ref, bf16[512,1920]{1,0:T(8,128)(2,1)S(1)} %get-tuple-element.112.q_ref.k_ref.v_ref, ...), custom_call_target="tpu_custom_call" | custom-call | flops 1 | bytes 1 | tf_op jit(solution)/shard_map/pallas_call | solution.py:56
  151.9 3.5 %collective-permute-start.31 = (bf16[320,640]{1,0:T(8,128)(2,1)S(1)}, bf16[320,640]{1,0:T(8,128)(2,1)S(1)}, u32[]{:S(2)}, u32[]{:S(2)}) collective-permute-start(bf16[320,640]{1,0:T(8,128)(2,1)S(1)} %fusion.3), channel_id=1, source_target_pairs={{0,8},{24,16},{1,9},{25,17},{2,10},{26,18},{3,11},{27,19},{4,12},{... | collective-permute-start | bytes 1228808 | tf_op jit(solution)/shard_map/ppermute | solution.py:754
  156.6 1.6 collective-permute-start.32
  158.2 8.5 %shard_map.317 = (bf16[8,88,1280]{2,1,0:T(8,128)(2,1)S(1)}, bf16[8,88,1280]{2,1,0:T(8,128)(2,1)S(1)}, f32[512,640]{1,0:T(8,128)}, f32[8,640]{1,0:T(8,128)}, bf16[640,2560]{1,0:T(8,128)(2,1)}) custom-call(s32[8]{0:T(128)S(1)} %copy-done.36, bf16[512,640]{1,0:T(8,128)(2,1)S(1)} %bitcast.71, bf16[512,640]{1,0:T(8,128)(2,1)S(1)} %copy-done.23, ...), custom_call_target="tpu_custom_call" | custom-call | flops 1 | bytes 1 | tf_op jit(solution)/shard_map/pallas_call | solution.py:56
  167.8 1.6 collective-permute-start.37
  174.9 5.3 %collective-permute-done.37 = bf16[80,2560]{1,0:T(8,128)(2,1)S(1)} collective-permute-done((bf16[80,2560]{1,0:T(8,128)(2,1)S(1)}, bf16[80,2560]{1,0:T(8,128)(2,1)S(1)}, u32[]{:S(2)}, u32[]{:S(2)}) %collective-permute-start.37) | collective-permute-done | bytes 409632 | tf_op jit(solution)/shard_map/ppermute | solution.py:718
  180.2 2.7 %collective-permute-done.38 = bf16[80,2560]{1,0:T(8,128)(2,1)S(1)} collective-permute-done((bf16[80,2560]{1,0:T(8,128)(2,1)S(1)}, bf16[80,2560]{1,0:T(8,128)(2,1)S(1)}, u32[]{:S(2)}, u32[]{:S(2)}) %collective-permute-start.38) | collective-permute-done | bytes 409632 | tf_op jit(solution)/shard_map/ppermute | solution.py:718
  187.9 4.0 %collective-permute-done.35 = bf16[2,88,1280]{2,1,0:T(8,128)(2,1)S(1)} collective-permute-done((bf16[2,88,1280]{2,1,0:T(8,128)(2,1)S(1)}, bf16[2,88,1280]{2,1,0:T(8,128)(2,1)S(1)}, u32[]{:S(2)}, u32[]{:S(2)}) %collective-permute-start.35) | collective-permute-done | bytes 450592 | tf_op jit(solution)/shard_map/ppermute | solution.py:718
  195.0 3.8 %collective-permute-done.39 = bf16[88,1280]{1,0:T(8,128)(2,1)S(1)} collective-permute-done((bf16[88,1280]{1,0:T(8,128)(2,1)S(1)}, bf16[88,1280]{1,0:T(8,128)(2,1)S(1)}, u32[]{:S(2)}, u32[]{:S(2)}) %collective-permute-start.39) | collective-permute-done | bytes 225312 | tf_op jit(solution)/shard_map/ppermute | solution.py:718
  202.6 2.5 %collective-permute-done.45 = bf16[80,2560]{1,0:T(8,128)(2,1)S(1)} collective-permute-done((bf16[80,2560]{1,0:T(8,128)(2,1)S(1)}, bf16[80,2560]{1,0:T(8,128)(2,1)S(1)}, u32[]{:S(2)}, u32[]{:S(2)}) %collective-permute-start.45) | collective-permute-done | bytes 409632 | tf_op jit(solution)/shard_map/ppermute | solution.py:754
  207.3 2.6 %collective-permute-done.42 = bf16[88,1280]{1,0:T(8,128)(2,1)S(1)} collective-permute-done((bf16[88,1280]{1,0:T(8,128)(2,1)S(1)}, bf16[88,1280]{1,0:T(8,128)(2,1)S(1)}, u32[]{:S(2)}, u32[]{:S(2)}) %collective-permute-start.42) | collective-permute-done | bytes 225312 | tf_op jit(solution)/shard_map/ppermute | solution.py:754
  217.8 7.5 %collective-permute-done.52 = bf16[80,2560]{1,0:T(8,128)(2,1)S(1)} collective-permute-done((bf16[80,2560]{1,0:T(8,128)(2,1)S(1)}, bf16[80,2560]{1,0:T(8,128)(2,1)S(1)}, u32[]{:S(2)}, u32[]{:S(2)}) %collective-permute-start.52) | collective-permute-done | bytes 409632 | tf_op jit(solution)/shard_map/ppermute | solution.py:754
  225.3 10.4 %collective-permute-done.53 = bf16[80,2560]{1,0:T(8,128)(2,1)S(1)} collective-permute-done((bf16[80,2560]{1,0:T(8,128)(2,1)S(1)}, bf16[80,2560]{1,0:T(8,128)(2,1)S(1)}, u32[]{:S(2)}, u32[]{:S(2)}) %collective-permute-start.53) | collective-permute-done | bytes 409632 | tf_op jit(solution)/shard_map/ppermute | solution.py:754
  235.7 3.7 %collective-permute-done.50.refs_2_ = bf16[88,1280]{1,0:T(8,128)(2,1)S(1)} collective-permute-done((bf16[88,1280]{1,0:T(8,128)(2,1)S(1)}, bf16[88,1280]{1,0:T(8,128)(2,1)S(1)}, u32[]{:S(2)}, u32[]{:S(2)}) %collective-permute-start.50) | collective-permute-done | bytes 225312 | tf_op jit(solution)/shard_map/ppermute | solution.py:754
  239.6 2.2 collective-permute-done.51.refs_3_
  (228 shorter events, 69.8 us)
Async XLA Ops:
  4.1 14.2 %collective-permute-start = (bf16[88,2560]{1,0:T(8,128)(2,1)S(1)}, bf16[88,2560]{1,0:T(8,128)(2,1)S(1)}, u32[]{:S(2)}, u32[]{:S(2)}) collective-permute-start(bf16[88,2560]{1,0:T(8,128)(2,1)S(1)} %shard_map.305.refs_0_), channel_id=1, source_target_pairs={{0,2},{1,3},{2,0},{3,1},{4,6},{5,7},{6,4},{7,5},{8,10},{9,11},{10,... | collective-permute-start | bytes 1351688 | tf_op jit(solution)/shard_map/ppermute | solution.py:718
  7.1 22.9 %collective-permute-start.2 = (bf16[88,2560]{1,0:T(8,128)(2,1)S(1)}, bf16[88,2560]{1,0:T(8,128)(2,1)S(1)}, u32[]{:S(2)}, u32[]{:S(2)}) collective-permute-start(bf16[88,2560]{1,0:T(8,128)(2,1)S(1)} %shard_map.305.refs_0_), channel_id=1, source_target_pairs={{0,4},{1,5},{2,6},{3,7},{4,0},{5,1},{6,2},{7,3},{8,12},{9,13},{10,... | collective-permute-start | bytes 1351688 | tf_op jit(solution)/shard_map/ppermute | solution.py:718
  8.6 21.4 %collective-permute-start.3 = (bf16[88,2560]{1,0:T(8,128)(2,1)S(1)}, bf16[88,2560]{1,0:T(8,128)(2,1)S(1)}, u32[]{:S(2)}, u32[]{:S(2)}) collective-permute-start(bf16[88,2560]{1,0:T(8,128)(2,1)S(1)} %shard_map.305.refs_0_), channel_id=1, source_target_pairs={{0,6},{1,7},{2,4},{3,5},{4,2},{5,3},{6,0},{7,1},{8,14},{9,15},{10,... | collective-permute-start | bytes 1351688 | tf_op jit(solution)/shard_map/ppermute | solution.py:718
  18.4 29.0 %collective-permute-start.8 = (bf16[80,5120]{1,0:T(8,128)(2,1)}, bf16[80,5120]{1,0:T(8,128)(2,1)S(1)}, u32[]{:S(2)}, u32[]{:S(2)}) collective-permute-start(bf16[80,5120]{1,0:T(8,128)(2,1)} %refs_0_.1), channel_id=1, source_target_pairs={{0,2},{1,3},{2,0},{3,1},{4,6},{5,7},{6,4},{7,5},{8,10},{9,11},{10,... | collective-permute-start | bytes 2457608 | tf_op jit(solution)/shard_map/ppermute | solution.py:718
  20.4 26.9 %collective-permute-start.9 = (bf16[80,5120]{1,0:T(8,128)(2,1)}, bf16[80,5120]{1,0:T(8,128)(2,1)S(1)}, u32[]{:S(2)}, u32[]{:S(2)}) collective-permute-start(bf16[80,5120]{1,0:T(8,128)(2,1)} %refs_0_.1), channel_id=1, source_target_pairs={{0,4},{1,5},{2,6},{3,7},{4,0},{5,1},{6,2},{7,3},{8,12},{9,13},{10,... | collective-permute-start | bytes 2457608 | tf_op jit(solution)/shard_map/ppermute | solution.py:718
  30.6 19.9 %collective-permute-start.12 = (bf16[80,5120]{1,0:T(8,128)(2,1)}, bf16[80,5120]{1,0:T(8,128)(2,1)S(1)}, u32[]{:S(2)}, u32[]{:S(2)}) collective-permute-start(bf16[80,5120]{1,0:T(8,128)(2,1)} %refs_0_.1), channel_id=1, source_target_pairs={{0,1},{1,0},{2,3},{3,2},{4,5},{5,4},{6,7},{7,6},{8,9},{9,8},{10,11... | collective-permute-start | bytes 2457608 | tf_op jit(solution)/shard_map/ppermute | solution.py:718
  47.4 15.6 %collective-permute-start.13 = (bf16[80,5120]{1,0:T(8,128)(2,1)S(1)}, bf16[80,5120]{1,0:T(8,128)(2,1)S(1)}, u32[]{:S(2)}, u32[]{:S(2)}) collective-permute-start(bf16[80,5120]{1,0:T(8,128)(2,1)S(1)} %collective-permute-done.8.refs_1_), channel_id=1, source_target_pairs={{0,1},{1,0},{2,3},{3,2},{4,5},{5,4},{6,7},{7,6},{8,9},{9,8},{10,11... | collective-permute-start | bytes 2457608 | tf_op jit(solution)/shard_map/ppermute | solution.py:718
  48.7 13.2 %collective-permute-start.7 = (bf16[512,640]{1,0:T(8,128)(2,1)S(1)}, bf16[512,640]{1,0:T(8,128)(2,1)S(1)}, u32[]{:S(2)}, u32[]{:S(2)}) collective-permute-start(bf16[512,640]{1,0:T(8,128)(2,1)S(1)} %get-tuple-element.117.own_ref.second_ref), channel_id=1, source_target_pairs={{0,1},{1,0},{2,3},{3,2},{4,5},{5,4},{6,7},{7,6},{8,9},{9,8},{10,11... | collective-permute-start | bytes 1966088 | tf_op jit(solution)/shard_map/ppermute | solution.py:718
  49.2 15.2 %collective-permute-start.14 = (bf16[80,5120]{1,0:T(8,128)(2,1)S(1)}, bf16[80,5120]{1,0:T(8,128)(2,1)S(1)}, u32[]{:S(2)}, u32[]{:S(2)}) collective-permute-start(bf16[80,5120]{1,0:T(8,128)(2,1)S(1)} %collective-permute-done.9.refs_2_), channel_id=1, source_target_pairs={{0,1},{1,0},{2,3},{3,2},{4,5},{5,4},{6,7},{7,6},{8,9},{9,8},{10,11... | collective-permute-start | bytes 2457608 | tf_op jit(solution)/shard_map/ppermute | solution.py:718
  61.9 13.7 %collective-permute-start.18 = (bf16[320,640]{1,0:T(8,128)(2,1)S(1)}, bf16[320,640]{1,0:T(8,128)(2,1)S(1)}, u32[]{:S(2)}, u32[]{:S(2)}) collective-permute-start(bf16[320,640]{1,0:T(8,128)(2,1)S(1)} %get-tuple-element.124), channel_id=1, source_target_pairs={{0,2},{1,3},{2,0},{3,1},{4,6},{5,7},{6,4},{7,5},{8,10},{9,11},{10,... | collective-permute-start | bytes 1228808 | tf_op jit(solution)/shard_map/ppermute | solution.py:718
  64.5 18.5 %collective-permute-start.17 = (bf16[320,640]{1,0:T(8,128)(2,1)S(1)}, bf16[320,640]{1,0:T(8,128)(2,1)S(1)}, u32[]{:S(2)}, u32[]{:S(2)}) collective-permute-start(bf16[320,640]{1,0:T(8,128)(2,1)S(1)} %get-tuple-element.123), channel_id=1, source_target_pairs={{0,2},{1,3},{2,0},{3,1},{4,6},{5,7},{6,4},{7,5},{8,10},{9,11},{10,... | collective-permute-start | bytes 1228808 | tf_op jit(solution)/shard_map/ppermute | solution.py:718
  65.4 18.7 %collective-permute-start.20 = (bf16[320,640]{1,0:T(8,128)(2,1)S(1)}, bf16[320,640]{1,0:T(8,128)(2,1)S(1)}, u32[]{:S(2)}, u32[]{:S(2)}) collective-permute-start(bf16[320,640]{1,0:T(8,128)(2,1)S(1)} %get-tuple-element.124), channel_id=1, source_target_pairs={{0,4},{1,5},{2,6},{3,7},{4,0},{5,1},{6,2},{7,3},{8,12},{9,13},{10,... | collective-permute-start | bytes 1228808 | tf_op jit(solution)/shard_map/ppermute | solution.py:718
  75.6 15.7 %collective-permute-start.21 = (bf16[320,640]{1,0:T(8,128)(2,1)S(1)}, bf16[320,640]{1,0:T(8,128)(2,1)S(1)}, u32[]{:S(2)}, u32[]{:S(2)}) collective-permute-start(bf16[320,640]{1,0:T(8,128)(2,1)S(1)} %collective-permute-done.19.refs_3_), channel_id=1, source_target_pairs={{0,2},{1,3},{2,0},{3,1},{4,6},{5,7},{6,4},{7,5},{8,10},{9,11},{10,... | collective-permute-start | bytes 1228808 | tf_op jit(solution)/shard_map/ppermute | solution.py:718
  76.7 15.4 %collective-permute-start.22 = (bf16[320,640]{1,0:T(8,128)(2,1)S(1)}, bf16[320,640]{1,0:T(8,128)(2,1)S(1)}, u32[]{:S(2)}, u32[]{:S(2)}) collective-permute-start(bf16[320,640]{1,0:T(8,128)(2,1)S(1)} %collective-permute-done.18.refs_2_), channel_id=1, source_target_pairs={{0,4},{1,5},{2,6},{3,7},{4,0},{5,1},{6,2},{7,3},{8,12},{9,13},{10,... | collective-permute-start | bytes 1228808 | tf_op jit(solution)/shard_map/ppermute | solution.py:718
  106.9 20.4 %collective-permute-start.26 = (bf16[2,320,640]{2,1,0:T(8,128)(2,1)S(1)}, bf16[2,320,640]{2,1,0:T(8,128)(2,1)S(1)}, u32[]{:S(2)}, u32[]{:S(2)}) collective-permute-start(bf16[2,320,640]{2,1,0:T(8,128)(2,1)S(1)} %get-tuple-element.132), channel_id=1, source_target_pairs={{0,2},{1,3},{2,0},{3,1},{4,6},{5,7},{6,4},{7,5},{8,10},{9,11},{10,... | collective-permute-start | bytes 2457608 | tf_op jit(solution)/shard_map/ppermute | solution.py:718
  107.9 21.8 %collective-permute-start.27 = (bf16[2,320,640]{2,1,0:T(8,128)(2,1)S(1)}, bf16[2,320,640]{2,1,0:T(8,128)(2,1)S(1)}, u32[]{:S(2)}, u32[]{:S(2)}) collective-permute-start(bf16[2,320,640]{2,1,0:T(8,128)(2,1)S(1)} %get-tuple-element.141), channel_id=1, source_target_pairs={{0,4},{1,5},{2,6},{3,7},{4,0},{5,1},{6,2},{7,3},{8,12},{9,13},{10,... | collective-permute-start | bytes 2457608 | tf_op jit(solution)/shard_map/ppermute | solution.py:718
  128.2 22.4 %collective-permute-start.28 = (bf16[320,640]{1,0:T(8,128)(2,1)}, bf16[320,640]{1,0:T(8,128)(2,1)}, u32[]{:S(2)}, u32[]{:S(2)}) collective-permute-start(bf16[320,640]{1,0:T(8,128)(2,1)} %fusion.6), channel_id=1, source_target_pairs={{0,4},{1,5},{2,6},{3,7},{4,0},{5,1},{6,2},{7,3},{8,12},{9,13},{10,... | collective-permute-start | bytes 1228808 | tf_op jit(solution)/shard_map/ppermute | solution.py:718
  130.8 19.8 %collective-permute-start.29 = (bf16[320,640]{1,0:T(8,128)(2,1)}, bf16[320,640]{1,0:T(8,128)(2,1)}, u32[]{:S(2)}, u32[]{:S(2)}) collective-permute-start(bf16[320,640]{1,0:T(8,128)(2,1)} %fusion.7), channel_id=1, source_target_pairs={{0,2},{1,3},{2,0},{3,1},{4,6},{5,7},{6,4},{7,5},{8,10},{9,11},{10,... | collective-permute-start | bytes 1228808 | tf_op jit(solution)/shard_map/ppermute | solution.py:718
  131.3 35.4 %collective-permute-start.33 = (bf16[2,80,2560]{2,1,0:T(8,128)(2,1)}, bf16[2,80,2560]{2,1,0:T(8,128)(2,1)}, u32[]{:S(2)}, u32[]{:S(2)}) collective-permute-start(bf16[2,80,2560]{2,1,0:T(8,128)(2,1)} %get-tuple-element.168), channel_id=1, source_target_pairs={{0,2},{1,3},{2,0},{3,1},{4,6},{5,7},{6,4},{7,5},{8,10},{9,11},{10,... | collective-permute-start | bytes 2457608 | tf_op jit(solution)/shard_map/ppermute | solution.py:718
  132.8 33.9 %collective-permute-start.34 = (bf16[2,80,2560]{2,1,0:T(8,128)(2,1)}, bf16[2,80,2560]{2,1,0:T(8,128)(2,1)}, u32[]{:S(2)}, u32[]{:S(2)}) collective-permute-start(bf16[2,80,2560]{2,1,0:T(8,128)(2,1)} %get-tuple-element.169), channel_id=1, source_target_pairs={{0,4},{1,5},{2,6},{3,7},{4,0},{5,1},{6,2},{7,3},{8,12},{9,13},{10,... | collective-permute-start | bytes 2457608 | tf_op jit(solution)/shard_map/ppermute | solution.py:718
  151.9 19.2 %collective-permute-start.31 = (bf16[320,640]{1,0:T(8,128)(2,1)S(1)}, bf16[320,640]{1,0:T(8,128)(2,1)S(1)}, u32[]{:S(2)}, u32[]{:S(2)}) collective-permute-start(bf16[320,640]{1,0:T(8,128)(2,1)S(1)} %fusion.3), channel_id=1, source_target_pairs={{0,8},{24,16},{1,9},{25,17},{2,10},{26,18},{3,11},{27,19},{4,12},{... | collective-permute-start | bytes 1228808 | tf_op jit(solution)/shard_map/ppermute | solution.py:754
  156.6 14.6 %collective-permute-start.32 = (bf16[320,640]{1,0:T(8,128)(2,1)S(1)}, bf16[320,640]{1,0:T(8,128)(2,1)S(1)}, u32[]{:S(2)}, u32[]{:S(2)}) collective-permute-start(bf16[320,640]{1,0:T(8,128)(2,1)S(1)} %fusion.2), channel_id=1, source_target_pairs={{0,8},{24,16},{1,9},{25,17},{2,10},{26,18},{3,11},{27,19},{4,12},{... | collective-permute-start | bytes 1228808 | tf_op jit(solution)/shard_map/ppermute | solution.py:754
  171.5 22.0 %collective-permute-start.41 = (bf16[640,640]{1,0:T(8,128)(2,1)S(1)}, bf16[640,640]{1,0:T(8,128)(2,1)S(1)}, u32[]{:S(2)}, u32[]{:S(2)}) collective-permute-start(bf16[640,640]{1,0:T(8,128)(2,1)S(1)} %pad_maximum_fusion), channel_id=1, source_target_pairs={{8,16},{16,8},{9,17},{17,9},{10,18},{18,10},{11,19},{19,11},{12,20... | collective-permute-start | bytes 2457608 | tf_op jit(solution)/shard_map/ppermute | solution.py:754
  172.8 19.0 %collective-permute-start.35 = (bf16[2,88,1280]{2,1,0:T(8,128)(2,1)S(1)}, bf16[2,88,1280]{2,1,0:T(8,128)(2,1)S(1)}, u32[]{:S(2)}, u32[]{:S(2)}) collective-permute-start(bf16[2,88,1280]{2,1,0:T(8,128)(2,1)S(1)} %get-tuple-element.211), channel_id=1, source_target_pairs={{0,2},{1,3},{2,0},{3,1},{4,6},{5,7},{6,4},{7,5},{8,10},{9,11},{10,... | collective-permute-start | bytes 1351688 | tf_op jit(solution)/shard_map/ppermute | solution.py:718
  174.3 17.5 %collective-permute-start.36 = (bf16[2,88,1280]{2,1,0:T(8,128)(2,1)S(1)}, bf16[2,88,1280]{2,1,0:T(8,128)(2,1)S(1)}, u32[]{:S(2)}, u32[]{:S(2)}) collective-permute-start(bf16[2,88,1280]{2,1,0:T(8,128)(2,1)S(1)} %get-tuple-element.210), channel_id=1, source_target_pairs={{0,4},{1,5},{2,6},{3,7},{4,0},{5,1},{6,2},{7,3},{8,12},{9,13},{10,... | collective-permute-start | bytes 1351688 | tf_op jit(solution)/shard_map/ppermute | solution.py:718
  185.2 16.6 %collective-permute-start.43 = (bf16[80,2560]{1,0:T(8,128)(2,1)S(1)}, bf16[80,2560]{1,0:T(8,128)(2,1)S(1)}, u32[]{:S(2)}, u32[]{:S(2)}) collective-permute-start(bf16[80,2560]{1,0:T(8,128)(2,1)S(1)} %fusion.1), channel_id=1, source_target_pairs={{0,8},{24,16},{1,9},{25,17},{2,10},{26,18},{3,11},{27,19},{4,12},{... | collective-permute-start | bytes 1228808 | tf_op jit(solution)/shard_map/ppermute | solution.py:754
  186.6 18.6 %collective-permute-start.45 = (bf16[80,2560]{1,0:T(8,128)(2,1)S(1)}, bf16[80,2560]{1,0:T(8,128)(2,1)S(1)}, u32[]{:S(2)}, u32[]{:S(2)}) collective-permute-start(bf16[80,2560]{1,0:T(8,128)(2,1)S(1)} %fusion), channel_id=1, source_target_pairs={{0,8},{24,16},{1,9},{25,17},{2,10},{26,18},{3,11},{27,19},{4,12},{... | collective-permute-start | bytes 1228808 | tf_op jit(solution)/shard_map/ppermute | solution.py:754
  193.7 22.8 %collective-permute-start.54 = (bf16[640,640]{1,0:T(8,128)(2,1)S(1)}, bf16[640,640]{1,0:T(8,128)(2,1)S(1)}, u32[]{:S(2)}, u32[]{:S(2)}) collective-permute-start(bf16[640,640]{1,0:T(8,128)(2,1)S(1)} %add_convert_fusion.1), channel_id=1, source_target_pairs={{8,0},{16,24},{9,1},{17,25},{10,2},{18,26},{11,3},{19,27},{12,4},{... | collective-permute-start | bytes 2457608 | tf_op jit(solution)/shard_map/ppermute | solution.py:754
  206.1 19.2 %collective-permute-start.52 = (bf16[80,2560]{1,0:T(8,128)(2,1)S(1)}, bf16[80,2560]{1,0:T(8,128)(2,1)S(1)}, u32[]{:S(2)}, u32[]{:S(2)}) collective-permute-start(bf16[80,2560]{1,0:T(8,128)(2,1)S(1)} %add_convert_fusion.3), channel_id=1, source_target_pairs={{8,0},{16,24},{9,1},{17,25},{10,2},{18,26},{11,3},{19,27},{12,4},{... | collective-permute-start | bytes 1228808 | tf_op jit(solution)/shard_map/ppermute | solution.py:754
  210.8 24.9 %collective-permute-start.53 = (bf16[80,2560]{1,0:T(8,128)(2,1)S(1)}, bf16[80,2560]{1,0:T(8,128)(2,1)S(1)}, u32[]{:S(2)}, u32[]{:S(2)}) collective-permute-start(bf16[80,2560]{1,0:T(8,128)(2,1)S(1)} %add_convert_fusion.2), channel_id=1, source_target_pairs={{8,0},{16,24},{9,1},{17,25},{10,2},{18,26},{11,3},{19,27},{12,4},{... | collective-permute-start | bytes 1228808 | tf_op jit(solution)/shard_map/ppermute | solution.py:754
  213.5 25.8 %collective-permute-start.50 = (bf16[88,1280]{1,0:T(8,128)(2,1)S(1)}, bf16[88,1280]{1,0:T(8,128)(2,1)S(1)}, u32[]{:S(2)}, u32[]{:S(2)}) collective-permute-start(bf16[88,1280]{1,0:T(8,128)(2,1)S(1)} %add_convert_fusion.13.refs_0_), channel_id=1, source_target_pairs={{8,0},{16,24},{9,1},{17,25},{10,2},{18,26},{11,3},{19,27},{12,4},{... | collective-permute-start | bytes 675848 | tf_op jit(solution)/shard_map/ppermute | solution.py:754
  214.9 26.8 %collective-permute-start.51 = (bf16[88,1280]{1,0:T(8,128)(2,1)S(1)}, bf16[88,1280]{1,0:T(8,128)(2,1)S(1)}, u32[]{:S(2)}, u32[]{:S(2)}) collective-permute-start(bf16[88,1280]{1,0:T(8,128)(2,1)S(1)} %add_convert_fusion.12.refs_1_), channel_id=1, source_target_pairs={{8,0},{16,24},{9,1},{17,25},{10,2},{18,26},{11,3},{19,27},{12,4},{... | collective-permute-start | bytes 675848 | tf_op jit(solution)/shard_map/ppermute | solution.py:754
  (72 other events, 656.2 us)
